TPU v7x, 128 devices: a whole 4x4x4 slice. The times are simulated.
128 devices in a mesh: grp: 8 (over y, core), mem: 16 (over x, z).
Axes of the slice: x: 4, y: 4, z: 4, core: 2. Of those that a mesh axis runs over, the one named last changes fastest.
Arguments:
- background: float32 [256, 256, 512], P(('grp', 'mem')), may hold values from -6 to 6
- obs_ensemble: float32 [256, 256, 1024], P(('grp', 'mem')), may hold values from -6 to 6
- obs_value: float32 [256, 1024], replicated, may hold values from -12 to 12
- obs_precision: float32 [256, 1024], replicated, may hold values from 0.5 to 4
- obs_count: int32 [256], replicated, may hold values from 64 to 1024, as said below
Outputs:
- analysis: float32 [256, 256, 512], P(('grp', 'mem'))
Inputs may be any that keep to these rules, and one draw needn't show every extreme that they name: `obs_count`: the number of leading slots of each patch that hold observations; exactly 128 patches use more than 512 slots, and some patch uses exactly 1024.
All inputs are finite; a program needn't handle non-finite values.
Results may differ from a plain program's by a relative error of at most 0.0003.
Values sent between devices are 32-bit elements; how exact they have to be, the bound alone decides.
No kernel may reach another device: no remote copies, remote signals or barrier semaphores. Data moves between devices by JAX's collectives and lax.ppermute only.
A program may use at most 64 MiB of HBM per device.

v0:
```python
import jax
import jax.numpy as jnp
from jax import lax
from jax.sharding import Mesh
from jax.sharding import PartitionSpec as P

SWEEPS = 8
GRP_MEM = ("grp_0", "grp_1", "mem_0", "mem_1")


highest = lax.Precision.HIGHEST


def side_by_side(arrays, axis, split_dim, concat_dim, along):
    widths = [a.shape[along] for a in arrays]
    both = jnp.concatenate(arrays, axis=along)
    result = lax.all_to_all(both, axis, split_axis=split_dim, concat_axis=concat_dim, tiled=True)
    return tuple(jnp.split(result, [sum(widths[:k]) for k in range(1, len(widths))], axis=along))


def over_axes(value, axes):
    for axis in axes:
        value = lax.psum(value, axis)
    return value


def inverse_root(amatrix):
    members = amatrix.shape[0]
    identity = jnp.eye(members, dtype=jnp.float32)
    scaler = jnp.sqrt(jnp.sum(amatrix * amatrix))
    iterate = amatrix / scaler
    result = identity
    for sweep in range(SWEEPS):
        factor = 1.5 * identity - 0.5 * jnp.dot(result, iterate, precision=highest)
        iterate = jnp.dot(iterate, factor, precision=highest)
        result = jnp.dot(factor, result, precision=highest)
    return result / jnp.sqrt(scaler)


def send_patches(arrays):
    return side_by_side((arrays[0], arrays[1]), GRP_MEM, 1, 0, 2)


def per_device(background, obs_ensemble, obs_value, obs_precision, obs_count):
    devices = lax.axis_size(GRP_MEM)
    local_members, patches, cells = background.shape
    obs_max = obs_ensemble.shape[2]
    per_dev = patches // devices
    members = local_members * devices
    order = jnp.arange(patches, dtype=jnp.int32)
    states, ensemble = send_patches((background, obs_ensemble))
    mine = lax.axis_index(GRP_MEM)
    owned = lax.dynamic_slice_in_dim(order, mine * per_dev, per_dev)
    values = jnp.take(obs_value, owned, axis=0)
    precision_rows = jnp.take(obs_precision, owned, axis=0)
    counts = jnp.take(obs_count, owned, axis=0)
    slots = jnp.arange(obs_max, dtype=jnp.int32)
    live = (slots[None, :] < counts[:, None]).astype(jnp.float32)
    weight = precision_rows * live
    obs_mean = jnp.mean(ensemble, axis=0)
    perturb = ensemble - obs_mean[None]
    innov = values - obs_mean
    spread = jnp.sum(perturb * perturb, axis=0) / (members - 1.0)
    misfit_part = jnp.sum(weight * innov * innov)
    expected_part = jnp.sum(live * (1.0 + precision_rows * spread))
    misfit, expected = (over_axes(misfit_part, GRP_MEM), over_axes(expected_part, GRP_MEM))
    inflation = jnp.sqrt(misfit / expected)
    block = min(512, obs_max)
    identity = jnp.eye(members, dtype=jnp.float32)

    def patch_step(index, analysis):
        perturb_patch = lax.dynamic_index_in_dim(perturb, index, 1, keepdims=False)
        weight_patch = lax.dynamic_index_in_dim(weight, index, 0, keepdims=False)
        innov_patch = lax.dynamic_index_in_dim(innov, index, 0, keepdims=False)
        count = lax.dynamic_index_in_dim(counts, index, 0, keepdims=False)
        blocks = (count + block - 1) // block

        def gram_step(step, total):
            start = step * block
            rows = lax.dynamic_slice_in_dim(perturb_patch, start, block, 1)
            scale = lax.dynamic_slice_in_dim(weight_patch, start, block, 0)
            return total + jnp.dot(rows * scale[None, :], rows.T, precision=highest)

        gram = lax.fori_loop(0, blocks, gram_step, jnp.zeros((members, members), jnp.float32))
        amatrix = (members - 1.0) * identity + inflation * inflation * gram
        root = inverse_root(amatrix)
        inverse = jnp.dot(root, root, precision=highest)
        forcing = inflation * jnp.dot(perturb_patch, weight_patch * innov_patch, precision=highest)
        shifts = jnp.dot(inverse, forcing, precision=highest)
        transform = jnp.sqrt(members - 1.0) * root + shifts[:, None]
        state_patch = lax.dynamic_index_in_dim(states, index, 1, keepdims=False)
        center = jnp.mean(state_patch, axis=0)
        deviation = state_patch - center[None, :]
        updated = center[None, :] + inflation * jnp.dot(transform.T, deviation, precision=highest)
        return lax.dynamic_update_index_in_dim(analysis, updated, index, 1)

    analysis = lax.fori_loop(0, per_dev, patch_step, jnp.zeros_like(states))
    result = lax.all_to_all(analysis, GRP_MEM, split_axis=0, concat_axis=1, tiled=True)
    return result


def solution(mesh):
    finer = Mesh(mesh.devices.reshape(4, 2, 4, 4), ("grp_0", "grp_1", "mem_0", "mem_1"))
    placed = (P(GRP_MEM, None, None), P(GRP_MEM, None, None), P(), P(), P())
    return jax.shard_map(
        per_device, mesh=finer, in_specs=placed, out_specs=P(GRP_MEM, None, None), check_vma=False
    )
```

profile of v0, /device:TPU:0, one launch (start us, length us, event | category | flops | bytes accessed | tf_op | source)
XLA Modules:
  0.0 182.4 jit_solution(524359615544923023)
XLA Ops:
  0.0 2.1 %pad_maximum_fusion = f32[2,256,1536]{2,1,0:T(8,128)S(1)} fusion(f32[2,256,1024]{2,1,0:T(8,128)} %param.12, f32[2,256,512]{2,1,0:T(8,128)} %param.11), kind=kLoop, calls=%fused_computation.58 | loop fusion | flops 786432 | bytes 6291456 | tf_op jit(solution)/shard_map/concatenate | solution.py:16
  2.2 4.1 %copy.15 = f32[2,256,1536]{2,0,1:T(2,128)} copy(f32[2,256,1536]{2,1,0:T(8,128)S(1)} %pad_maximum_fusion) | data formatting | bytes 6291456 | tf_op jit(solution)/shard_map/concatenate | solution.py:16
  6.3 11.6 %all-to-all-start = ((f32[2,256,1536]{2,0,1:T(2,128)}), f32[2,256,1536]{2,0,1:T(2,128)}, u32[]{:S(2)}, u32[]{:S(2)}) async-start(f32[2,256,1536]{2,0,1:T(2,128)} %copy.15), calls=%async_computation | async-start | bytes 6291456 | tf_op jit(solution)/shard_map/all_to_all | solution.py:17
  19.3 1.8 gather_fusion.2
  21.1 37.2 %all-to-all-done = f32[2,256,1536]{2,0,1:T(2,128)} async-done(((f32[2,256,1536]{2,0,1:T(2,128)}), f32[2,256,1536]{2,0,1:T(2,128)}, u32[]{:S(2)}, u32[]{:S(2)}) %all-to-all-start) | async-done | bytes 3145760 | tf_op jit(solution)/shard_map/all_to_all | solution.py:17
  58.3 4.7 %copy.16 = f32[128,2,2,1536]{3,1,0,2:T(2,128)} copy(f32[128,2,2,1536]{3,1,2,0:T(2,128)} %bitcast.1) | data formatting | bytes 6291456 | tf_op jit(solution)/shard_map/all_to_all | solution.py:17
  62.9 5.2 %all_to_all.29 = f32[256,2,1536]{2,0,1:T(8,128)} reshape(f32[128,2,2,1536]{3,1,0,2:T(2,128)} %copy.16) | data formatting | bytes 6291456 | tf_op jit(solution)/shard_map/all_to_all | solution.py:17
  68.2 1.9 %slice_reduce_fusion = f32[2,1024]{1,0:T(2,128)S(1)} fusion(f32[256,2,1536]{2,0,1:T(8,128)} %all_to_all.29), kind=kLoop, calls=%fused_computation.61 | loop fusion | flops 522240 | bytes 2105344 | tf_op jit(solution)/shard_map/reduce_sum | solution.py:60
  70.0 2.3 %split.8 = f32[256,2,512]{2,0,1:T(8,128)} slice(f32[256,2,1536]{2,0,1:T(8,128)} %all_to_all.29), slice={[0:256], [0:2], [0:512]} | slice | bytes 2097152 | tf_op jit(solution)/shard_map/split | solution.py:18
  72.3 1.7 multiply_reduce_fusion.1
  74.7 9.7 %all-reduce.2 = (f32[]{:T(128)}, f32[]{:T(128)}) all-reduce(f32[]{:T(128)} %get-tuple-element.422, f32[]{:T(128)} %get-tuple-element.427), channel_id=1, replica_groups=mesh['grp_0'=4,'grp_1'=2,'mem_0'=4,'mem_1'=4] {'grp_0'}, use_global_device_ids=true, to_apply=%region_2.4 | all-reduce | flops 2 | bytes 16 | tf_op jit(solution)/shard_map/psum | solution.py:23
  84.4 3.1 %all-reduce.3 = (f32[]{:T(128)}, f32[]{:T(128)}) all-reduce(f32[]{:T(128)} %get-tuple-element.416, f32[]{:T(128)} %get-tuple-element.417), channel_id=1, replica_groups=mesh['grp_0'=4,'grp_1'=2,'mem_0'=4,'mem_1'=4] {'grp_1'}, use_global_device_ids=true, to_apply=%region_3.5 | all-reduce | flops 2 | bytes 16 | tf_op jit(solution)/shard_map/psum | solution.py:23
  87.5 9.1 %all-reduce.1 = (f32[]{:T(128)}, f32[]{:T(128)}) all-reduce(f32[]{:T(128)} %get-tuple-element.418, f32[]{:T(128)} %get-tuple-element.419), channel_id=1, replica_groups=mesh['grp_0'=4,'grp_1'=2,'mem_0'=4,'mem_1'=4] {'mem_0'}, use_global_device_ids=true, to_apply=%region_4.6 | all-reduce | flops 2 | bytes 16 | tf_op jit(solution)/shard_map/psum | solution.py:23
  96.6 10.0 %all-reduce = (f32[]{:T(128)}, f32[]{:T(128)}) all-reduce(f32[]{:T(128)} %get-tuple-element.414, f32[]{:T(128)} %get-tuple-element.415), channel_id=1, replica_groups=mesh['grp_0'=4,'grp_1'=2,'mem_0'=4,'mem_1'=4] {'mem_1'}, use_global_device_ids=true, to_apply=%region_5.7 | all-reduce | flops 2 | bytes 16 | tf_op jit(solution)/shard_map/psum | solution.py:23
  107.9 48.4 %while.64 = (s32[]{:T(128)}, f32[256,2,512]{2,1,0:T(2,128)}, f32[256,2,512]{2,0,1:T(8,128)}, f32[]{:T(128)}, f32[]{:T(128)}, /*index=5*/s32[2]{0:T(128)S(1)}, f3...) while((s32[]{:T(128)}, f32[256,2,512]{2,1,0:T(2,128)}, ...), condition=%wide.region_17.19_spmd.clone, body=%wide.region_12.18_spmd.clone.sunk | while | flops 5645272064 | bytes 48538364 | solution.py:97
  109.3 1.3 dynamic-slice_bitcast_fusion.5
  120.8 1.1 fusion.250
  122.0 1.4 convolution_divide_fusion.2
  126.5 4.7 %dynamic_update_slice.17 = f32[256,2,512]{2,1,0:T(2,128)S(1)} dynamic-update-slice(f32[256,2,512]{2,1,0:T(2,128)S(1)} %copy-done.5, f32[256,1,512]{2,1,0:T(1,128)S(1)} %copy.26, s32[]{:T(128)} %constant.266.clone.1..sunk, s32[]{:T(128)} %get-tuple-element.575, s32[]{:T(128)} %constant.266.clone.1..sunk) | dynamic-update-slice | bytes 1048580 | tf_op jit(solution)/shard_map/while/body/eval_jaxpr/jit(dynamic_update_index_in_dim)/dynamic_update_slice | solution.py:95
  133.4 1.3 dynamic-slice_bitcast_fusion.5
  146.1 1.4 convolution_divide_fusion.2
  150.6 4.7 %dynamic_update_slice.17 = f32[256,2,512]{2,1,0:T(2,128)S(1)} dynamic-update-slice(f32[256,2,512]{2,1,0:T(2,128)S(1)} %copy-done.5, f32[256,1,512]{2,1,0:T(1,128)S(1)} %copy.26, s32[]{:T(128)} %constant.266.clone.1..sunk, s32[]{:T(128)} %get-tuple-element.575, s32[]{:T(128)} %constant.266.clone.1..sunk) | dynamic-update-slice | bytes 1048580 | tf_op jit(solution)/shard_map/while/body/eval_jaxpr/jit(dynamic_update_index_in_dim)/dynamic_update_slice | solution.py:95
  156.2 24.1 %all_to_all.36 = f32[256,2,512]{2,1,0:T(2,128)S(1)} all-to-all(f32[256,2,512]{2,1,0:T(2,128)} %get-tuple-element.362), channel_id=1, replica_groups=mesh['grp_0'=4,'grp_1'=2,'mem_0'=4,'mem_1'=4] {'grp_0','grp_1','mem_0','..., dimensions={0} | all-to-all | bytes 2097152 | tf_op jit(solution)/shard_map/all_to_all | solution.py:98
  180.7 1.7 all_to_all.33
  (105 shorter events, 32.9 us)
Async XLA Ops:
  0.0 18.7 %copy-start = (f32[256,1024]{1,0:T(8,128)S(1)}, f32[256,1024]{1,0:T(8,128)}, u32[]{:S(2)}) copy-start(f32[256,1024]{1,0:T(8,128)} %param.14) | copy-start | bytes 3145732
  6.3 11.8 %copy-start.1 = (s32[256]{0:T(256)S(1)}, s32[256]{0:T(256)}, u32[]{:S(2)}) copy-start(s32[256]{0:T(256)} %param.15) | copy-start | bytes 3076
  6.3 52.0 %all-to-all-start = ((f32[2,256,1536]{2,0,1:T(2,128)}), f32[2,256,1536]{2,0,1:T(2,128)}, u32[]{:S(2)}, u32[]{:S(2)}) async-start(f32[2,256,1536]{2,0,1:T(2,128)} %copy.15), calls=%async_computation | async-start | bytes 6291456 | tf_op jit(solution)/shard_map/all_to_all | solution.py:17
  68.2 4.2 %copy-start.4 = (f32[256,2,1536]{2,0,1:T(8,128)S(1)}, f32[256,2,1536]{2,0,1:T(8,128)}, u32[]{:S(2)}) copy-start(f32[256,2,1536]{2,0,1:T(8,128)} %all_to_all.29) | copy-start | bytes 9437188
  120.1 3.8 %copy-start.2 = (f32[256,2,1024]{2,0,1:T(8,128)S(1)}, f32[256,2,1024]{2,0,1:T(8,128)}, u32[]{:S(2)}) copy-start(f32[256,2,1024]{2,0,1:T(8,128)} %get-tuple-element.601) | copy-start | bytes 6291460 | tf_op jit(solution)/shard_map/while
  122.0 3.1 %copy-start.3 = (f32[256,2,512]{2,0,1:T(8,128)S(1)}, f32[256,2,512]{2,0,1:T(8,128)}, u32[]{:S(2)}) copy-start(f32[256,2,512]{2,0,1:T(8,128)} %get-tuple-element.597) | copy-start | bytes 3145732 | tf_op jit(solution)/shard_map/while
  124.8 1.7 copy-start.5
  131.2 1.0 copy-start.6
  144.2 3.8 %copy-start.2 = (f32[256,2,1024]{2,0,1:T(8,128)S(1)}, f32[256,2,1024]{2,0,1:T(8,128)}, u32[]{:S(2)}) copy-start(f32[256,2,1024]{2,0,1:T(8,128)} %get-tuple-element.601) | copy-start | bytes 6291460 | tf_op jit(solution)/shard_map/while
  146.1 3.1 %copy-start.3 = (f32[256,2,512]{2,0,1:T(8,128)S(1)}, f32[256,2,512]{2,0,1:T(8,128)}, u32[]{:S(2)}) copy-start(f32[256,2,512]{2,0,1:T(8,128)} %get-tuple-element.597) | copy-start | bytes 3145732 | tf_op jit(solution)/shard_map/while
  148.9 1.7 copy-start.5
  155.3 1.0 copy-start.6
where the time goes:
time: 183 us; the launch traced here: 182 us
  blocking collectives  56.1 us (31%)
  local copies, waits for them, and re-layouts  37.8 us (21%)
  waiting for transfers between devices  37.2 us (20%)
  matrix products  26.8 us (15%)
  starting transfers between devices  11.6 us (6%)
  other arithmetic  8.09 us (4%)
  loops' own time  3.56 us (2%)
    all_to_all x1, waiting for transfers between devices, side_by_side(): lax.all_to_all(both, axis, split_axis=split_dim, concat_axis=concat_dim,...  37.2 us
    psum x4, blocking collectives, over_axes(): value = lax.psum(value, axis)  31.9 us
    all_to_all x1, blocking collectives, per_device(): lax.all_to_all(analysis, GRP_MEM, split_axis=0, concat_axis=1, tiled=True)  24.1 us
    all_to_all x1, starting transfers between devices, side_by_side(): lax.all_to_all(both, axis, split_axis=split_dim, concat_axis=concat_dim,...  11.6 us
    dynamic_update_slice x4, local copies, waits for them, and re-layouts, patch_step(): return lax.dynamic_update_index_in_dim(analysis, updated, index, 1)  10.5 us
    all_to_all x2, local copies, waits for them, and re-layouts, side_by_side(): lax.all_to_all(both, axis, split_axis=split_dim, concat_axis=concat_dim,...  9.91 us
    dot_general x16, matrix products, inverse_root(): result = jnp.dot(factor, result, precision=highest)  7.93 us
    dot_general x16, matrix products, inverse_root(): factor = 1.5 * identity - 0.5 * jnp.dot(result, iterate, precision=highest)  7.49 us
  transfers between devices with their start and end apart: 1, of which 1 were waited for; matrix products, arithmetic and copies ran while one was open for 2% of the time, Pallas kernels for 0%

commit v1 on v0

v1 whole, which is shorter than its diff:
```python
import functools

import jax
import jax.numpy as jnp
from jax import lax
from jax.experimental import pallas as pl
from jax.experimental.pallas import tpu as pltpu
from jax.sharding import PartitionSpec as P

SWEEPS = 8
LANES = 128
AXES = ("grp", "mem")
F32 = jnp.float32
BF16 = jnp.bfloat16
VMEM_LIMIT = 48 << 20


def dot(a, b):
    return jnp.dot(a, b, preferred_element_type=F32)


def dot_nt(a, b):
    return lax.dot_general(a, b, (((1,), (1,)), ((), ())), preferred_element_type=F32)


def halves(x):
    high = x.astype(BF16)
    return high, (x - high.astype(F32)).astype(BF16)


def thirds(x):
    high = x.astype(BF16)
    rest = x - high.astype(F32)
    mid = rest.astype(BF16)
    return high, mid, (rest - mid.astype(F32)).astype(BF16)


def left_form(x):
    high, low = halves(x)
    return jnp.concatenate([high, high, low], axis=1)


def right_form(x):
    high, low = halves(x)
    return jnp.concatenate([high, low, high], axis=0)


def owners(counts, half, devices):
    patches = counts.shape[1]
    heavy = (counts > half).astype(F32)
    before = lax.broadcasted_iota(jnp.int32, (patches, patches), 0) < lax.broadcasted_iota(
        jnp.int32, (patches, patches), 1
    )
    rank = dot(jnp.broadcast_to(heavy, (8, patches)).astype(BF16), before.astype(F32).astype(BF16))[:1]
    position = lax.broadcasted_iota(jnp.int32, (1, patches), 1).astype(F32)
    device = lax.broadcasted_iota(jnp.int32, (devices, patches), 0).astype(F32)
    heavies = jnp.where((device == rank) & (heavy > 0.0), 1.0, 0.0)
    lights = jnp.where((device == position - rank) & (heavy == 0.0), 1.0, 0.0)
    return heavies, lights


def pick(onehot, x):
    chosen = onehot.astype(BF16)
    return dot(jnp.concatenate([chosen] * 3, axis=1), jnp.concatenate(thirds(x), axis=0))


def pack_obs_kernel(counts_ref, obs_ref, out_ref):
    local, _, slots = obs_ref.shape
    half = slots // 2
    per = (slots + half) // LANES * local
    devices = out_ref.shape[0] // per
    heavies, lights = owners(counts_ref[...], half, devices)
    for member in range(local):
        heavy = pick(heavies, obs_ref[member])
        for c in range(slots // LANES):
            row = member * (slots // LANES) + c
            out_ref[pl.ds(row, devices, stride=per), :] = heavy[:, c * LANES : (c + 1) * LANES]
        light = pick(lights, obs_ref[member, :, :half])
        for c in range(half // LANES):
            row = local * (slots // LANES) + member * (half // LANES) + c
            out_ref[pl.ds(row, devices, stride=per), :] = light[:, c * LANES : (c + 1) * LANES]


def pack_states_kernel(mine_ref, counts_ref, states_ref, value_ref, precision_ref, out_ref, rows_ref):
    local, patches, cells = states_ref.shape
    slots = value_ref.shape[1]
    blocks = cells // LANES
    per = 2 * local * blocks
    devices = out_ref.shape[0] // per
    counts = counts_ref[...]
    heavies, lights = owners(counts, slots // 2, devices)
    for member in range(local):
        x = states_ref[member]
        for k, onehot in enumerate((heavies, lights)):
            chosen = pick(onehot, x)
            for c in range(blocks):
                row = (k * local + member) * blocks + c
                out_ref[pl.ds(row, devices, stride=per), :] = chosen[:, c * LANES : (c + 1) * LANES]
    here = lax.broadcasted_iota(jnp.int32, (devices, patches), 0) == mine_ref[0]
    own = [jnp.sum(jnp.where(here, onehot, 0.0), axis=0, keepdims=True) for onehot in (heavies, lights)]
    both = jnp.concatenate(own + [jnp.zeros((6, patches), F32)], axis=0)
    values = pick(both, value_ref[...])
    precisions = pick(both, precision_ref[...])
    slot = lax.broadcasted_iota(jnp.int32, (1, slots), 1).astype(F32)
    rows = []
    for k in range(2):
        count = jnp.sum(own[k] * counts.astype(F32), axis=1, keepdims=True)
        live = jnp.where(slot < count, 1.0, 0.0)
        rows += [values[k : k + 1], precisions[k : k + 1], live]
    rows_ref[...] = jnp.concatenate(rows + [jnp.zeros((2, slots), F32)], axis=0)


def gram_kernel(obs_ref, rows_ref, part_ref, gram_ref, high_ref, low_ref, *, local):
    slots = rows_ref.shape[1]
    half = slots // 2
    per = (slots + half) // LANES * local
    devices = obs_ref.shape[0] // per
    members = local * devices
    misfit = jnp.zeros((1, LANES), F32)
    expected = jnp.zeros((1, LANES), F32)
    for k in range(2):
        width = slots if k == 0 else half
        base = 0 if k == 0 else local * (slots // LANES)
        for c in range(width // LANES):
            columns = slice(c * LANES, (c + 1) * LANES)
            parts = [
                obs_ref[pl.ds(base + m * (width // LANES) + c, devices, stride=per), :] for m in range(local)
            ]
            mean = sum(jnp.sum(p, axis=0, keepdims=True) for p in parts) * (1.0 / members)
            parts = [p - mean for p in parts]
            spread = sum(jnp.sum(p * p, axis=0, keepdims=True) for p in parts) * (1.0 / (members - 1.0))
            value = rows_ref[3 * k : 3 * k + 1, columns]
            precision = rows_ref[3 * k + 1 : 3 * k + 2, columns]
            live = rows_ref[3 * k + 2 : 3 * k + 3, columns]
            innov = value - mean
            weight = precision * live
            misfit += weight * innov * innov
            expected += live * (1.0 + precision * spread)
            scale = jnp.sqrt(weight)
            for m in range(local):
                high, low = halves(parts[m] * scale)
                high_ref[m * devices : (m + 1) * devices, columns] = high
                low_ref[m * devices : (m + 1) * devices, columns] = low
            high, low = halves(jnp.broadcast_to(scale * innov, (16, LANES)))
            high_ref[members : members + 16, columns] = high
            low_ref[members : members + 16, columns] = low
        high = high_ref[:, :width]
        low = low_ref[:, :width]
        gram_ref[k] = (
            dot_nt(high, high_ref[:members, :width])
            + dot_nt(high, low_ref[:members, :width])
            + dot_nt(low, high_ref[:members, :width])
        )
    lane = lax.broadcasted_iota(jnp.int32, (1, LANES), 1)
    row = jnp.where(
        lane == 0,
        jnp.sum(misfit, axis=1, keepdims=True),
        jnp.where(lane == 1, jnp.sum(expected, axis=1, keepdims=True), 0.0),
    )
    part_ref[...] = jnp.broadcast_to(row[None], part_ref.shape)


def root_kernel(part_ref, gram_ref, out_ref, inflation_ref, y_right, z_right, z_left):
    members = gram_ref.shape[2]
    total = jnp.sum(part_ref[...], axis=0)
    lane = lax.broadcasted_iota(jnp.int32, total.shape, 1)
    misfit = jnp.sum(jnp.where(lane == 0, total, 0.0), axis=1, keepdims=True)
    expected = jnp.sum(jnp.where(lane == 1, total, 0.0), axis=1, keepdims=True)
    inflation = jnp.sqrt(misfit / expected)
    inflation_ref[...] = jnp.broadcast_to(inflation, inflation_ref.shape)
    identity = jnp.where(
        lax.broadcasted_iota(jnp.int32, (members, members), 0)
        == lax.broadcasted_iota(jnp.int32, (members, members), 1),
        1.0,
        0.0,
    )
    scalers = []
    for k in range(2):
        amat = (members - 1.0) * identity + inflation * inflation * gram_ref[k, :members, :]
        scaler = jnp.sqrt(jnp.sum(jnp.sum(amat * amat, axis=0, keepdims=True), axis=1, keepdims=True))
        scalers.append(scaler)
        iterate = amat / scaler
        factor = 1.5 * identity - 0.5 * iterate
        y_right[k] = right_form(dot(left_form(factor), right_form(iterate)))
        z_right[k] = right_form(factor)
        z_left[k] = left_form(factor)

    def sweep(_, carry):
        for k in range(2):
            factor = left_form(1.5 * identity - 0.5 * dot(z_left[k], y_right[k]))
            iterate = dot(factor, y_right[k])
            root = dot(factor, z_right[k])
            y_right[k] = right_form(iterate)
            z_right[k] = right_form(root)
            z_left[k] = left_form(root)
        return carry

    lax.fori_loop(0, SWEEPS - 2, sweep, 0)
    for k in range(2):
        factor = left_form(1.5 * identity - 0.5 * dot(z_left[k], y_right[k]))
        root = dot(factor, z_right[k]) / jnp.sqrt(scalers[k])
        root_right = right_form(root)
        forcing = inflation * gram_ref[k, members:, :]
        shifts = dot(left_form(dot(left_form(forcing), root_right)), root_right)[:1]
        out_ref[k] = inflation * ((members - 1.0) ** 0.5 * root + shifts)


def update_kernel(states_ref, transform_ref, out_ref, high_ref, low_ref, *, local):
    members = transform_ref.shape[1]
    devices = members // local
    per = states_ref.shape[0] // devices
    blocks = per // (2 * local)
    for k in range(2):
        centers = []
        for c in range(blocks):
            rows = [(k * local + m) * blocks + c for m in range(local)]
            parts = [states_ref[pl.ds(r, devices, stride=per), :] for r in rows]
            center = sum(jnp.sum(p, axis=0, keepdims=True) for p in parts) * (1.0 / members)
            centers.append(center)
            for m in range(local):
                high, low = halves(parts[m] - center)
                high_ref[m * devices : (m + 1) * devices, c * LANES : (c + 1) * LANES] = high
                low_ref[m * devices : (m + 1) * devices, c * LANES : (c + 1) * LANES] = low
        high, low = halves(transform_ref[k])
        update = dot(high, high_ref[...]) + dot(high, low_ref[...]) + dot(low, high_ref[...])
        for c in range(blocks):
            for m in range(local):
                piece = update[m * devices : (m + 1) * devices, c * LANES : (c + 1) * LANES] + centers[c]
                out_ref[pl.ds((k * local + m) * blocks + c, devices, stride=per), :] = piece


def unpack_kernel(counts_ref, rows_ref, out_ref, *, half):
    local, patches, cells = out_ref.shape
    blocks = cells // LANES
    per = 2 * local * blocks
    devices = rows_ref.shape[0] // per
    onehot = jnp.concatenate(owners(counts_ref[...], half, devices), axis=0).T
    for m in range(local):
        x = jnp.concatenate(
            [
                jnp.concatenate(
                    [
                        rows_ref[pl.ds((k * local + m) * blocks + c, devices, stride=per), :]
                        for c in range(blocks)
                    ],
                    axis=1,
                )
                for k in range(2)
            ],
            axis=0,
        )
        out_ref[m] = pick(onehot, x)


def call(kernel, out_shapes, inputs, scratch=(), smem=()):
    whole = pl.BlockSpec(memory_space=pltpu.VMEM)
    shapes = [jax.ShapeDtypeStruct(s, F32) for s in out_shapes]
    return pl.pallas_call(
        kernel,
        out_shape=shapes,
        in_specs=[pl.BlockSpec(memory_space=pltpu.SMEM) if i in smem else whole for i in range(len(inputs))],
        out_specs=[whole] * len(shapes),
        scratch_shapes=list(scratch),
        compiler_params=pltpu.CompilerParams(vmem_limit_bytes=VMEM_LIMIT),
    )(*inputs)


def exchange(x, devices):
    return lax.all_to_all(x, AXES, split_axis=0, concat_axis=0, tiled=True)


def per_device(background, obs_ensemble, obs_value, obs_precision, obs_count):
    devices = lax.axis_size(AXES)
    local, patches, cells = background.shape
    slots = obs_ensemble.shape[2]
    half = slots // 2
    members = local * devices
    counts = obs_count.reshape(1, patches)
    mine = lax.axis_index(AXES).astype(jnp.int32).reshape(1)
    obs_rows = (slots + half) // LANES * local
    state_rows = 2 * local * cells // LANES
    (obs_sent,) = call(pack_obs_kernel, [(devices * obs_rows, LANES)], (counts, obs_ensemble))
    obs = exchange(obs_sent, devices)
    states_sent, rows = call(
        pack_states_kernel,
        [(devices * state_rows, LANES), (8, slots)],
        (mine, counts, background, obs_value, obs_precision),
        smem=(0,),
    )
    states = exchange(states_sent, devices)
    part, gram = call(
        functools.partial(gram_kernel, local=local),
        [(devices, 1, LANES), (2, members + 16, members)],
        (obs, rows),
        scratch=[pltpu.VMEM((members + 16, slots), BF16)] * 2,
    )
    parts = exchange(part, devices)
    transform, inflation = call(
        root_kernel,
        [(2, members, members), (8, LANES)],
        (parts, gram),
        scratch=[
            pltpu.VMEM((2, 3 * members, members), BF16),
            pltpu.VMEM((2, 3 * members, members), BF16),
            pltpu.VMEM((2, members, 3 * members), BF16),
        ],
    )
    (update,) = call(
        functools.partial(update_kernel, local=local),
        [(devices * state_rows, LANES)],
        (states, transform),
        scratch=[pltpu.VMEM((members, cells), BF16)] * 2,
    )
    returned = exchange(update, devices)
    (analysis,) = call(
        functools.partial(unpack_kernel, half=half), [(local, patches, cells)], (counts, returned)
    )
    return analysis


def solution(mesh):
    placed = (P(AXES, None, None), P(AXES, None, None), P(), P(), P())
    return jax.shard_map(
        per_device, mesh=mesh, in_specs=placed, out_specs=P(AXES, None, None), check_vma=False
    )
```

time: 183 us -> 106 us (0.58)
  local copies, waits for them, and re-layouts: 37.8 us -> 4.72 us
  matrix products: 26.8 us -> 0 us
  blocking collectives: 56.1 us -> 36.5 us
  Pallas kernels: 0 us -> 18.9 us
  other arithmetic: 8.09 us -> 0 us
  waiting for transfers between devices: 37.2 us -> 29.4 us
  starting transfers between devices: 11.6 us -> 15.8 us
  loops' own time: 3.56 us -> 0 us
    psum x4 -> x0, blocking collectives: 31.9 us -> none  [over_axes(): value = lax.psum(value, axis)]
    dot_general x56 -> x0, matrix products: 26.8 us -> none  [the longest x16 7.93 us: inverse_root(): result = jnp.dot(factor, result, precision=highest)]
    pallas_call x0 -> x6, Pallas kernels: none -> 18.9 us  [call(): pl.pallas_call(kernel, out_shape=shapes, in_specs=[pl.BlockSpec(memory_sp...]
    all_to_all x1 -> x2, blocking collectives: 24.1 us -> 36.5 us  [exchange(): return lax.all_to_all(x, AXES, split_axis=0, concat_axis=0, tiled=True)]
    all_to_all x4 -> x0, local copies, waits for them, and re-layouts: 12 us -> none  [the longest x2 9.91 us: side_by_side(): lax.all_to_all(both, axis, split_axis=split_dim, concat_axis=concat_dim,...]
    dynamic_update_slice x4 -> x0, local copies, waits for them, and re-layouts: 10.5 us -> none  [patch_step(): return lax.dynamic_update_index_in_dim(analysis, updated, index, 1)]
    all_to_all x1 -> x2, waiting for transfers between devices: 37.2 us -> 29.4 us  [exchange(): return lax.all_to_all(x, AXES, split_axis=0, concat_axis=0, tiled=True)]
    reduce_sum x7 -> x0, other arithmetic: 5.8 us -> none  [the longest x1 1.86 us: per_device(): obs_mean = jnp.mean(ensemble, axis=0)]
  transfers between devices with their start and end apart: 1 -> 2, of which waited for: 1 -> 2; matrix products, arithmetic and copies ran while one was open for 2% -> 0% of each run, Pallas kernels for 0% -> 11%
where the time goes in v1:
time: 106 us; the launch traced here: 105 us
  blocking collectives  36.5 us (34%)
  waiting for transfers between devices  29.4 us (28%)
  Pallas kernels  18.9 us (18%)
  starting transfers between devices  15.8 us (15%)
  local copies, waits for them, and re-layouts  4.72 us (4%)
    all_to_all x2, blocking collectives, exchange(): return lax.all_to_all(x, AXES, split_axis=0, concat_axis=0, tiled=True)  36.5 us
    all_to_all x2, waiting for transfers between devices, exchange(): return lax.all_to_all(x, AXES, split_axis=0, concat_axis=0, tiled=True)  29.4 us
    pallas_call x6, Pallas kernels, call(): pl.pallas_call(kernel, out_shape=shapes, in_specs=[pl.BlockSpec(memory_sp...  18.9 us
    all_to_all x2, starting transfers between devices, exchange(): return lax.all_to_all(x, AXES, split_axis=0, concat_axis=0, tiled=True)  15.8 us
    unnamed x12, local copies, waits for them, and re-layouts  4.72 us
  transfers between devices with their start and end apart: 2, of which 2 were waited for; matrix products, arithmetic and copies ran while one was open for 0% of the time, Pallas kernels for 11%

profile of v1, /device:TPU:0, one launch (start us, length us, event | category | flops | bytes accessed | tf_op | source)
XLA Modules:
  0.0 105.5 jit_solution(3699802915725944575)
XLA Ops:
  0.0 0.0 copy-start
  0.0 1.6 %copy-done = f32[2,256,1024]{2,1,0:T(8,128)S(1)} copy-done((f32[2,256,1024]{2,1,0:T(8,128)S(1)}, f32[2,256,1024]{2,1,0:T(8,128)}, u32[]{:S(2)}) %copy-start) | copy-done | bytes 2097176
  1.6 0.0 copy-start.4
  1.6 0.7 copy-done.4
  2.3 2.5 %shard_map.56 = f32[3072,128]{1,0:T(8,128)} custom-call(s32[1,256]{1,0:T(1,128)S(1)} %bitcast.12, f32[2,256,1024]{2,1,0:T(8,128)S(1)} %copy-done), custom_call_target="tpu_custom_call" | custom-call | tf_op jit(solution)/shard_map/pallas_call | solution.py:258
  4.7 0.0 copy-start.1
  4.7 0.0 copy-start.5
  4.7 11.2 %all-to-all-start.1 = ((f32[128,24,128]{2,1,0:T(8,128)}), f32[128,24,128]{2,1,0:T(8,128)S(1)}, u32[]{:S(2)}, u32[]{:S(2)}) async-start(f32[128,24,128]{2,1,0:T(8,128)} %bitcast.4), calls=%async_computation.1 | async-start | bytes 3145728 | tf_op jit(solution)/shard_map/all_to_all | solution.py:269
  15.9 0.0 copy-done.1
  15.9 0.0 copy-done.5
  16.0 0.0 copy-start.2
  16.0 1.2 %copy-done.2 = f32[256,1024]{1,0:T(8,128)S(1)} copy-done((f32[256,1024]{1,0:T(8,128)S(1)}, f32[256,1024]{1,0:T(8,128)}, u32[]{:S(2)}) %copy-start.2) | copy-done | bytes 1048600
  17.2 0.0 copy-start.3
  17.2 1.2 %copy-done.3 = f32[256,1024]{1,0:T(8,128)S(1)} copy-done((f32[256,1024]{1,0:T(8,128)S(1)}, f32[256,1024]{1,0:T(8,128)}, u32[]{:S(2)}) %copy-start.3) | copy-done | bytes 1048600
  18.4 2.0 %shard_map.55 = (f32[2048,128]{1,0:T(8,128)}, f32[8,1024]{1,0:T(8,128)S(1)}) custom-call(s32[1]{0:T(128)} %bitcast.1.mine_ref, s32[1,256]{1,0:T(1,128)S(1)} %bitcast.13, f32[2,256,512]{2,1,0:T(8,128)S(1)} %copy-done.1, f32[256,1024]{1,0:T(8,128)S(1)} %copy-done.2, f32[256,1024]{1,0:T(8,128)S(1)} %copy-done.3), custom_call_target="tpu_custom_call" | custom-call | tf_op jit(solution)/shard_map/pallas_call | solution.py:258
  20.5 19.9 %all-to-all-done.1 = f32[128,24,128]{2,1,0:T(8,128)S(1)} async-done(((f32[128,24,128]{2,1,0:T(8,128)}), f32[128,24,128]{2,1,0:T(8,128)S(1)}, u32[]{:S(2)}, u32[]{:S(2)}) %all-to-all-start.1) | async-done | bytes 1572896 | tf_op jit(solution)/shard_map/all_to_all | solution.py:269
  40.4 1.6 %shard_map.57 = (f32[128,1,128]{2,1,0:T(1,128)S(1)}, f32[2,272,256]{2,1,0:T(8,128)S(1)}) custom-call(f32[3072,128]{1,0:T(8,128)S(1)} %bitcast.8, f32[8,1024]{1,0:T(8,128)S(1)} %get-tuple-element.11.rows_ref), custom_call_target="tpu_custom_call" | custom-call | tf_op jit(solution)/shard_map/pallas_call | solution.py:258
  42.0 13.5 %all_to_all.38.part_ref = f32[128,1,128]{2,1,0:T(1,128)S(1)} all-to-all(f32[128,1,128]{2,1,0:T(1,128)S(1)} %get-tuple-element.12), channel_id=1, replica_groups=mesh['grp'=8,'mem'=16] {'grp','mem'}, dimensions={0} | all-to-all | bytes 131072 | tf_op jit(solution)/shard_map/all_to_all | solution.py:269
  55.5 4.6 %all-to-all-start = ((f32[128,16,128]{2,1,0:T(8,128)}), f32[128,16,128]{2,1,0:T(8,128)S(1)}, u32[]{:S(2)}, u32[]{:S(2)}) async-start(f32[128,16,128]{2,1,0:T(8,128)} %bitcast.2), calls=%async_computation | async-start | bytes 2097152 | tf_op jit(solution)/shard_map/all_to_all | solution.py:269
  60.1 9.6 %shard_map.58 = (f32[2,256,256]{2,1,0:T(8,128)S(1)}, f32[8,128]{1,0:T(8,128)}) custom-call(f32[128,1,128]{2,1,0:T(1,128)S(1)} %all_to_all.38.part_ref, f32[2,272,256]{2,1,0:T(8,128)S(1)} %get-tuple-element.13.gram_ref), custom_call_target="tpu_custom_call" | custom-call | tf_op jit(solution)/shard_map/pallas_call | solution.py:258
  69.7 9.4 %all-to-all-done = f32[128,16,128]{2,1,0:T(8,128)S(1)} async-done(((f32[128,16,128]{2,1,0:T(8,128)}), f32[128,16,128]{2,1,0:T(8,128)S(1)}, u32[]{:S(2)}, u32[]{:S(2)}) %all-to-all-start) | async-done | bytes 1048608 | tf_op jit(solution)/shard_map/all_to_all | solution.py:269
  79.2 1.3 %shard_map.59 = f32[2048,128]{1,0:T(8,128)S(1)} custom-call(f32[2048,128]{1,0:T(8,128)S(1)} %bitcast.9, f32[2,256,256]{2,1,0:T(8,128)S(1)} %get-tuple-element.14.transform_ref), custom_call_target="tpu_custom_call" | custom-call | tf_op jit(solution)/shard_map/pallas_call | solution.py:258
  80.5 23.0 %all_to_all.39 = f32[128,16,128]{2,1,0:T(8,128)S(1)} all-to-all(f32[128,16,128]{2,1,0:T(8,128)S(1)} %bitcast.10), channel_id=1, replica_groups=mesh['grp'=8,'mem'=16] {'grp','mem'}, dimensions={0} | all-to-all | bytes 2097152 | tf_op jit(solution)/shard_map/all_to_all | solution.py:269
  103.5 1.9 %shard_map.60 = f32[2,256,512]{2,1,0:T(8,128)} custom-call(s32[1,256]{1,0:T(1,128)S(1)} %bitcast.14, f32[2048,128]{1,0:T(8,128)S(1)} %bitcast.11), custom_call_target="tpu_custom_call" | custom-call | tf_op jit(solution)/shard_map/pallas_call | solution.py:258
Async XLA Ops:
  0.0 1.6 %copy-start = (f32[2,256,1024]{2,1,0:T(8,128)S(1)}, f32[2,256,1024]{2,1,0:T(8,128)}, u32[]{:S(2)}) copy-start(f32[2,256,1024]{2,1,0:T(8,128)} %obs_ref.1) | copy-start | bytes 6291460
  1.6 0.7 copy-start.4
  4.7 11.2 %copy-start.1 = (f32[2,256,512]{2,1,0:T(8,128)S(1)}, f32[2,256,512]{2,1,0:T(8,128)}, u32[]{:S(2)}) copy-start(f32[2,256,512]{2,1,0:T(8,128)} %states_ref.1) | copy-start | bytes 3145732
  4.7 11.2 %copy-start.5 = (s32[256]{0:T(256)S(1)}, s32[256]{0:T(256)}, u32[]{:S(2)}) copy-start(s32[256]{0:T(256)} %param.9) | copy-start | bytes 3076
  4.7 35.6 %all-to-all-start.1 = ((f32[128,24,128]{2,1,0:T(8,128)}), f32[128,24,128]{2,1,0:T(8,128)S(1)}, u32[]{:S(2)}, u32[]{:S(2)}) async-start(f32[128,24,128]{2,1,0:T(8,128)} %bitcast.4), calls=%async_computation.1 | async-start | bytes 3145728 | tf_op jit(solution)/shard_map/all_to_all | solution.py:269
  16.0 1.2 %copy-start.2 = (f32[256,1024]{1,0:T(8,128)S(1)}, f32[256,1024]{1,0:T(8,128)}, u32[]{:S(2)}) copy-start(f32[256,1024]{1,0:T(8,128)} %value_ref.1) | copy-start | bytes 3145732
  17.2 1.2 %copy-start.3 = (f32[256,1024]{1,0:T(8,128)S(1)}, f32[256,1024]{1,0:T(8,128)}, u32[]{:S(2)}) copy-start(f32[256,1024]{1,0:T(8,128)} %precision_ref.1) | copy-start | bytes 3145732
  55.5 23.7 %all-to-all-start = ((f32[128,16,128]{2,1,0:T(8,128)}), f32[128,16,128]{2,1,0:T(8,128)S(1)}, u32[]{:S(2)}, u32[]{:S(2)}) async-start(f32[128,16,128]{2,1,0:T(8,128)} %bitcast.2), calls=%async_computation | async-start | bytes 2097152 | tf_op jit(solution)/shard_map/all_to_all | solution.py:269

commit v2 on v1

v2 whole, which is shorter than its diff:
```python
import functools

import jax
import jax.numpy as jnp
from jax import lax
from jax.experimental import pallas as pl
from jax.experimental.pallas import tpu as pltpu
from jax.sharding import PartitionSpec as P

SWEEPS = 8
LANES = 128
AXES = ("grp", "mem")
F32 = jnp.float32
BF16 = jnp.bfloat16
VMEM_LIMIT = 12 << 20


def dot(a, b):
    return jnp.dot(a, b, preferred_element_type=F32)


def dot_nt(a, b):
    return lax.dot_general(a, b, (((1,), (1,)), ((), ())), preferred_element_type=F32)


def exact_dot(a, b):
    return jnp.dot(a, b, preferred_element_type=F32, precision=lax.Precision.HIGHEST)


def halves(x):
    high = x.astype(BF16)
    return high, (x - high.astype(F32)).astype(BF16)


def thirds(x):
    high = x.astype(BF16)
    rest = x - high.astype(F32)
    mid = rest.astype(BF16)
    return high, mid, (rest - mid.astype(F32)).astype(BF16)


def left_form(x):
    high, low = halves(x)
    return jnp.concatenate([high, high, low], axis=1)


def right_form(x):
    high, low = halves(x)
    return jnp.concatenate([high, low, high], axis=0)


def owners(counts, half, devices):
    patches = counts.shape[1]
    heavy = (counts > half).astype(F32)
    before = lax.broadcasted_iota(jnp.int32, (patches, patches), 0) < lax.broadcasted_iota(
        jnp.int32, (patches, patches), 1
    )
    rank = dot(jnp.broadcast_to(heavy, (8, patches)).astype(BF16), before.astype(F32).astype(BF16))[:1]
    position = lax.broadcasted_iota(jnp.int32, (1, patches), 1).astype(F32)
    device = lax.broadcasted_iota(jnp.int32, (devices, patches), 0).astype(F32)
    heavies = jnp.where((device == rank) & (heavy > 0.0), 1.0, 0.0)
    lights = jnp.where((device == position - rank) & (heavy == 0.0), 1.0, 0.0)
    return heavies, lights


def store_rows(ref, first, stride, x):
    for j in range(x.shape[1] // LANES):
        ref[pl.ds(first + j, x.shape[0], stride=stride), :] = x[:, j * LANES : (j + 1) * LANES]


def gather_rows(ref, first, stride, rows, blocks):
    return jnp.concatenate([ref[pl.ds(first + j, rows, stride=stride), :] for j in range(blocks)], axis=1)


def load_rows(ref, first, rows, blocks):
    return jnp.concatenate([ref[first + j * rows : first + (j + 1) * rows] for j in range(blocks)], axis=1)


def pick(onehot, x):
    chosen = onehot.astype(BF16)
    return dot(jnp.concatenate([chosen] * 3, axis=1), jnp.concatenate(thirds(x), axis=0))


def pack_obs_kernel(counts_hbm, obs_hbm, out_hbm, counts_ref, obs_ref, out_ref, sems):
    local, patches, slots = obs_hbm.shape
    half = slots // 2
    pieces, wide = obs_ref.shape[1], obs_ref.shape[3]
    blocks = slots // LANES
    per = (slots + half) // LANES * local
    devices = out_ref.shape[0] // per
    count_copy = pltpu.make_async_copy(counts_hbm, counts_ref, sems.at[local * pieces])
    count_copy.start()
    copies = {}
    for m in range(local):
        for j in range(pieces):
            copies[m, j] = pltpu.make_async_copy(
                obs_hbm.at[m, :, pl.ds(j * wide, wide)], obs_ref.at[m, j], sems.at[m * pieces + j]
            )
            copies[m, j].start()
    count_copy.wait()
    heavies, lights = owners(counts_ref[...], half, devices)
    both = jnp.concatenate([heavies, lights], axis=0)
    for m in range(local):
        for j in range(pieces):
            copies[m, j].wait()
            first = j * wide // LANES
            if (j + 1) * wide <= half:
                chosen = pick(both, obs_ref[m, j])
                store_rows(out_ref, local * blocks + m * blocks // 2 + first, per, chosen[devices:])
            else:
                chosen = pick(heavies, obs_ref[m, j])
            store_rows(out_ref, m * blocks + first, per, chosen[:devices])
    done = pltpu.make_async_copy(out_ref, out_hbm, sems.at[local * pieces])
    done.start()
    done.wait()


def pack_states_kernel(mine_ref, counts_ref, states_ref, value_ref, precision_ref, out_ref, rows_ref):
    local, patches, cells = states_ref.shape
    slots = value_ref.shape[1]
    blocks = cells // LANES
    per = 2 * local * blocks + 1
    devices = out_ref.shape[0] // per
    counts = counts_ref[...]
    heavies, lights = owners(counts, slots // 2, devices)
    both = jnp.concatenate([heavies, lights], axis=0)
    for m in range(local):
        chosen = pick(both, states_ref[m])
        for k in range(2):
            store_rows(out_ref, (k * local + m) * blocks, per, chosen[k * devices : (k + 1) * devices])
    out_ref[pl.ds(per - 1, devices, stride=per), :] = jnp.zeros((devices, LANES), F32)
    here = lax.broadcasted_iota(jnp.int32, (devices, patches), 0) == mine_ref[0]
    own = [jnp.sum(jnp.where(here, onehot, 0.0), axis=0, keepdims=True) for onehot in (heavies, lights)]
    both = jnp.concatenate(own + [jnp.zeros((6, patches), F32)], axis=0)
    values = pick(both, value_ref[...])
    precisions = pick(both, precision_ref[...])
    slot = lax.broadcasted_iota(jnp.int32, (1, slots), 1).astype(F32)
    rows = []
    for k in range(2):
        count = jnp.sum(own[k] * counts.astype(F32), axis=1, keepdims=True)
        live = jnp.where(slot < count, 1.0, 0.0)
        rows += [values[k : k + 1], precisions[k : k + 1], live]
    rows_ref[...] = jnp.concatenate(rows + [jnp.zeros((2, slots), F32)], axis=0)


def obs_columns(obs_ref, rows_ref, local):
    slots = rows_ref.shape[1]
    half = slots // 2
    per = (slots + half) // LANES * local
    devices = obs_ref.shape[0] // per
    for k in range(2):
        width = slots if k == 0 else half
        base = 0 if k == 0 else local * (slots // LANES)
        for c in range(width // LANES):
            columns = slice(c * LANES, (c + 1) * LANES)
            parts = [
                obs_ref[pl.ds(base + m * (width // LANES) + c, devices, stride=per), :] for m in range(local)
            ]
            mean = sum(jnp.sum(p, axis=0, keepdims=True) for p in parts) * (1.0 / (local * devices))
            value, precision, live = (rows_ref[3 * k + i : 3 * k + i + 1, columns] for i in range(3))
            yield k, columns, [p - mean for p in parts], value - mean, precision, live


def sums_kernel(obs_ref, rows_ref, out_ref, *, local):
    members = local * out_ref.shape[0]
    misfit = jnp.zeros((1, LANES), F32)
    expected = jnp.zeros((1, LANES), F32)
    for _, _, parts, innov, precision, live in obs_columns(obs_ref, rows_ref, local):
        spread = sum(jnp.sum(p * p, axis=0, keepdims=True) for p in parts) * (1.0 / (members - 1.0))
        misfit += precision * live * innov * innov
        expected += live * (1.0 + precision * spread)
    lane = lax.broadcasted_iota(jnp.int32, (1, LANES), 1)
    row = jnp.where(
        lane == 0,
        jnp.sum(misfit, axis=1, keepdims=True),
        jnp.where(lane == 1, jnp.sum(expected, axis=1, keepdims=True), 0.0),
    )
    out_ref[...] = jnp.broadcast_to(row[None], out_ref.shape)


def place_kernel(sums_ref, states_hbm, out_hbm, sem):
    copy = pltpu.make_async_copy(sums_ref, out_hbm.at[:, out_hbm.shape[1] - 1], sem)
    copy.start()
    copy.wait()


def gram_kernel(obs_ref, rows_ref, powers_ref, side_ref, high_ref, low_ref, *, local):
    slots = rows_ref.shape[1]
    members = side_ref.shape[2]
    devices = members // local
    for k, columns, parts, innov, precision, live in obs_columns(obs_ref, rows_ref, local):
        scale = jnp.sqrt(precision * live)
        for m in range(local):
            high, low = halves(parts[m] * scale)
            high_ref[k, m * devices : (m + 1) * devices, columns] = high
            low_ref[k, m * devices : (m + 1) * devices, columns] = low
        high, low = halves(jnp.broadcast_to(scale * innov, (16, LANES)))
        high_ref[k, members:, columns] = high
        low_ref[k, members:, columns] = low
    diagonal = lax.broadcasted_iota(jnp.int32, (members, members), 0) == lax.broadcasted_iota(
        jnp.int32, (members, members), 1
    )
    for k in range(2):
        width = slots if k == 0 else slots // 2
        high, low = high_ref[k, :, :width], low_ref[k, :, :width]
        gram = dot_nt(high, high[:members]) + dot_nt(high, low[:members]) + dot_nt(low, high[:members])
        forcing = gram[members : members + 8]
        gram = gram[:members]
        size = jnp.sqrt(jnp.sum(jnp.sum(gram * gram, axis=0, keepdims=True), axis=1, keepdims=True))
        unit = gram / jnp.maximum(size, 1e-30)
        trace = jnp.sum(
            jnp.sum(jnp.where(diagonal, unit, 0.0), axis=0, keepdims=True), axis=1, keepdims=True
        )
        second = exact_dot(unit, unit)
        for i, power in enumerate((unit, second, exact_dot(unit, second))):
            for h in range(members // LANES):
                first = ((k * 3 + i) * (members // LANES) + h) * members
                powers_ref[first : first + members] = power[:, h * LANES : (h + 1) * LANES]
        side_ref[k] = jnp.concatenate(
            [forcing, jnp.broadcast_to(size, (8, members)), jnp.broadcast_to(trace, (8, members))], axis=0
        )


def update_kernel(states_ref, powers_ref, side_ref, out_ref, s_left, sz_right, states_right, *, local):
    members = side_ref.shape[2]
    devices = members // local
    per = states_ref.shape[0] // devices
    blocks = out_ref.shape[0] // devices // (2 * local)
    total = jnp.sum(states_ref[pl.ds(per - 1, devices, stride=per), :], axis=0, keepdims=True)
    lane = lax.broadcasted_iota(jnp.int32, total.shape, 1)
    misfit = jnp.sum(jnp.where(lane == 0, total, 0.0), axis=1, keepdims=True)
    expected = jnp.sum(jnp.where(lane == 1, total, 0.0), axis=1, keepdims=True)
    squared = misfit / expected
    inflation = jnp.sqrt(squared)
    diagonal = lax.broadcasted_iota(jnp.int32, (members, members), 0) == lax.broadcasted_iota(
        jnp.int32, (members, members), 1
    )
    free = members - 1.0

    def plus_diagonal(x, value):
        return x + jnp.where(diagonal, value, 0.0)

    def refine(k, product):
        s = s_left[k, :, :members].astype(F32) + s_left[k, :, 2 * members :].astype(F32)
        return dot(left_form(plus_diagonal(0.25 * product - 1.5 * s, 2.25)), sz_right[k, :, :members])

    scalers = []
    for k in range(2):
        size, trace = side_ref[k, 8:9, :1], side_ref[k, 16:17, :1]
        strength = squared * size
        scaler = jnp.sqrt(free * free * members + strength * (2.0 * free * trace + strength))
        scalers.append(scaler)
        a, b = free / scaler, strength / scaler
        f = 1.5 - 0.5 * a
        s1 = (a * f * f, b * f * (f - a), b * b * (0.25 * a - f), 0.25 * b * b * b)
        powers = [
            load_rows(powers_ref, (k * 3 + i) * (members // LANES) * members, members, members // LANES)
            for i in range(3)
        ]
        s = plus_diagonal(sum(c * p for c, p in zip(s1[1:], powers)), s1[0])
        z = plus_diagonal(-0.5 * b * powers[0], f)
        s_left[k] = left_form(s)
        sz_right[k, :, :members] = right_form(s)
        sz_right[k, :, members:] = right_form(z)
    def times(k):
        z = sz_right[k, :members, members:].astype(F32) + sz_right[k, members : 2 * members, members:].astype(F32)
        return z

    def sweep(_, carry):
        for k in range(2):
            product = dot(s_left[k], sz_right[k])
            z = 1.5 * times(k) - 0.5 * product[:, members:]
            s = refine(k, product[:, :members])
            s_left[k] = left_form(s)
            sz_right[k, :, :members] = right_form(s)
            sz_right[k, :, members:] = right_form(z)
        return carry

    lax.fori_loop(0, SWEEPS - 2, sweep, 0)
    for k in range(2):
        centers = []
        for c in range(blocks):
            rows = [(k * local + m) * blocks + c for m in range(local)]
            parts = [states_ref[pl.ds(r, devices, stride=per), :] for r in rows]
            center = sum(jnp.sum(p, axis=0, keepdims=True) for p in parts) * (1.0 / members)
            centers.append(center)
            for m in range(local):
                high, low = halves(parts[m] - center)
                span = slice(m * devices, (m + 1) * devices)
                columns = slice(c * LANES, (c + 1) * LANES)
                states_right[span, columns] = high
                states_right[members + m * devices : members + (m + 1) * devices, columns] = low
                states_right[2 * members + m * devices : 2 * members + (m + 1) * devices, columns] = high
        product = dot(s_left[k], sz_right[k, :, members:])
        root = (1.5 * times(k) - 0.5 * product) / jnp.sqrt(scalers[k])
        root_right = right_form(root)
        forcing = inflation * side_ref[k, :8]
        shifts = dot(left_form(dot(left_form(forcing), root_right)), root_right)[:1]
        transform = inflation * (free**0.5 * root + shifts)
        update = dot(left_form(transform), states_right[...])
        for c in range(blocks):
            for m in range(local):
                piece = update[m * devices : (m + 1) * devices, c * LANES : (c + 1) * LANES] + centers[c]
                out_ref[pl.ds((k * local + m) * blocks + c, devices, stride=2 * local * blocks), :] = piece


def unpack_kernel(counts_ref, rows_ref, out_hbm, out_ref, sems, *, half):
    local, patches, cells = out_ref.shape
    blocks = cells // LANES
    per = 2 * local * blocks
    devices = rows_ref.shape[0] // per
    onehot = jnp.concatenate(owners(counts_ref[...], half, devices), axis=0).T
    copies = []
    for m in range(local):
        for part in range(2):
            wide = blocks // 2
            x = jnp.concatenate(
                [gather_rows(rows_ref, (k * local + m) * blocks + part * wide, per, devices, wide) for k in range(2)],
                axis=0,
            )
            columns = pl.ds(part * wide * LANES, wide * LANES)
            out_ref[m, :, columns] = pick(onehot, x)
            copies.append(
                pltpu.make_async_copy(
                    out_ref.at[m, :, columns], out_hbm.at[m, :, columns], sems.at[2 * m + part]
                )
            )
            copies[-1].start()
    for copy in copies:
        copy.wait()


HBM = pl.BlockSpec(memory_space=pltpu.HBM)
WHOLE = pl.BlockSpec(memory_space=pltpu.VMEM)
SCALAR = pl.BlockSpec(memory_space=pltpu.SMEM)


def call(kernel, out_shapes, inputs, ins=None, outs=None, scratch=(), aliases={}, limit=VMEM_LIMIT):
    return pl.pallas_call(
        kernel,
        out_shape=[jax.ShapeDtypeStruct(s, F32) for s in out_shapes],
        in_specs=ins or [WHOLE] * len(inputs),
        out_specs=outs or [WHOLE] * len(out_shapes),
        scratch_shapes=list(scratch),
        input_output_aliases=aliases,
        compiler_params=pltpu.CompilerParams(vmem_limit_bytes=limit),
    )(*inputs)


def exchange(x, name):
    with jax.named_scope(name):
        rows = x.reshape(-1, 1, LANES)
        return lax.all_to_all(rows, AXES, split_axis=0, concat_axis=0, tiled=True).reshape(-1, LANES)


def per_device(background, obs_ensemble, obs_value, obs_precision, obs_count):
    devices = lax.axis_size(AXES)
    local, patches, cells = background.shape
    slots = obs_ensemble.shape[2]
    half = slots // 2
    members = local * devices
    counts = obs_count.reshape(1, patches)
    mine = lax.axis_index(AXES).astype(jnp.int32).reshape(1)
    obs_rows = (slots + half) // LANES * local
    state_rows = 2 * local * cells // LANES
    pieces = 4
    (obs_sent,) = call(
        pack_obs_kernel,
        [(devices * obs_rows, LANES)],
        (counts, obs_ensemble),
        ins=[HBM, HBM],
        outs=[HBM],
        scratch=[
            pltpu.VMEM((1, patches), jnp.int32),
            pltpu.VMEM((local, pieces, patches, slots // pieces), F32),
            pltpu.VMEM((devices * obs_rows, LANES), F32),
            pltpu.SemaphoreType.DMA((local * pieces + 1,)),
        ],
        limit=None,
    )
    obs = exchange(obs_sent, "obs_exchange")
    states_sent, rows = call(
        pack_states_kernel,
        [(devices * (state_rows + 1), LANES), (8, slots)],
        (mine, counts, background, obs_value, obs_precision),
        ins=[SCALAR] + [WHOLE] * 4,
        limit=None,
    )
    states_sent = states_sent.reshape(devices, state_rows + 1, 1, LANES)
    (sums,) = call(functools.partial(sums_kernel, local=local), [(devices, 1, LANES)], (obs, rows))
    (states_sent,) = call(
        place_kernel,
        [states_sent.shape],
        (sums, states_sent),
        ins=[WHOLE, HBM],
        outs=[HBM],
        scratch=[pltpu.SemaphoreType.DMA],
        aliases={1: 0},
        limit=None,
    )
    states = exchange(states_sent, "states_exchange")
    powers, side = call(
        functools.partial(gram_kernel, local=local),
        [obs.shape, (2, 24, members)],
        (obs, rows),
        scratch=[pltpu.VMEM((2, members + 16, slots), BF16)] * 2,
        aliases={0: 0},
    )
    (update,) = call(
        functools.partial(update_kernel, local=local),
        [(devices * state_rows, LANES)],
        (states, powers, side),
        scratch=[
            pltpu.VMEM((2, members, 3 * members), BF16),
            pltpu.VMEM((2, 3 * members, 2 * members), BF16),
            pltpu.VMEM((3 * members, cells), BF16),
        ],
    )
    returned = exchange(update, "return_exchange")
    (analysis,) = call(
        functools.partial(unpack_kernel, half=half),
        [(local, patches, cells)],
        (counts, returned),
        outs=[HBM],
        scratch=[pltpu.VMEM((local, patches, cells), F32), pltpu.SemaphoreType.DMA((2 * local,))],
    )
    return analysis


def solution(mesh):
    placed = (P(AXES, None, None), P(AXES, None, None), P(), P(), P())
    return jax.shard_map(
        per_device, mesh=mesh, in_specs=placed, out_specs=P(AXES, None, None), check_vma=False
    )
```

time: 106 us -> 102 us (0.962)
  blocking collectives: 36.5 us -> 23 us
  waiting for transfers between devices: 29.4 us -> 36.2 us
  Pallas kernels: 18.9 us -> 24.8 us
  local copies, waits for them, and re-layouts: 4.72 us -> 1.39 us
    all_to_all x2 -> x1, blocking collectives: 36.5 us -> 23 us  [exchange(): lax.all_to_all(rows, AXES, split_axis=0, concat_axis=0, tiled=True)]
    all_to_all x2, waiting for transfers between devices: 29.4 us -> 36.2 us  [exchange(): lax.all_to_all(rows, AXES, split_axis=0, concat_axis=0, tiled=True)]
    pallas_call x6 -> x7, Pallas kernels: 18.9 us -> 24.8 us  [call(): pl.pallas_call(kernel, out_shape=[jax.ShapeDtypeStruct(s, F32) for s in o...]
    unnamed x12 -> x8, local copies, waits for them, and re-layouts: 4.72 us -> 1.39 us
  transfers between devices with their start and end apart: 2 -> 2, of which waited for: 2 -> 2; matrix products, arithmetic and copies ran while one was open for 0% -> 0% of each run, Pallas kernels for 11% -> 8%
where the time goes in v2:
time: 102 us; the launch traced here: 101 us
  waiting for transfers between devices  36.2 us (35%)
  Pallas kernels  24.8 us (24%)
  blocking collectives  23 us (23%)
  starting transfers between devices  15.8 us (15%)
  local copies, waits for them, and re-layouts  1.39 us (1%)
    all_to_all x2, waiting for transfers between devices, exchange(): lax.all_to_all(rows, AXES, split_axis=0, concat_axis=0, tiled=True)  36.2 us
    pallas_call x7, Pallas kernels, call(): pl.pallas_call(kernel, out_shape=[jax.ShapeDtypeStruct(s, F32) for s in o...  24.8 us
    all_to_all x1, blocking collectives, exchange(): lax.all_to_all(rows, AXES, split_axis=0, concat_axis=0, tiled=True)  23 us
    all_to_all x2, starting transfers between devices, exchange(): lax.all_to_all(rows, AXES, split_axis=0, concat_axis=0, tiled=True)  15.8 us
  transfers between devices with their start and end apart: 2, of which 2 were waited for; matrix products, arithmetic and copies ran while one was open for 0% of the time, Pallas kernels for 8%

profile of v2, /device:TPU:0, one launch (start us, length us, event | category | flops | bytes accessed | tf_op | source)
XLA Modules:
  0.0 101.4 jit_solution(7259474210025696138)
XLA Ops:
  0.0 4.6 %shard_map.55 = f32[3072,128]{1,0:T(8,128)} custom-call(s32[1,256]{1,0:T(1,128)} %bitcast.20, f32[2,256,1024]{2,1,0:T(8,128)} %obs_hbm.1), custom_call_target="tpu_custom_call" | custom-call | tf_op jit(solution)/shard_map/pallas_call | solution.py:339
  4.6 11.2 %all-to-all-start = ((f32[3072,1,128]{2,1,0:T(1,128)}), f32[3072,1,128]{2,1,0:T(1,128)S(1)}, u32[]{:S(2)}, u32[]{:S(2)}) async-start(f32[3072,1,128]{2,1,0:T(1,128)} %bitcast.23), calls=%async_computation | async-start | bytes 3145728 | tf_op jit(solution)/shard_map/obs_exchange/all_to_all | solution.py:353
  15.8 3.7 %shard_map.56 = (f32[2176,128]{1,0:T(8,128)}, f32[8,1024]{1,0:T(8,128)}) custom-call(s32[1]{0:T(128)} %bitcast.4.mine_ref, s32[1,256]{1,0:T(1,128)} %bitcast.21, f32[2,256,512]{2,1,0:T(8,128)} %states_ref.1, f32[256,1024]{1,0:T(8,128)} %value_ref.1, f32[256,1024]{1,0:T(8,128)} %precision_ref.1), custom_call_target="tpu_custom_call" | custom-call | tf_op jit(solution)/shard_map/pallas_call | solution.py:339
  19.5 20.7 %all-to-all-done = f32[3072,1,128]{2,1,0:T(1,128)S(1)} async-done(((f32[3072,1,128]{2,1,0:T(1,128)}), f32[3072,1,128]{2,1,0:T(1,128)S(1)}, u32[]{:S(2)}, u32[]{:S(2)}) %all-to-all-start) | async-done | bytes 1572896 | tf_op jit(solution)/shard_map/obs_exchange/all_to_all | solution.py:353
  40.3 0.0 copy-start.1
  40.3 0.8 copy-done.1
  41.0 0.5 shard_map.57.sums_ref
  41.6 0.0 copy-start
  41.6 0.6 copy-done
  42.2 1.5 %shard_map.58 = f32[128,17,1,128]{3,2,1,0:T(1,128)} custom-call(f32[128,1,128]{2,1,0:T(1,128)} %copy-done, f32[128,17,1,128]{3,2,1,0:T(1,128)} %bitcast.24), custom_call_target="tpu_custom_call", output_to_operand_aliasing={{}: (1, {})} | custom-call | tf_op jit(solution)/shard_map/pallas_call | solution.py:339
  43.7 0.0 copy-start.2
  43.7 4.6 %all-to-all-start.1 = ((f32[2176,1,128]{2,1,0:T(1,128)}), f32[2176,1,128]{2,1,0:T(1,128)S(1)}, u32[]{:S(2)}, u32[]{:S(2)}) async-start(f32[2176,1,128]{2,1,0:T(1,128)} %bitcast.25), calls=%async_computation.1 | async-start | bytes 2228224 | tf_op jit(solution)/shard_map/states_exchange/all_to_all | solution.py:353
  48.4 0.0 copy-done.2
  48.4 4.2 %shard_map.59 = (f32[3072,128]{1,0:T(8,128)S(1)}, f32[2,24,256]{2,1,0:T(8,128)S(1)}) custom-call(f32[3072,128]{1,0:T(8,128)S(1)} %bitcast.16, f32[8,1024]{1,0:T(8,128)S(1)} %copy-done.2), custom_call_target="tpu_custom_call", output_to_operand_aliasing={{0}: (0, {})} | custom-call | tf_op jit(solution)/shard_map/pallas_call | solution.py:339
  52.6 15.5 %all-to-all-done.1 = f32[2176,1,128]{2,1,0:T(1,128)S(1)} async-done(((f32[2176,1,128]{2,1,0:T(1,128)}), f32[2176,1,128]{2,1,0:T(1,128)S(1)}, u32[]{:S(2)}, u32[]{:S(2)}) %all-to-all-start.1) | async-done | bytes 1114144 | tf_op jit(solution)/shard_map/states_exchange/all_to_all | solution.py:353
  68.1 8.5 %shard_map.60 = f32[2048,128]{1,0:T(8,128)S(1)} custom-call(f32[2176,128]{1,0:T(8,128)S(1)} %bitcast.17, f32[3072,128]{1,0:T(8,128)S(1)} %get-tuple-element.11.powers_ref, f32[2,24,256]{2,1,0:T(8,128)S(1)} %get-tuple-element.12.side_ref), custom_call_target="tpu_custom_call" | custom-call | tf_op jit(solution)/shard_map/pallas_call | solution.py:339
  76.5 0.0 copy-start.3
  76.5 23.0 %all_to_all.15 = f32[2048,1,128]{2,1,0:T(1,128)S(1)} all-to-all(f32[2048,1,128]{2,1,0:T(1,128)S(1)} %bitcast.19), channel_id=1, replica_groups=mesh['grp'=8,'mem'=16] {'grp','mem'}, dimensions={0} | all-to-all | bytes 2097152 | tf_op jit(solution)/shard_map/return_exchange/all_to_all | solution.py:353
  99.6 0.0 copy-done.3
  99.6 1.8 %shard_map.61 = f32[2,256,512]{2,1,0:T(8,128)} custom-call(s32[1,256]{1,0:T(1,128)S(1)} %bitcast.22, f32[2048,128]{1,0:T(8,128)S(1)} %bitcast.18), custom_call_target="tpu_custom_call" | custom-call | tf_op jit(solution)/shard_map/pallas_call | solution.py:339
Async XLA Ops:
  4.6 35.7 %all-to-all-start = ((f32[3072,1,128]{2,1,0:T(1,128)}), f32[3072,1,128]{2,1,0:T(1,128)S(1)}, u32[]{:S(2)}, u32[]{:S(2)}) async-start(f32[3072,1,128]{2,1,0:T(1,128)} %bitcast.23), calls=%async_computation | async-start | bytes 3145728 | tf_op jit(solution)/shard_map/obs_exchange/all_to_all | solution.py:353
  40.3 0.8 copy-start.1
  41.6 0.6 copy-start
  43.7 4.7 %copy-start.2 = (f32[8,1024]{1,0:T(8,128)S(1)}, f32[8,1024]{1,0:T(8,128)}, u32[]{:S(2)}) copy-start(f32[8,1024]{1,0:T(8,128)} %get-tuple-element.9.rows_ref) | copy-start | bytes 98308
  43.7 24.4 %all-to-all-start.1 = ((f32[2176,1,128]{2,1,0:T(1,128)}), f32[2176,1,128]{2,1,0:T(1,128)S(1)}, u32[]{:S(2)}, u32[]{:S(2)}) async-start(f32[2176,1,128]{2,1,0:T(1,128)} %bitcast.25), calls=%async_computation.1 | async-start | bytes 2228224 | tf_op jit(solution)/shard_map/states_exchange/all_to_all | solution.py:353
  76.5 23.0 %copy-start.3 = (s32[256]{0:T(256)S(1)}, s32[256]{0:T(256)}, u32[]{:S(2)}) copy-start(s32[256]{0:T(256)} %param.9) | copy-start | bytes 3076

commit v3 on v2

--- a/solution.py
+++ b/solution.py
@@ -81,41 +81,54 @@
     return dot(jnp.concatenate([chosen] * 3, axis=1), jnp.concatenate(thirds(x), axis=0))
 
 
-def pack_obs_kernel(counts_hbm, obs_hbm, out_hbm, counts_ref, obs_ref, out_ref, sems):
-    local, patches, slots = obs_hbm.shape
-    half = slots // 2
-    pieces, wide = obs_ref.shape[1], obs_ref.shape[3]
+def pack_obs_kernel(counts_hbm, obs_hbm, out_hbm, counts_ref, obs_ref, out_ref, table_ref, table, sems, *, slots):
+    patches = counts_ref.shape[1]
     blocks = slots // LANES
-    per = (slots + half) // LANES * local
-    devices = out_ref.shape[0] // per
-    count_copy = pltpu.make_async_copy(counts_hbm, counts_ref, sems.at[local * pieces])
+    each = patches * blocks
+    local = obs_hbm.shape[0] // each
+    devices, per = out_hbm.shape[:2]
+    count_copy = pltpu.make_async_copy(counts_hbm, counts_ref, sems.at[0])
     count_copy.start()
-    copies = {}
+    copies = []
     for m in range(local):
-        for j in range(pieces):
-            copies[m, j] = pltpu.make_async_copy(
-                obs_hbm.at[m, :, pl.ds(j * wide, wide)], obs_ref.at[m, j], sems.at[m * pieces + j]
+        span = pl.ds(m * each, each)
+        copies.append(pltpu.make_async_copy(obs_hbm.at[span], obs_ref.at[span], sems.at[1 + m]))
+        copies[-1].start()
+    count_copy.wait()
+    onehots = owners(counts_ref[...], slots // 2, devices)
+    position = lax.broadcasted_iota(jnp.int32, (8, patches), 1).astype(F32).astype(BF16)
+    index = [dot_nt(position, onehot.astype(BF16)).astype(jnp.int32) for onehot in onehots]
+    start = [(p >> 3) * (8 * blocks) + (p & 7) for p in index]
+    row = lax.broadcasted_iota(jnp.int32, (8, devices), 0)
+    table_ref[...] = jnp.where(row == 0, start[0], start[1])
+    table_copy = pltpu.make_async_copy(table_ref, table, sems.at[1 + local])
+    table_copy.start()
+    table_copy.wait()
+    sent = []
+    for m in range(local):
+        copies[m].wait()
+
+        @pl.loop(0, devices, unroll=8)
+        def _(d):
+            heavy = m * each + table[0, d]
+            light = m * each + table[1, d]
+            out_ref[d, m * blocks : (m + 1) * blocks, :] = obs_ref[pl.ds(heavy, blocks, stride=8), :]
+            first = local * blocks + m * blocks // 2
+            out_ref[d, first : first + blocks // 2, :] = obs_ref[pl.ds(light, blocks // 2, stride=8), :]
+
+        first = m * blocks
+        last = first + blocks if m < local - 1 else per
+        sent.append(
+            pltpu.make_async_copy(
+                out_ref.at[:, first:last], out_hbm.at[:, first:last], sems.at[2 + local + m]
             )
-            copies[m, j].start()
-    count_copy.wait()
-    heavies, lights = owners(counts_ref[...], half, devices)
-    both = jnp.concatenate([heavies, lights], axis=0)
-    for m in range(local):
-        for j in range(pieces):
-            copies[m, j].wait()
-            first = j * wide // LANES
-            if (j + 1) * wide <= half:
-                chosen = pick(both, obs_ref[m, j])
-                store_rows(out_ref, local * blocks + m * blocks // 2 + first, per, chosen[devices:])
-            else:
-                chosen = pick(heavies, obs_ref[m, j])
-            store_rows(out_ref, m * blocks + first, per, chosen[:devices])
-    done = pltpu.make_async_copy(out_ref, out_hbm, sems.at[local * pieces])
-    done.start()
-    done.wait()
-
-
-def pack_states_kernel(mine_ref, counts_ref, states_ref, value_ref, precision_ref, out_ref, rows_ref):
+        )
+        sent[-1].start()
+    for copy in sent:
+        copy.wait()
+
+
+def pack_states_kernel(mine_ref, counts_ref, states_ref, value_ref, precision_ref, out_hbm, rows_ref, out_ref, sem):
     local, patches, cells = states_ref.shape
     slots = value_ref.shape[1]
     blocks = cells // LANES
@@ -129,6 +142,8 @@
         for k in range(2):
             store_rows(out_ref, (k * local + m) * blocks, per, chosen[k * devices : (k + 1) * devices])
     out_ref[pl.ds(per - 1, devices, stride=per), :] = jnp.zeros((devices, LANES), F32)
+    copy = pltpu.make_async_copy(out_ref, out_hbm, sem)
+    copy.start()
     here = lax.broadcasted_iota(jnp.int32, (devices, patches), 0) == mine_ref[0]
     own = [jnp.sum(jnp.where(here, onehot, 0.0), axis=0, keepdims=True) for onehot in (heavies, lights)]
     both = jnp.concatenate(own + [jnp.zeros((6, patches), F32)], axis=0)
@@ -141,6 +156,7 @@
         live = jnp.where(slot < count, 1.0, 0.0)
         rows += [values[k : k + 1], precisions[k : k + 1], live]
     rows_ref[...] = jnp.concatenate(rows + [jnp.zeros((2, slots), F32)], axis=0)
+    copy.wait()
 
 
 def obs_columns(obs_ref, rows_ref, local):
@@ -161,8 +177,9 @@
             yield k, columns, [p - mean for p in parts], value - mean, precision, live
 
 
-def sums_kernel(obs_ref, rows_ref, out_ref, *, local):
-    members = local * out_ref.shape[0]
+def sums_kernel(obs_ref, rows_ref, states_hbm, out_hbm, row_ref, sem, *, local):
+    devices, per = out_hbm.shape[:2]
+    members = local * devices
     misfit = jnp.zeros((1, LANES), F32)
     expected = jnp.zeros((1, LANES), F32)
     for _, _, parts, innov, precision, live in obs_columns(obs_ref, rows_ref, local):
@@ -175,19 +192,21 @@
         jnp.sum(misfit, axis=1, keepdims=True),
         jnp.where(lane == 1, jnp.sum(expected, axis=1, keepdims=True), 0.0),
     )
-    out_ref[...] = jnp.broadcast_to(row[None], out_ref.shape)
-
-
-def place_kernel(sums_ref, states_hbm, out_hbm, sem):
-    copy = pltpu.make_async_copy(sums_ref, out_hbm.at[:, out_hbm.shape[1] - 1], sem)
+    row_ref[...] = jnp.broadcast_to(row[None], row_ref.shape)
+    copy = pltpu.make_async_copy(row_ref, out_hbm.at[:, per - 1], sem)
     copy.start()
     copy.wait()
 
 
-def gram_kernel(obs_ref, rows_ref, powers_ref, side_ref, high_ref, low_ref, *, local):
+def gram_kernel(
+    obs_ref, rows_ref, counts_ref, powers_ref, fourth_ref, side_ref, spread_hbm, high_ref, low_ref, spread_ref, sem, *, local
+):
     slots = rows_ref.shape[1]
     members = side_ref.shape[2]
     devices = members // local
+    spread_ref[...] = jnp.concatenate(owners(counts_ref[...], slots // 2, devices), axis=0).T
+    copy = pltpu.make_async_copy(spread_ref, spread_hbm, sem)
+    copy.start()
     for k, columns, parts, innov, precision, live in obs_columns(obs_ref, rows_ref, local):
         scale = jnp.sqrt(precision * live)
         for m in range(local):
@@ -216,12 +235,19 @@
             for h in range(members // LANES):
                 first = ((k * 3 + i) * (members // LANES) + h) * members
                 powers_ref[first : first + members] = power[:, h * LANES : (h + 1) * LANES]
+        fourth = exact_dot(second, second)
+        for h in range(members // LANES):
+            first = (k * (members // LANES) + h) * members
+            fourth_ref[first : first + members] = fourth[:, h * LANES : (h + 1) * LANES]
         side_ref[k] = jnp.concatenate(
             [forcing, jnp.broadcast_to(size, (8, members)), jnp.broadcast_to(trace, (8, members))], axis=0
         )
-
-
-def update_kernel(states_ref, powers_ref, side_ref, out_ref, s_left, sz_right, states_right, *, local):
+    copy.wait()
+
+
+def update_kernel(
+    states_ref, powers_ref, fourth_ref, side_ref, out_ref, s_left, s_right, z_right, states_right, center_ref, *, local
+):
     members = side_ref.shape[2]
     devices = members // local
     per = states_ref.shape[0] // devices
@@ -240,9 +266,22 @@
     def plus_diagonal(x, value):
         return x + jnp.where(diagonal, value, 0.0)
 
+    def put(k, s):
+        s_left[k] = left_form(s)
+        s_right[k] = right_form(s)
+
+    def square(k):
+        high = s_left[k, :, :members]
+        cross = dot(high, s_right[k, members : 2 * members])
+        return dot(high, s_right[k, :members]) + (cross + cross.T)
+
     def refine(k, product):
         s = s_left[k, :, :members].astype(F32) + s_left[k, :, 2 * members :].astype(F32)
-        return dot(left_form(plus_diagonal(0.25 * product - 1.5 * s, 2.25)), sz_right[k, :, :members])
+        return dot(left_form(plus_diagonal(0.25 * product - 1.5 * s, 2.25)), s_right[k])
+
+    def advance(k):
+        z = z_right[k, :members].astype(F32) + z_right[k, members : 2 * members].astype(F32)
+        return 1.5 * z - 0.5 * dot(s_left[k], z_right[k])
 
     scalers = []
     for k in range(2):
@@ -253,63 +292,56 @@
         a, b = free / scaler, strength / scaler
         f = 1.5 - 0.5 * a
         s1 = (a * f * f, b * f * (f - a), b * b * (0.25 * a - f), 0.25 * b * b * b)
-        powers = [
-            load_rows(powers_ref, (k * 3 + i) * (members // LANES) * members, members, members // LANES)
-            for i in range(3)
-        ]
-        s = plus_diagonal(sum(c * p for c, p in zip(s1[1:], powers)), s1[0])
-        z = plus_diagonal(-0.5 * b * powers[0], f)
-        s_left[k] = left_form(s)
-        sz_right[k, :, :members] = right_form(s)
-        sz_right[k, :, members:] = right_form(z)
-    def times(k):
-        z = sz_right[k, :members, members:].astype(F32) + sz_right[k, members : 2 * members, members:].astype(F32)
-        return z
-
-    def sweep(_, carry):
-        for k in range(2):
-            product = dot(s_left[k], sz_right[k])
-            z = 1.5 * times(k) - 0.5 * product[:, members:]
-            s = refine(k, product[:, :members])
-            s_left[k] = left_form(s)
-            sz_right[k, :, :members] = right_form(s)
-            sz_right[k, :, members:] = right_form(z)
-        return carry
-
-    lax.fori_loop(0, SWEEPS - 2, sweep, 0)
-    for k in range(2):
-        centers = []
+        d = (1.5 - 0.5 * s1[0], -0.5 * s1[1], -0.5 * s1[2], -0.5 * s1[3])
+        h = -0.5 * b
+        z2 = (f * d[0], f * d[1] + h * d[0], f * d[2] + h * d[1], f * d[3] + h * d[2], h * d[3])
+        halfs = members // LANES
+        powers = [load_rows(powers_ref, (k * 3 + i) * halfs * members, members, halfs) for i in range(3)]
+        powers.append(load_rows(fourth_ref, k * halfs * members, members, halfs))
+        put(k, plus_diagonal(sum(c * p for c, p in zip(s1[1:], powers)), s1[0]))
+        z_right[k] = right_form(plus_diagonal(sum(c * p for c, p in zip(z2[1:], powers)), z2[0]))
+    for k in range(2):
+        put(k, refine(k, square(k)))
         for c in range(blocks):
             rows = [(k * local + m) * blocks + c for m in range(local)]
             parts = [states_ref[pl.ds(r, devices, stride=per), :] for r in rows]
             center = sum(jnp.sum(p, axis=0, keepdims=True) for p in parts) * (1.0 / members)
-            centers.append(center)
+            columns = slice(c * LANES, (c + 1) * LANES)
+            center_ref[k, :, columns] = jnp.broadcast_to(center, (8, LANES))
             for m in range(local):
                 high, low = halves(parts[m] - center)
-                span = slice(m * devices, (m + 1) * devices)
-                columns = slice(c * LANES, (c + 1) * LANES)
-                states_right[span, columns] = high
-                states_right[members + m * devices : members + (m + 1) * devices, columns] = low
-                states_right[2 * members + m * devices : 2 * members + (m + 1) * devices, columns] = high
-        product = dot(s_left[k], sz_right[k, :, members:])
-        root = (1.5 * times(k) - 0.5 * product) / jnp.sqrt(scalers[k])
-        root_right = right_form(root)
-        forcing = inflation * side_ref[k, :8]
-        shifts = dot(left_form(dot(left_form(forcing), root_right)), root_right)[:1]
+                for i, piece in enumerate((high, low, high)):
+                    first = i * members + m * devices
+                    states_right[k, first : first + devices, columns] = piece
+
+    def sweep(_, carry):
+        for k in range(2):
+            s = refine(k, square(k))
+            z = advance(k)
+            put(k, s)
+            z_right[k] = right_form(z)
+        return carry
+
+    lax.fori_loop(0, SWEEPS - 3, sweep, 0)
+    for k in range(2):
+        root = advance(k) / jnp.sqrt(scalers[k])
+        forcing = inflation * side_ref[k, :1]
+        half_way = jnp.sum(root * forcing, axis=1, keepdims=True)
+        shifts = jnp.sum(root * half_way, axis=0, keepdims=True)
         transform = inflation * (free**0.5 * root + shifts)
-        update = dot(left_form(transform), states_right[...])
+        update = dot(left_form(transform), states_right[k]) + center_ref[k, :1]
         for c in range(blocks):
             for m in range(local):
-                piece = update[m * devices : (m + 1) * devices, c * LANES : (c + 1) * LANES] + centers[c]
+                piece = update[m * devices : (m + 1) * devices, c * LANES : (c + 1) * LANES]
                 out_ref[pl.ds((k * local + m) * blocks + c, devices, stride=2 * local * blocks), :] = piece
 
 
-def unpack_kernel(counts_ref, rows_ref, out_hbm, out_ref, sems, *, half):
+def unpack_kernel(spread_ref, rows_ref, out_hbm, out_ref, sems):
     local, patches, cells = out_ref.shape
     blocks = cells // LANES
     per = 2 * local * blocks
     devices = rows_ref.shape[0] // per
-    onehot = jnp.concatenate(owners(counts_ref[...], half, devices), axis=0).T
+    onehot = spread_ref[...]
     copies = []
     for m in range(local):
         for part in range(2):
@@ -336,11 +368,17 @@
 
 
 def call(kernel, out_shapes, inputs, ins=None, outs=None, scratch=(), aliases={}, limit=VMEM_LIMIT):
+    ins = ins or [WHOLE] * len(inputs)
+    outs = outs or [WHOLE] * len(out_shapes)
+    inputs = [pltpu.with_memory_space_constraint(x, pltpu.HBM) if s is HBM else x for x, s in zip(inputs, ins)]
     return pl.pallas_call(
         kernel,
-        out_shape=[jax.ShapeDtypeStruct(s, F32) for s in out_shapes],
-        in_specs=ins or [WHOLE] * len(inputs),
-        out_specs=outs or [WHOLE] * len(out_shapes),
+        out_shape=[
+            pltpu.HBM(shape, F32) if s is HBM else jax.ShapeDtypeStruct(shape, F32)
+            for shape, s in zip(out_shapes, outs)
+        ],
+        in_specs=ins,
+        out_specs=outs,
         scratch_shapes=list(scratch),
         input_output_aliases=aliases,
         compiler_params=pltpu.CompilerParams(vmem_limit_bytes=limit),
@@ -357,26 +395,27 @@
     devices = lax.axis_size(AXES)
     local, patches, cells = background.shape
     slots = obs_ensemble.shape[2]
-    half = slots // 2
     members = local * devices
     counts = obs_count.reshape(1, patches)
     mine = lax.axis_index(AXES).astype(jnp.int32).reshape(1)
-    obs_rows = (slots + half) // LANES * local
+    obs_rows = 3 * slots // 2 // LANES * local
     state_rows = 2 * local * cells // LANES
-    pieces = 4
+    blocks = slots // LANES
+    in_memory = obs_ensemble.reshape(local, patches // 8, 8, blocks, LANES).swapaxes(2, 3).reshape(-1, LANES)
     (obs_sent,) = call(
-        pack_obs_kernel,
-        [(devices * obs_rows, LANES)],
-        (counts, obs_ensemble),
+        functools.partial(pack_obs_kernel, slots=slots),
+        [(devices, obs_rows, LANES)],
+        (counts, in_memory),
         ins=[HBM, HBM],
         outs=[HBM],
         scratch=[
             pltpu.VMEM((1, patches), jnp.int32),
-            pltpu.VMEM((local, pieces, patches, slots // pieces), F32),
-            pltpu.VMEM((devices * obs_rows, LANES), F32),
-            pltpu.SemaphoreType.DMA((local * pieces + 1,)),
+            pltpu.VMEM(in_memory.shape, F32),
+            pltpu.VMEM((devices, obs_rows, LANES), F32),
+            pltpu.VMEM((8, devices), jnp.int32),
+            pltpu.SMEM((8, devices), jnp.int32),
+            pltpu.SemaphoreType.DMA((2 * local + 2,)),
         ],
-        limit=None,
     )
     obs = exchange(obs_sent, "obs_exchange")
     states_sent, rows = call(
@@ -384,43 +423,50 @@
         [(devices * (state_rows + 1), LANES), (8, slots)],
         (mine, counts, background, obs_value, obs_precision),
         ins=[SCALAR] + [WHOLE] * 4,
-        limit=None,
+        outs=[HBM, WHOLE],
+        scratch=[pltpu.VMEM((devices * (state_rows + 1), LANES), F32), pltpu.SemaphoreType.DMA],
     )
     states_sent = states_sent.reshape(devices, state_rows + 1, 1, LANES)
-    (sums,) = call(functools.partial(sums_kernel, local=local), [(devices, 1, LANES)], (obs, rows))
     (states_sent,) = call(
-        place_kernel,
+        functools.partial(sums_kernel, local=local),
         [states_sent.shape],
-        (sums, states_sent),
-        ins=[WHOLE, HBM],
+        (obs, rows, states_sent),
+        ins=[WHOLE, WHOLE, HBM],
         outs=[HBM],
-        scratch=[pltpu.SemaphoreType.DMA],
-        aliases={1: 0},
-        limit=None,
+        scratch=[pltpu.VMEM((devices, 1, LANES), F32), pltpu.SemaphoreType.DMA],
+        aliases={2: 0},
     )
     states = exchange(states_sent, "states_exchange")
-    powers, side = call(
+    powers, fourth, side, spread = call(
         functools.partial(gram_kernel, local=local),
-        [obs.shape, (2, 24, members)],
-        (obs, rows),
-        scratch=[pltpu.VMEM((2, members + 16, slots), BF16)] * 2,
+        [obs.shape, (2 * members * members // LANES, LANES), (2, 24, members), (patches, members)],
+        (obs, rows, counts),
+        outs=[WHOLE, WHOLE, WHOLE, HBM],
+        scratch=[
+            pltpu.VMEM((2, members + 16, slots), BF16),
+            pltpu.VMEM((2, members + 16, slots), BF16),
+            pltpu.VMEM((patches, members), F32),
+            pltpu.SemaphoreType.DMA,
+        ],
         aliases={0: 0},
     )
     (update,) = call(
         functools.partial(update_kernel, local=local),
         [(devices * state_rows, LANES)],
-        (states, powers, side),
+        (states, powers, fourth, side),
         scratch=[
             pltpu.VMEM((2, members, 3 * members), BF16),
-            pltpu.VMEM((2, 3 * members, 2 * members), BF16),
-            pltpu.VMEM((3 * members, cells), BF16),
+            pltpu.VMEM((2, 3 * members, members), BF16),
+            pltpu.VMEM((2, 3 * members, members), BF16),
+            pltpu.VMEM((2, 3 * members, cells), BF16),
+            pltpu.VMEM((2, 8, cells), F32),
         ],
     )
     returned = exchange(update, "return_exchange")
     (analysis,) = call(
-        functools.partial(unpack_kernel, half=half),
+        unpack_kernel,
         [(local, patches, cells)],
-        (counts, returned),
+        (spread, returned),
         outs=[HBM],
         scratch=[pltpu.VMEM((local, patches, cells), F32), pltpu.SemaphoreType.DMA((2 * local,))],
     )

time: 102 us -> 98.2 us (0.963)
  Pallas kernels: 24.8 us -> 21.1 us
  local copies, waits for them, and re-layouts: 1.39 us -> 2.46 us
    pallas_call x7 -> x6, Pallas kernels: 24.8 us -> 21.1 us  [call(): pl.pallas_call(kernel, out_shape=[pltpu.HBM(shape, F32) if s is HBM else...]
    unnamed x8 -> x10, local copies, waits for them, and re-layouts: 1.39 us -> 2.46 us
    all_to_all x2, waiting for transfers between devices: 36.2 us -> 35.2 us  [exchange(): lax.all_to_all(rows, AXES, split_axis=0, concat_axis=0, tiled=True)]
  transfers between devices with their start and end apart: 2 -> 2, of which waited for: 2 -> 2; matrix products, arithmetic and copies ran while one was open for 0% -> 0% of each run, Pallas kernels for 8% -> 7%
where the time goes in v3:
time: 98.2 us; the launch traced here: 97.9 us
  waiting for transfers between devices  35.2 us (36%)
  blocking collectives  23.1 us (24%)
  Pallas kernels  21.1 us (21%)
  starting transfers between devices  15.8 us (16%)
  local copies, waits for them, and re-layouts  2.46 us (3%)
    all_to_all x2, waiting for transfers between devices, exchange(): lax.all_to_all(rows, AXES, split_axis=0, concat_axis=0, tiled=True)  35.2 us
    all_to_all x1, blocking collectives, exchange(): lax.all_to_all(rows, AXES, split_axis=0, concat_axis=0, tiled=True)  23.1 us
    pallas_call x6, Pallas kernels, call(): pl.pallas_call(kernel, out_shape=[pltpu.HBM(shape, F32) if s is HBM else...  21.1 us
    all_to_all x2, starting transfers between devices, exchange(): lax.all_to_all(rows, AXES, split_axis=0, concat_axis=0, tiled=True)  15.8 us
    unnamed x10, local copies, waits for them, and re-layouts  2.46 us
  transfers between devices with their start and end apart: 2, of which 2 were waited for; matrix products, arithmetic and copies ran while one was open for 0% of the time, Pallas kernels for 7%

profile of v3, /device:TPU:0, one launch (start us, length us, event | category | flops | bytes accessed | tf_op | source)
XLA Modules:
  0.0 97.9 jit_solution(3012904614066839118)
XLA Ops:
  0.0 3.5 %shard_map.55 = f32[128,24,128]{2,1,0:T(8,128)} custom-call(s32[1,256]{1,0:T(1,128)} %bitcast.25, f32[4096,128]{1,0:T(8,128)} %bitcast.31), custom_call_target="tpu_custom_call" | custom-call | tf_op jit(solution)/shard_map/pallas_call | solution.py:374
  3.5 0.0 copy-start
  3.5 0.0 copy-start.4
  3.5 11.2 %all-to-all-start = ((f32[3072,1,128]{2,1,0:T(1,128)}), f32[3072,1,128]{2,1,0:T(1,128)S(1)}, u32[]{:S(2)}, u32[]{:S(2)}) async-start(f32[3072,1,128]{2,1,0:T(1,128)} %bitcast.28), calls=%async_computation | async-start | bytes 3145728 | tf_op jit(solution)/shard_map/obs_exchange/all_to_all | solution.py:391
  14.7 0.0 copy-done
  14.7 0.0 copy-done.4
  14.7 0.0 copy-start.1
  14.7 1.2 %copy-done.1 = f32[256,1024]{1,0:T(8,128)S(1)} copy-done((f32[256,1024]{1,0:T(8,128)S(1)}, f32[256,1024]{1,0:T(8,128)}, u32[]{:S(2)}) %copy-start.1) | copy-done | bytes 1048600
  16.0 0.0 copy-start.2
  16.0 1.2 %copy-done.2 = f32[256,1024]{1,0:T(8,128)S(1)} copy-done((f32[256,1024]{1,0:T(8,128)S(1)}, f32[256,1024]{1,0:T(8,128)}, u32[]{:S(2)}) %copy-start.2) | copy-done | bytes 1048600
  17.2 1.8 %shard_map.56 = (f32[2176,128]{1,0:T(8,128)}, f32[8,1024]{1,0:T(8,128)S(1)}) custom-call(s32[1]{0:T(128)} %bitcast.7.mine_ref, s32[1,256]{1,0:T(1,128)S(1)} %bitcast.26, f32[2,256,512]{2,1,0:T(8,128)S(1)} %copy-done, f32[256,1024]{1,0:T(8,128)S(1)} %copy-done.1, f32[256,1024]{1,0:T(8,128)S(1)} %copy-done.2), custom_call_target="tpu_custom_call" | custom-call | tf_op jit(solution)/shard_map/pallas_call | solution.py:374
  19.0 20.2 %all-to-all-done = f32[3072,1,128]{2,1,0:T(1,128)S(1)} async-done(((f32[3072,1,128]{2,1,0:T(1,128)}), f32[3072,1,128]{2,1,0:T(1,128)S(1)}, u32[]{:S(2)}, u32[]{:S(2)}) %all-to-all-start) | async-done | bytes 1572896 | tf_op jit(solution)/shard_map/obs_exchange/all_to_all | solution.py:391
  39.2 1.2 %shard_map.58 = f32[128,17,1,128]{3,2,1,0:T(1,128)} custom-call(f32[3072,128]{1,0:T(8,128)S(1)} %bitcast.20, f32[8,1024]{1,0:T(8,128)S(1)} %get-tuple-element.11.rows_ref, f32[128,17,1,128]{3,2,1,0:T(1,128)} %bitcast.29), custom_call_target="tpu_custom_call", output_to_operand_aliasing={{}: (2, {})} | custom-call | tf_op jit(solution)/shard_map/pallas_call | solution.py:374
  40.4 4.6 %all-to-all-start.1 = ((f32[2176,1,128]{2,1,0:T(1,128)}), f32[2176,1,128]{2,1,0:T(1,128)S(1)}, u32[]{:S(2)}, u32[]{:S(2)}) async-start(f32[2176,1,128]{2,1,0:T(1,128)} %bitcast.30), calls=%async_computation.1 | async-start | bytes 2228224 | tf_op jit(solution)/shard_map/states_exchange/all_to_all | solution.py:391
  45.0 4.7 %shard_map.57 = (f32[3072,128]{1,0:T(8,128)S(1)}, f32[1024,128]{1,0:T(8,128)S(1)}, f32[2,24,256]{2,1,0:T(8,128)S(1)}, f32[256,256]{1,0:T(8,128)}) custom-call(f32[3072,128]{1,0:T(8,128)S(1)} %bitcast.21, f32[8,1024]{1,0:T(8,128)S(1)} %get-tuple-element.11.rows_ref, s32[1,256]{1,0:T(1,128)S(1)} %bitcast.27), custom_call_target="tpu_custom_call", output_to_operand_aliasing={{0}: (0, {})} | custom-call | tf_op jit(solution)/shard_map/pallas_call | solution.py:374
  49.7 15.0 %all-to-all-done.1 = f32[2176,1,128]{2,1,0:T(1,128)S(1)} async-done(((f32[2176,1,128]{2,1,0:T(1,128)}), f32[2176,1,128]{2,1,0:T(1,128)S(1)}, u32[]{:S(2)}, u32[]{:S(2)}) %all-to-all-start.1) | async-done | bytes 1114144 | tf_op jit(solution)/shard_map/states_exchange/all_to_all | solution.py:391
  64.7 8.3 %shard_map.59 = f32[2048,128]{1,0:T(8,128)S(1)} custom-call(f32[2176,128]{1,0:T(8,128)S(1)} %bitcast.22, f32[3072,128]{1,0:T(8,128)S(1)} %get-tuple-element.14.powers_ref, f32[1024,128]{1,0:T(8,128)S(1)} %get-tuple-element.15.fourth_ref, f32[2,24,256]{2,1,0:T(8,128)S(1)} %get-tuple-element.16.side_ref), custom_call_target="tpu_custom_call" | custom-call | tf_op jit(solution)/shard_map/pallas_call | solution.py:374
  73.1 0.0 copy-start.3
  73.1 23.1 %all_to_all.15 = f32[2048,1,128]{2,1,0:T(1,128)S(1)} all-to-all(f32[2048,1,128]{2,1,0:T(1,128)S(1)} %bitcast.24), channel_id=1, replica_groups=mesh['grp'=8,'mem'=16] {'grp','mem'}, dimensions={0} | all-to-all | bytes 2097152 | tf_op jit(solution)/shard_map/return_exchange/all_to_all | solution.py:391
  96.2 0.0 copy-done.3
  96.2 1.6 %shard_map.60 = f32[2,256,512]{2,1,0:T(8,128)} custom-call(f32[256,256]{1,0:T(8,128)S(1)} %copy-done.3, f32[2048,128]{1,0:T(8,128)S(1)} %bitcast.23), custom_call_target="tpu_custom_call" | custom-call | tf_op jit(solution)/shard_map/pallas_call | solution.py:374
Async XLA Ops:
  3.5 11.2 %copy-start = (f32[2,256,512]{2,1,0:T(8,128)S(1)}, f32[2,256,512]{2,1,0:T(8,128)}, u32[]{:S(2)}) copy-start(f32[2,256,512]{2,1,0:T(8,128)} %states_ref.1) | copy-start | bytes 3145732
  3.5 11.2 %copy-start.4 = (s32[256]{0:T(256)S(1)}, s32[256]{0:T(256)}, u32[]{:S(2)}) copy-start(s32[256]{0:T(256)} %param.9) | copy-start | bytes 3076
  3.5 35.6 %all-to-all-start = ((f32[3072,1,128]{2,1,0:T(1,128)}), f32[3072,1,128]{2,1,0:T(1,128)S(1)}, u32[]{:S(2)}, u32[]{:S(2)}) async-start(f32[3072,1,128]{2,1,0:T(1,128)} %bitcast.28), calls=%async_computation | async-start | bytes 3145728 | tf_op jit(solution)/shard_map/obs_exchange/all_to_all | solution.py:391
  14.7 1.2 %copy-start.1 = (f32[256,1024]{1,0:T(8,128)S(1)}, f32[256,1024]{1,0:T(8,128)}, u32[]{:S(2)}) copy-start(f32[256,1024]{1,0:T(8,128)} %value_ref.1) | copy-start | bytes 3145732
  16.0 1.2 %copy-start.2 = (f32[256,1024]{1,0:T(8,128)S(1)}, f32[256,1024]{1,0:T(8,128)}, u32[]{:S(2)}) copy-start(f32[256,1024]{1,0:T(8,128)} %precision_ref.1) | copy-start | bytes 3145732
  40.4 24.4 %all-to-all-start.1 = ((f32[2176,1,128]{2,1,0:T(1,128)}), f32[2176,1,128]{2,1,0:T(1,128)S(1)}, u32[]{:S(2)}, u32[]{:S(2)}) async-start(f32[2176,1,128]{2,1,0:T(1,128)} %bitcast.30), calls=%async_computation.1 | async-start | bytes 2228224 | tf_op jit(solution)/shard_map/states_exchange/all_to_all | solution.py:391
  73.1 23.2 %copy-start.3 = (f32[256,256]{1,0:T(8,128)S(1)}, f32[256,256]{1,0:T(8,128)}, u32[]{:S(2)}) copy-start(f32[256,256]{1,0:T(8,128)} %get-tuple-element.12.spread_ref) | copy-start | bytes 786436

commit v4 on v3

--- a/solution.py
+++ b/solution.py
@@ -13,6 +13,8 @@
 F32 = jnp.float32
 BF16 = jnp.bfloat16
 VMEM_LIMIT = 12 << 20
+IN_PIECES = 2
+OUT_PIECES = 4
 
 
 def dot(a, b):
@@ -49,13 +51,19 @@
     return jnp.concatenate([high, low, high], axis=0)
 
 
-def owners(counts, half, devices):
+def ranks(counts, half):
     patches = counts.shape[1]
     heavy = (counts > half).astype(F32)
     before = lax.broadcasted_iota(jnp.int32, (patches, patches), 0) < lax.broadcasted_iota(
         jnp.int32, (patches, patches), 1
     )
     rank = dot(jnp.broadcast_to(heavy, (8, patches)).astype(BF16), before.astype(F32).astype(BF16))[:1]
+    return heavy, rank
+
+
+def owners(counts, half, devices):
+    patches = counts.shape[1]
+    heavy, rank = ranks(counts, half)
     position = lax.broadcasted_iota(jnp.int32, (1, patches), 1).astype(F32)
     device = lax.broadcasted_iota(jnp.int32, (devices, patches), 0).astype(F32)
     heavies = jnp.where((device == rank) & (heavy > 0.0), 1.0, 0.0)
@@ -66,10 +74,6 @@
 def store_rows(ref, first, stride, x):
     for j in range(x.shape[1] // LANES):
         ref[pl.ds(first + j, x.shape[0], stride=stride), :] = x[:, j * LANES : (j + 1) * LANES]
-
-
-def gather_rows(ref, first, stride, rows, blocks):
-    return jnp.concatenate([ref[pl.ds(first + j, rows, stride=stride), :] for j in range(blocks)], axis=1)
 
 
 def load_rows(ref, first, rows, blocks):
@@ -90,9 +94,10 @@
     count_copy = pltpu.make_async_copy(counts_hbm, counts_ref, sems.at[0])
     count_copy.start()
     copies = []
-    for m in range(local):
-        span = pl.ds(m * each, each)
-        copies.append(pltpu.make_async_copy(obs_hbm.at[span], obs_ref.at[span], sems.at[1 + m]))
+    cut = each // IN_PIECES
+    for i in range(local * IN_PIECES):
+        span = pl.ds(i * cut, cut)
+        copies.append(pltpu.make_async_copy(obs_hbm.at[span], obs_ref.at[span], sems.at[1 + i]))
         copies[-1].start()
     count_copy.wait()
     onehots = owners(counts_ref[...], slots // 2, devices)
@@ -101,28 +106,26 @@
     start = [(p >> 3) * (8 * blocks) + (p & 7) for p in index]
     row = lax.broadcasted_iota(jnp.int32, (8, devices), 0)
     table_ref[...] = jnp.where(row == 0, start[0], start[1])
-    table_copy = pltpu.make_async_copy(table_ref, table, sems.at[1 + local])
+    table_copy = pltpu.make_async_copy(table_ref, table, sems.at[0])
     table_copy.start()
     table_copy.wait()
     sent = []
-    for m in range(local):
-        copies[m].wait()
-
-        @pl.loop(0, devices, unroll=8)
+    for copy in copies:
+        copy.wait()
+    group = devices // OUT_PIECES
+    for g in range(OUT_PIECES):
+
+        @pl.loop(g * group, (g + 1) * group, unroll=32)
         def _(d):
-            heavy = m * each + table[0, d]
-            light = m * each + table[1, d]
-            out_ref[d, m * blocks : (m + 1) * blocks, :] = obs_ref[pl.ds(heavy, blocks, stride=8), :]
-            first = local * blocks + m * blocks // 2
-            out_ref[d, first : first + blocks // 2, :] = obs_ref[pl.ds(light, blocks // 2, stride=8), :]
-
-        first = m * blocks
-        last = first + blocks if m < local - 1 else per
-        sent.append(
-            pltpu.make_async_copy(
-                out_ref.at[:, first:last], out_hbm.at[:, first:last], sems.at[2 + local + m]
-            )
-        )
+            heavy = table[0, d]
+            light = table[1, d]
+            for m in range(local):
+                out_ref[d, m * blocks : (m + 1) * blocks, :] = obs_ref[pl.ds(m * each + heavy, blocks, stride=8), :]
+                at = local * blocks + m * blocks // 2
+                out_ref[d, at : at + blocks // 2, :] = obs_ref[pl.ds(m * each + light, blocks // 2, stride=8), :]
+
+        some = pl.ds(g * group, group)
+        sent.append(pltpu.make_async_copy(out_ref.at[some], out_hbm.at[some], sems.at[1 + local * IN_PIECES + g]))
         sent[-1].start()
     for copy in sent:
         copy.wait()
@@ -199,14 +202,15 @@
 
 
 def gram_kernel(
-    obs_ref, rows_ref, counts_ref, powers_ref, fourth_ref, side_ref, spread_hbm, high_ref, low_ref, spread_ref, sem, *, local
+    obs_ref, rows_ref, counts_ref, powers_ref, fourth_ref, side_ref, table_ref, high_ref, low_ref, *, local, tile
 ):
     slots = rows_ref.shape[1]
     members = side_ref.shape[2]
     devices = members // local
-    spread_ref[...] = jnp.concatenate(owners(counts_ref[...], slots // 2, devices), axis=0).T
-    copy = pltpu.make_async_copy(spread_ref, spread_hbm, sem)
-    copy.start()
+    heavy, rank = ranks(counts_ref[...], slots // 2)
+    position = lax.broadcasted_iota(jnp.int32, rank.shape, 1).astype(F32)
+    place = jnp.where(heavy > 0.0, 2.0 * rank, 2.0 * (position - rank) + 1.0)
+    table_ref[...] = place.astype(jnp.int32) * tile
     for k, columns, parts, innov, precision, live in obs_columns(obs_ref, rows_ref, local):
         scale = jnp.sqrt(precision * live)
         for m in range(local):
@@ -242,11 +246,10 @@
         side_ref[k] = jnp.concatenate(
             [forcing, jnp.broadcast_to(size, (8, members)), jnp.broadcast_to(trace, (8, members))], axis=0
         )
-    copy.wait()
 
 
 def update_kernel(
-    states_ref, powers_ref, fourth_ref, side_ref, out_ref, s_left, s_right, z_right, states_right, center_ref, *, local
+    states_ref, powers_ref, fourth_ref, side_ref, out_ref, s_ref, z_ref, states_right, center_ref, *, local
 ):
     members = side_ref.shape[2]
     devices = members // local
@@ -266,22 +269,27 @@
     def plus_diagonal(x, value):
         return x + jnp.where(diagonal, value, 0.0)
 
-    def put(k, s):
-        s_left[k] = left_form(s)
-        s_right[k] = right_form(s)
+    def put(ref, k, x):
+        ref[k, 0], ref[k, 1] = halves(x)
+
+    def left(ref, k):
+        return jnp.concatenate([ref[k, 0], ref[k, 0], ref[k, 1]], axis=1)
+
+    def right(ref, k):
+        return jnp.concatenate([ref[k, 0], ref[k, 1], ref[k, 0]], axis=0)
+
+    def whole(ref, k):
+        return ref[k, 0].astype(F32) + ref[k, 1].astype(F32)
 
     def square(k):
-        high = s_left[k, :, :members]
-        cross = dot(high, s_right[k, members : 2 * members])
-        return dot(high, s_right[k, :members]) + (cross + cross.T)
+        return dot(left(s_ref, k), right(s_ref, k))
 
     def refine(k, product):
-        s = s_left[k, :, :members].astype(F32) + s_left[k, :, 2 * members :].astype(F32)
-        return dot(left_form(plus_diagonal(0.25 * product - 1.5 * s, 2.25)), s_right[k])
+        s = whole(s_ref, k)
+        return 2.25 * s + dot(left_form(0.25 * product - 1.5 * s), right(s_ref, k))
 
     def advance(k):
-        z = z_right[k, :members].astype(F32) + z_right[k, members : 2 * members].astype(F32)
-        return 1.5 * z - 0.5 * dot(s_left[k], z_right[k])
+        return 1.5 * whole(z_ref, k) - 0.5 * dot(left(s_ref, k), right(z_ref, k))
 
     scalers = []
     for k in range(2):
@@ -298,10 +306,10 @@
         halfs = members // LANES
         powers = [load_rows(powers_ref, (k * 3 + i) * halfs * members, members, halfs) for i in range(3)]
         powers.append(load_rows(fourth_ref, k * halfs * members, members, halfs))
-        put(k, plus_diagonal(sum(c * p for c, p in zip(s1[1:], powers)), s1[0]))
-        z_right[k] = right_form(plus_diagonal(sum(c * p for c, p in zip(z2[1:], powers)), z2[0]))
-    for k in range(2):
-        put(k, refine(k, square(k)))
+        put(s_ref, k, plus_diagonal(sum(c * p for c, p in zip(s1[1:], powers)), s1[0]))
+        put(z_ref, k, plus_diagonal(sum(c * p for c, p in zip(z2[1:], powers)), z2[0]))
+    for k in range(2):
+        put(s_ref, k, refine(k, square(k)))
         for c in range(blocks):
             rows = [(k * local + m) * blocks + c for m in range(local)]
             parts = [states_ref[pl.ds(r, devices, stride=per), :] for r in rows]
@@ -314,21 +322,20 @@
                     first = i * members + m * devices
                     states_right[k, first : first + devices, columns] = piece
 
-    def sweep(_, carry):
+    for _ in range(SWEEPS - 3):
+        products = [square(k) for k in range(2)]
+        roots = [advance(k) for k in range(2)]
         for k in range(2):
-            s = refine(k, square(k))
-            z = advance(k)
-            put(k, s)
-            z_right[k] = right_form(z)
-        return carry
-
-    lax.fori_loop(0, SWEEPS - 3, sweep, 0)
-    for k in range(2):
-        root = advance(k) / jnp.sqrt(scalers[k])
-        forcing = inflation * side_ref[k, :1]
+            s = refine(k, products[k])
+            put(s_ref, k, s)
+            put(z_ref, k, roots[k])
+
+    for k in range(2):
+        root = advance(k)
+        forcing = squared / scalers[k] * side_ref[k, :1]
         half_way = jnp.sum(root * forcing, axis=1, keepdims=True)
         shifts = jnp.sum(root * half_way, axis=0, keepdims=True)
-        transform = inflation * (free**0.5 * root + shifts)
+        transform = (inflation * free**0.5 / jnp.sqrt(scalers[k])) * root + shifts
         update = dot(left_form(transform), states_right[k]) + center_ref[k, :1]
         for c in range(blocks):
             for m in range(local):
@@ -336,26 +343,26 @@
                 out_ref[pl.ds((k * local + m) * blocks + c, devices, stride=2 * local * blocks), :] = piece
 
 
-def unpack_kernel(spread_ref, rows_ref, out_hbm, out_ref, sems):
-    local, patches, cells = out_ref.shape
-    blocks = cells // LANES
-    per = 2 * local * blocks
-    devices = rows_ref.shape[0] // per
-    onehot = spread_ref[...]
+def unpack_kernel(table, rows_ref, out_hbm, out_ref, sems, *, local):
+    patches = table.shape[1]
+    tile = rows_ref.shape[0] // patches
+    blocks = tile // local
+    each = patches * blocks
+    group = patches // OUT_PIECES
     copies = []
-    for m in range(local):
-        for part in range(2):
-            wide = blocks // 2
-            x = jnp.concatenate(
-                [gather_rows(rows_ref, (k * local + m) * blocks + part * wide, per, devices, wide) for k in range(2)],
-                axis=0,
-            )
-            columns = pl.ds(part * wide * LANES, wide * LANES)
-            out_ref[m, :, columns] = pick(onehot, x)
+    for g in range(OUT_PIECES):
+
+        @pl.loop(g * group, (g + 1) * group, unroll=32)
+        def _(p):
+            x = rows_ref[pl.ds(pl.multiple_of(table[0, p], tile), tile), :]
+            first = (p >> 3) * (8 * blocks) + (p & 7)
+            for m in range(local):
+                out_ref[pl.ds(m * each + first, blocks, stride=8), :] = x[m * blocks : (m + 1) * blocks]
+
+        for m in range(local):
+            some = pl.ds(m * each + g * group * blocks, group * blocks)
             copies.append(
-                pltpu.make_async_copy(
-                    out_ref.at[m, :, columns], out_hbm.at[m, :, columns], sems.at[2 * m + part]
-                )
+                pltpu.make_async_copy(out_ref.at[some], out_hbm.at[some], sems.at[m * OUT_PIECES + g])
             )
             copies[-1].start()
     for copy in copies:
@@ -367,21 +374,21 @@
 SCALAR = pl.BlockSpec(memory_space=pltpu.SMEM)
 
 
-def call(kernel, out_shapes, inputs, ins=None, outs=None, scratch=(), aliases={}, limit=VMEM_LIMIT):
+def call(kernel, out_shapes, inputs, ins=None, outs=None, types=None, scratch=(), aliases={}):
     ins = ins or [WHOLE] * len(inputs)
     outs = outs or [WHOLE] * len(out_shapes)
     inputs = [pltpu.with_memory_space_constraint(x, pltpu.HBM) if s is HBM else x for x, s in zip(inputs, ins)]
     return pl.pallas_call(
         kernel,
         out_shape=[
-            pltpu.HBM(shape, F32) if s is HBM else jax.ShapeDtypeStruct(shape, F32)
-            for shape, s in zip(out_shapes, outs)
+            pltpu.HBM(shape, kind) if s is HBM else jax.ShapeDtypeStruct(shape, kind)
+            for shape, kind, s in zip(out_shapes, types or [F32] * len(outs), outs)
         ],
         in_specs=ins,
         out_specs=outs,
         scratch_shapes=list(scratch),
         input_output_aliases=aliases,
-        compiler_params=pltpu.CompilerParams(vmem_limit_bytes=limit),
+        compiler_params=pltpu.CompilerParams(vmem_limit_bytes=VMEM_LIMIT),
     )(*inputs)
 
 
@@ -414,7 +421,7 @@
             pltpu.VMEM((devices, obs_rows, LANES), F32),
             pltpu.VMEM((8, devices), jnp.int32),
             pltpu.SMEM((8, devices), jnp.int32),
-            pltpu.SemaphoreType.DMA((2 * local + 2,)),
+            pltpu.SemaphoreType.DMA((1 + local * IN_PIECES + OUT_PIECES,)),
         ],
     )
     obs = exchange(obs_sent, "obs_exchange")
@@ -437,17 +444,12 @@
         aliases={2: 0},
     )
     states = exchange(states_sent, "states_exchange")
-    powers, fourth, side, spread = call(
-        functools.partial(gram_kernel, local=local),
-        [obs.shape, (2 * members * members // LANES, LANES), (2, 24, members), (patches, members)],
+    powers, fourth, side, table = call(
+        functools.partial(gram_kernel, local=local, tile=state_rows // 2),
+        [obs.shape, (2 * members * members // LANES, LANES), (2, 24, members), (1, patches)],
         (obs, rows, counts),
-        outs=[WHOLE, WHOLE, WHOLE, HBM],
-        scratch=[
-            pltpu.VMEM((2, members + 16, slots), BF16),
-            pltpu.VMEM((2, members + 16, slots), BF16),
-            pltpu.VMEM((patches, members), F32),
-            pltpu.SemaphoreType.DMA,
-        ],
+        types=[F32, F32, F32, jnp.int32],
+        scratch=[pltpu.VMEM((2, members + 16, slots), BF16)] * 2,
         aliases={0: 0},
     )
     (update,) = call(
@@ -455,22 +457,23 @@
         [(devices * state_rows, LANES)],
         (states, powers, fourth, side),
         scratch=[
-            pltpu.VMEM((2, members, 3 * members), BF16),
-            pltpu.VMEM((2, 3 * members, members), BF16),
-            pltpu.VMEM((2, 3 * members, members), BF16),
+            pltpu.VMEM((2, 2, members, members), BF16),
+            pltpu.VMEM((2, 2, members, members), BF16),
             pltpu.VMEM((2, 3 * members, cells), BF16),
             pltpu.VMEM((2, 8, cells), F32),
         ],
     )
     returned = exchange(update, "return_exchange")
     (analysis,) = call(
-        unpack_kernel,
-        [(local, patches, cells)],
-        (spread, returned),
+        functools.partial(unpack_kernel, local=local),
+        [(devices * state_rows, LANES)],
+        (table, returned),
+        ins=[SCALAR, WHOLE],
         outs=[HBM],
-        scratch=[pltpu.VMEM((local, patches, cells), F32), pltpu.SemaphoreType.DMA((2 * local,))],
-    )
-    return analysis
+        scratch=[pltpu.VMEM((devices * state_rows, LANES), F32), pltpu.SemaphoreType.DMA((local * OUT_PIECES,))],
+    )
+    in_memory = analysis.reshape(local, patches // 8, cells // LANES, 8, LANES)
+    return in_memory.swapaxes(2, 3).reshape(local, patches, cells)
 
 
 def solution(mesh):

time: 98.2 us -> 95.9 us (0.977)
  Pallas kernels: 21.1 us -> 18.2 us
    pallas_call x6, Pallas kernels: 21.1 us -> 18.2 us  [call(): pl.pallas_call(kernel, out_shape=[pltpu.HBM(shape, kind) if s is HBM else...]
    unnamed x10 -> x8, local copies, waits for them, and re-layouts: 2.46 us -> 2.46 us
  transfers between devices with their start and end apart: 2 -> 2, of which waited for: 2 -> 2; matrix products, arithmetic and copies ran while one was open for 0% -> 0% of each run, Pallas kernels for 7% -> 6%
where the time goes in v4:
time: 95.9 us; the launch traced here: 95.6 us
  waiting for transfers between devices  35.7 us (37%)
  blocking collectives  23 us (24%)
  Pallas kernels  18.2 us (19%)
  starting transfers between devices  16 us (17%)
  local copies, waits for them, and re-layouts  2.46 us (3%)
    all_to_all x2, waiting for transfers between devices, exchange(): lax.all_to_all(rows, AXES, split_axis=0, concat_axis=0, tiled=True)  35.7 us
    all_to_all x1, blocking collectives, exchange(): lax.all_to_all(rows, AXES, split_axis=0, concat_axis=0, tiled=True)  23 us
    pallas_call x6, Pallas kernels, call(): pl.pallas_call(kernel, out_shape=[pltpu.HBM(shape, kind) if s is HBM else...  18.2 us
    all_to_all x2, starting transfers between devices, exchange(): lax.all_to_all(rows, AXES, split_axis=0, concat_axis=0, tiled=True)  16 us
    unnamed x8, local copies, waits for them, and re-layouts  2.46 us
  transfers between devices with their start and end apart: 2, of which 2 were waited for; matrix products, arithmetic and copies ran while one was open for 0% of the time, Pallas kernels for 6%

profile of v4, /device:TPU:0, one launch (start us, length us, event | category | flops | bytes accessed | tf_op | source)
XLA Modules:
  0.0 95.6 jit_solution(18184602725833049265)
XLA Ops:
  0.0 2.9 %shard_map.55 = f32[128,24,128]{2,1,0:T(8,128)} custom-call(s32[1,256]{1,0:T(1,128)} %bitcast.30, f32[4096,128]{1,0:T(8,128)} %bitcast.36), custom_call_target="tpu_custom_call" | custom-call | tf_op jit(solution)/shard_map/pallas_call | solution.py:381
  2.9 0.0 copy-start
  2.9 0.0 copy-start.3
  2.9 11.2 %all-to-all-start = ((f32[3072,1,128]{2,1,0:T(1,128)}), f32[3072,1,128]{2,1,0:T(1,128)S(1)}, u32[]{:S(2)}, u32[]{:S(2)}) async-start(f32[3072,1,128]{2,1,0:T(1,128)} %bitcast.33), calls=%async_computation | async-start | bytes 3145728 | tf_op jit(solution)/shard_map/obs_exchange/all_to_all | solution.py:398
  14.1 0.0 copy-done
  14.1 0.0 copy-done.3
  14.2 0.0 copy-start.1
  14.2 1.2 %copy-done.1 = f32[256,1024]{1,0:T(8,128)S(1)} copy-done((f32[256,1024]{1,0:T(8,128)S(1)}, f32[256,1024]{1,0:T(8,128)}, u32[]{:S(2)}) %copy-start.1) | copy-done | bytes 1048600
  15.4 0.0 copy-start.2
  15.4 1.2 %copy-done.2 = f32[256,1024]{1,0:T(8,128)S(1)} copy-done((f32[256,1024]{1,0:T(8,128)S(1)}, f32[256,1024]{1,0:T(8,128)}, u32[]{:S(2)}) %copy-start.2) | copy-done | bytes 1048600
  16.6 1.8 %shard_map.56 = (f32[2176,128]{1,0:T(8,128)}, f32[8,1024]{1,0:T(8,128)S(1)}) custom-call(s32[1]{0:T(128)} %bitcast.7.mine_ref, s32[1,256]{1,0:T(1,128)S(1)} %bitcast.31, f32[2,256,512]{2,1,0:T(8,128)S(1)} %copy-done, f32[256,1024]{1,0:T(8,128)S(1)} %copy-done.1, f32[256,1024]{1,0:T(8,128)S(1)} %copy-done.2), custom_call_target="tpu_custom_call" | custom-call | tf_op jit(solution)/shard_map/pallas_call | solution.py:381
  18.4 20.2 %all-to-all-done = f32[3072,1,128]{2,1,0:T(1,128)S(1)} async-done(((f32[3072,1,128]{2,1,0:T(1,128)}), f32[3072,1,128]{2,1,0:T(1,128)S(1)}, u32[]{:S(2)}, u32[]{:S(2)}) %all-to-all-start) | async-done | bytes 1572896 | tf_op jit(solution)/shard_map/obs_exchange/all_to_all | solution.py:398
  38.6 1.2 %shard_map.58 = f32[128,17,1,128]{3,2,1,0:T(1,128)} custom-call(f32[3072,128]{1,0:T(8,128)S(1)} %bitcast.25, f32[8,1024]{1,0:T(8,128)S(1)} %get-tuple-element.11.rows_ref, f32[128,17,1,128]{3,2,1,0:T(1,128)} %bitcast.34), custom_call_target="tpu_custom_call", output_to_operand_aliasing={{}: (2, {})} | custom-call | tf_op jit(solution)/shard_map/pallas_call | solution.py:381
  39.8 4.8 %all-to-all-start.1 = ((f32[2176,1,128]{2,1,0:T(1,128)}), f32[2176,1,128]{2,1,0:T(1,128)S(1)}, u32[]{:S(2)}, u32[]{:S(2)}) async-start(f32[2176,1,128]{2,1,0:T(1,128)} %bitcast.35), calls=%async_computation.1 | async-start | bytes 2228224 | tf_op jit(solution)/shard_map/states_exchange/all_to_all | solution.py:398
  44.6 4.0 %shard_map.57 = (f32[3072,128]{1,0:T(8,128)S(1)}, f32[1024,128]{1,0:T(8,128)S(1)}, f32[2,24,256]{2,1,0:T(8,128)S(1)}, s32[1,256]{1,0:T(1,128)S(1)}) custom-call(f32[3072,128]{1,0:T(8,128)S(1)} %bitcast.26, f32[8,1024]{1,0:T(8,128)S(1)} %get-tuple-element.11.rows_ref, s32[1,256]{1,0:T(1,128)S(1)} %bitcast.32), custom_call_target="tpu_custom_call", output_to_operand_aliasing={{0}: (0, {})} | custom-call | tf_op jit(solution)/shard_map/pallas_call | solution.py:381
  48.6 15.5 %all-to-all-done.1 = f32[2176,1,128]{2,1,0:T(1,128)S(1)} async-done(((f32[2176,1,128]{2,1,0:T(1,128)}), f32[2176,1,128]{2,1,0:T(1,128)S(1)}, u32[]{:S(2)}, u32[]{:S(2)}) %all-to-all-start.1) | async-done | bytes 1114144 | tf_op jit(solution)/shard_map/states_exchange/all_to_all | solution.py:398
  64.2 6.3 %shard_map.59 = f32[2048,128]{1,0:T(8,128)S(1)} custom-call(f32[2176,128]{1,0:T(8,128)S(1)} %bitcast.27, f32[3072,128]{1,0:T(8,128)S(1)} %get-tuple-element.14.powers_ref, f32[1024,128]{1,0:T(8,128)S(1)} %get-tuple-element.15.fourth_ref, f32[2,24,256]{2,1,0:T(8,128)S(1)} %get-tuple-element.16.side_ref), custom_call_target="tpu_custom_call" | custom-call | tf_op jit(solution)/shard_map/pallas_call | solution.py:381
  70.5 23.0 %all_to_all.15 = f32[2048,1,128]{2,1,0:T(1,128)S(1)} all-to-all(f32[2048,1,128]{2,1,0:T(1,128)S(1)} %bitcast.29), channel_id=1, replica_groups=mesh['grp'=8,'mem'=16] {'grp','mem'}, dimensions={0} | all-to-all | bytes 2097152 | tf_op jit(solution)/shard_map/return_exchange/all_to_all | solution.py:398
  93.5 1.9 %shard_map.60 = f32[2048,128]{1,0:T(8,128)} custom-call(s32[1,256]{1,0:T(1,128)S(1)} %get-tuple-element.12.table, f32[2048,128]{1,0:T(8,128)S(1)} %bitcast.28), custom_call_target="tpu_custom_call" | custom-call | tf_op jit(solution)/shard_map/pallas_call | solution.py:381
Async XLA Ops:
  2.9 11.2 %copy-start = (f32[2,256,512]{2,1,0:T(8,128)S(1)}, f32[2,256,512]{2,1,0:T(8,128)}, u32[]{:S(2)}) copy-start(f32[2,256,512]{2,1,0:T(8,128)} %states_ref.1) | copy-start | bytes 3145732
  2.9 11.2 %copy-start.3 = (s32[256]{0:T(256)S(1)}, s32[256]{0:T(256)}, u32[]{:S(2)}) copy-start(s32[256]{0:T(256)} %param.9) | copy-start | bytes 3076
  2.9 35.6 %all-to-all-start = ((f32[3072,1,128]{2,1,0:T(1,128)}), f32[3072,1,128]{2,1,0:T(1,128)S(1)}, u32[]{:S(2)}, u32[]{:S(2)}) async-start(f32[3072,1,128]{2,1,0:T(1,128)} %bitcast.33), calls=%async_computation | async-start | bytes 3145728 | tf_op jit(solution)/shard_map/obs_exchange/all_to_all | solution.py:398
  14.2 1.2 %copy-start.1 = (f32[256,1024]{1,0:T(8,128)S(1)}, f32[256,1024]{1,0:T(8,128)}, u32[]{:S(2)}) copy-start(f32[256,1024]{1,0:T(8,128)} %value_ref.1) | copy-start | bytes 3145732
  15.4 1.2 %copy-start.2 = (f32[256,1024]{1,0:T(8,128)S(1)}, f32[256,1024]{1,0:T(8,128)}, u32[]{:S(2)}) copy-start(f32[256,1024]{1,0:T(8,128)} %precision_ref.1) | copy-start | bytes 3145732
  39.8 24.4 %all-to-all-start.1 = ((f32[2176,1,128]{2,1,0:T(1,128)}), f32[2176,1,128]{2,1,0:T(1,128)S(1)}, u32[]{:S(2)}, u32[]{:S(2)}) async-start(f32[2176,1,128]{2,1,0:T(1,128)} %bitcast.35), calls=%async_computation.1 | async-start | bytes 2228224 | tf_op jit(solution)/shard_map/states_exchange/all_to_all | solution.py:398

commit v5 on v4

--- a/solution.py
+++ b/solution.py
@@ -51,19 +51,13 @@
     return jnp.concatenate([high, low, high], axis=0)
 
 
-def ranks(counts, half):
+def owners(counts, half, devices):
     patches = counts.shape[1]
     heavy = (counts > half).astype(F32)
     before = lax.broadcasted_iota(jnp.int32, (patches, patches), 0) < lax.broadcasted_iota(
         jnp.int32, (patches, patches), 1
     )
     rank = dot(jnp.broadcast_to(heavy, (8, patches)).astype(BF16), before.astype(F32).astype(BF16))[:1]
-    return heavy, rank
-
-
-def owners(counts, half, devices):
-    patches = counts.shape[1]
-    heavy, rank = ranks(counts, half)
     position = lax.broadcasted_iota(jnp.int32, (1, patches), 1).astype(F32)
     device = lax.broadcasted_iota(jnp.int32, (devices, patches), 0).astype(F32)
     heavies = jnp.where((device == rank) & (heavy > 0.0), 1.0, 0.0)
@@ -202,15 +196,12 @@
 
 
 def gram_kernel(
-    obs_ref, rows_ref, counts_ref, powers_ref, fourth_ref, side_ref, table_ref, high_ref, low_ref, *, local, tile
+    obs_ref, rows_ref, counts_ref, powers_ref, fourth_ref, side_ref, spread_ref, high_ref, low_ref, *, local
 ):
     slots = rows_ref.shape[1]
     members = side_ref.shape[2]
     devices = members // local
-    heavy, rank = ranks(counts_ref[...], slots // 2)
-    position = lax.broadcasted_iota(jnp.int32, rank.shape, 1).astype(F32)
-    place = jnp.where(heavy > 0.0, 2.0 * rank, 2.0 * (position - rank) + 1.0)
-    table_ref[...] = place.astype(jnp.int32) * tile
+    spread_ref[...] = jnp.concatenate(owners(counts_ref[...], slots // 2, devices), axis=0).T.astype(BF16)
     for k, columns, parts, innov, precision, live in obs_columns(obs_ref, rows_ref, local):
         scale = jnp.sqrt(precision * live)
         for m in range(local):
@@ -343,26 +334,35 @@
                 out_ref[pl.ds((k * local + m) * blocks + c, devices, stride=2 * local * blocks), :] = piece
 
 
-def unpack_kernel(table, rows_ref, out_hbm, out_ref, sems, *, local):
-    patches = table.shape[1]
-    tile = rows_ref.shape[0] // patches
-    blocks = tile // local
-    each = patches * blocks
-    group = patches // OUT_PIECES
+def unpack_kernel(spread_ref, rows_ref, out_hbm, out_ref, sems):
+    local, patches, cells = out_ref.shape
+    blocks = cells // LANES
+    per = 2 * local * blocks
+    devices = rows_ref.shape[0] // per
+    spread = jnp.concatenate([spread_ref[...]] * 2, axis=1)
+    wide = blocks // 2
     copies = []
-    for g in range(OUT_PIECES):
-
-        @pl.loop(g * group, (g + 1) * group, unroll=32)
-        def _(p):
-            x = rows_ref[pl.ds(pl.multiple_of(table[0, p], tile), tile), :]
-            first = (p >> 3) * (8 * blocks) + (p & 7)
-            for m in range(local):
-                out_ref[pl.ds(m * each + first, blocks, stride=8), :] = x[m * blocks : (m + 1) * blocks]
-
-        for m in range(local):
-            some = pl.ds(m * each + g * group * blocks, group * blocks)
+    for m in range(local):
+        for part in range(2):
+            x = jnp.concatenate(
+                [
+                    jnp.concatenate(
+                        [
+                            rows_ref[pl.ds((k * local + m) * blocks + part * wide + j, devices, stride=per), :]
+                            for j in range(wide)
+                        ],
+                        axis=1,
+                    )
+                    for k in range(2)
+                ],
+                axis=0,
+            )
+            columns = pl.ds(part * wide * LANES, wide * LANES)
+            out_ref[m, :, columns] = dot(spread, jnp.concatenate(halves(x), axis=0))
             copies.append(
-                pltpu.make_async_copy(out_ref.at[some], out_hbm.at[some], sems.at[m * OUT_PIECES + g])
+                pltpu.make_async_copy(
+                    out_ref.at[m, :, columns], out_hbm.at[m, :, columns], sems.at[2 * m + part]
+                )
             )
             copies[-1].start()
     for copy in copies:
@@ -444,11 +444,11 @@
         aliases={2: 0},
     )
     states = exchange(states_sent, "states_exchange")
-    powers, fourth, side, table = call(
-        functools.partial(gram_kernel, local=local, tile=state_rows // 2),
-        [obs.shape, (2 * members * members // LANES, LANES), (2, 24, members), (1, patches)],
+    powers, fourth, side, spread = call(
+        functools.partial(gram_kernel, local=local),
+        [obs.shape, (2 * members * members // LANES, LANES), (2, 24, members), (patches, members)],
         (obs, rows, counts),
-        types=[F32, F32, F32, jnp.int32],
+        types=[F32, F32, F32, BF16],
         scratch=[pltpu.VMEM((2, members + 16, slots), BF16)] * 2,
         aliases={0: 0},
     )
@@ -465,15 +465,13 @@
     )
     returned = exchange(update, "return_exchange")
     (analysis,) = call(
-        functools.partial(unpack_kernel, local=local),
-        [(devices * state_rows, LANES)],
-        (table, returned),
-        ins=[SCALAR, WHOLE],
+        unpack_kernel,
+        [(local, patches, cells)],
+        (spread, returned),
         outs=[HBM],
-        scratch=[pltpu.VMEM((devices * state_rows, LANES), F32), pltpu.SemaphoreType.DMA((local * OUT_PIECES,))],
-    )
-    in_memory = analysis.reshape(local, patches // 8, cells // LANES, 8, LANES)
-    return in_memory.swapaxes(2, 3).reshape(local, patches, cells)
+        scratch=[pltpu.VMEM((local, patches, cells), F32), pltpu.SemaphoreType.DMA((2 * local,))],
+    )
+    return analysis
 
 
 def solution(mesh):

time: 95.9 us -> 95.5 us (level)
  no operation moved by 1% of the time
where the time goes in v5:
time: 95.5 us; the launch traced here: 95.1 us
  waiting for transfers between devices  35.7 us (37%)
  blocking collectives  23 us (24%)
  Pallas kernels  17.7 us (19%)
  starting transfers between devices  16 us (17%)
  local copies, waits for them, and re-layouts  2.46 us (3%)
    all_to_all x2, waiting for transfers between devices, exchange(): lax.all_to_all(rows, AXES, split_axis=0, concat_axis=0, tiled=True)  35.7 us
    all_to_all x1, blocking collectives, exchange(): lax.all_to_all(rows, AXES, split_axis=0, concat_axis=0, tiled=True)  23 us
    pallas_call x6, Pallas kernels, call(): pl.pallas_call(kernel, out_shape=[pltpu.HBM(shape, kind) if s is HBM else...  17.7 us
    all_to_all x2, starting transfers between devices, exchange(): lax.all_to_all(rows, AXES, split_axis=0, concat_axis=0, tiled=True)  16 us
    unnamed x8, local copies, waits for them, and re-layouts  2.46 us
  transfers between devices with their start and end apart: 2, of which 2 were waited for; matrix products, arithmetic and copies ran while one was open for 0% of the time, Pallas kernels for 6%

profile of v5, /device:TPU:0, one launch (start us, length us, event | category | flops | bytes accessed | tf_op | source)
XLA Modules:
  0.0 95.1 jit_solution(7837064789863775457)
XLA Ops:
  0.0 2.9 %shard_map.55 = f32[128,24,128]{2,1,0:T(8,128)} custom-call(s32[1,256]{1,0:T(1,128)} %bitcast.25, f32[4096,128]{1,0:T(8,128)} %bitcast.31), custom_call_target="tpu_custom_call" | custom-call | tf_op jit(solution)/shard_map/pallas_call | solution.py:381
  2.9 0.0 copy-start
  2.9 0.0 copy-start.3
  2.9 11.2 %all-to-all-start = ((f32[3072,1,128]{2,1,0:T(1,128)}), f32[3072,1,128]{2,1,0:T(1,128)S(1)}, u32[]{:S(2)}, u32[]{:S(2)}) async-start(f32[3072,1,128]{2,1,0:T(1,128)} %bitcast.28), calls=%async_computation | async-start | bytes 3145728 | tf_op jit(solution)/shard_map/obs_exchange/all_to_all | solution.py:398
  14.1 0.0 copy-done
  14.1 0.0 copy-done.3
  14.2 0.0 copy-start.1
  14.2 1.2 %copy-done.1 = f32[256,1024]{1,0:T(8,128)S(1)} copy-done((f32[256,1024]{1,0:T(8,128)S(1)}, f32[256,1024]{1,0:T(8,128)}, u32[]{:S(2)}) %copy-start.1) | copy-done | bytes 1048600
  15.4 0.0 copy-start.2
  15.4 1.2 %copy-done.2 = f32[256,1024]{1,0:T(8,128)S(1)} copy-done((f32[256,1024]{1,0:T(8,128)S(1)}, f32[256,1024]{1,0:T(8,128)}, u32[]{:S(2)}) %copy-start.2) | copy-done | bytes 1048600
  16.6 1.8 %shard_map.56 = (f32[2176,128]{1,0:T(8,128)}, f32[8,1024]{1,0:T(8,128)S(1)}) custom-call(s32[1]{0:T(128)} %bitcast.7.mine_ref, s32[1,256]{1,0:T(1,128)S(1)} %bitcast.26, f32[2,256,512]{2,1,0:T(8,128)S(1)} %copy-done, f32[256,1024]{1,0:T(8,128)S(1)} %copy-done.1, f32[256,1024]{1,0:T(8,128)S(1)} %copy-done.2), custom_call_target="tpu_custom_call" | custom-call | tf_op jit(solution)/shard_map/pallas_call | solution.py:381
  18.4 20.2 %all-to-all-done = f32[3072,1,128]{2,1,0:T(1,128)S(1)} async-done(((f32[3072,1,128]{2,1,0:T(1,128)}), f32[3072,1,128]{2,1,0:T(1,128)S(1)}, u32[]{:S(2)}, u32[]{:S(2)}) %all-to-all-start) | async-done | bytes 1572896 | tf_op jit(solution)/shard_map/obs_exchange/all_to_all | solution.py:398
  38.6 1.2 %shard_map.58 = f32[128,17,1,128]{3,2,1,0:T(1,128)} custom-call(f32[3072,128]{1,0:T(8,128)S(1)} %bitcast.20, f32[8,1024]{1,0:T(8,128)S(1)} %get-tuple-element.11.rows_ref, f32[128,17,1,128]{3,2,1,0:T(1,128)} %bitcast.29), custom_call_target="tpu_custom_call", output_to_operand_aliasing={{}: (2, {})} | custom-call | tf_op jit(solution)/shard_map/pallas_call | solution.py:381
  39.8 4.8 %all-to-all-start.1 = ((f32[2176,1,128]{2,1,0:T(1,128)}), f32[2176,1,128]{2,1,0:T(1,128)S(1)}, u32[]{:S(2)}, u32[]{:S(2)}) async-start(f32[2176,1,128]{2,1,0:T(1,128)} %bitcast.30), calls=%async_computation.1 | async-start | bytes 2228224 | tf_op jit(solution)/shard_map/states_exchange/all_to_all | solution.py:398
  44.6 4.0 %shard_map.57 = (f32[3072,128]{1,0:T(8,128)S(1)}, f32[1024,128]{1,0:T(8,128)S(1)}, f32[2,24,256]{2,1,0:T(8,128)S(1)}, bf16[256,256]{1,0:T(8,128)(2,1)S(1)}) custom-call(f32[3072,128]{1,0:T(8,128)S(1)} %bitcast.21, f32[8,1024]{1,0:T(8,128)S(1)} %get-tuple-element.11.rows_ref, s32[1,256]{1,0:T(1,128)S(1)} %bitcast.27), custom_call_target="tpu_custom_call", output_to_operand_aliasing={{0}: (0, {})} | custom-call | tf_op jit(solution)/shard_map/pallas_call | solution.py:381
  48.7 15.5 %all-to-all-done.1 = f32[2176,1,128]{2,1,0:T(1,128)S(1)} async-done(((f32[2176,1,128]{2,1,0:T(1,128)}), f32[2176,1,128]{2,1,0:T(1,128)S(1)}, u32[]{:S(2)}, u32[]{:S(2)}) %all-to-all-start.1) | async-done | bytes 1114144 | tf_op jit(solution)/shard_map/states_exchange/all_to_all | solution.py:398
  64.2 6.3 %shard_map.59 = f32[2048,128]{1,0:T(8,128)S(1)} custom-call(f32[2176,128]{1,0:T(8,128)S(1)} %bitcast.22, f32[3072,128]{1,0:T(8,128)S(1)} %get-tuple-element.14.powers_ref, f32[1024,128]{1,0:T(8,128)S(1)} %get-tuple-element.15.fourth_ref, f32[2,24,256]{2,1,0:T(8,128)S(1)} %get-tuple-element.16.side_ref), custom_call_target="tpu_custom_call" | custom-call | tf_op jit(solution)/shard_map/pallas_call | solution.py:381
  70.5 23.0 %all_to_all.15 = f32[2048,1,128]{2,1,0:T(1,128)S(1)} all-to-all(f32[2048,1,128]{2,1,0:T(1,128)S(1)} %bitcast.24), channel_id=1, replica_groups=mesh['grp'=8,'mem'=16] {'grp','mem'}, dimensions={0} | all-to-all | bytes 2097152 | tf_op jit(solution)/shard_map/return_exchange/all_to_all | solution.py:398
  93.5 1.5 %shard_map.60 = f32[2,256,512]{2,1,0:T(8,128)} custom-call(bf16[256,256]{1,0:T(8,128)(2,1)S(1)} %get-tuple-element.12.spread_ref, f32[2048,128]{1,0:T(8,128)S(1)} %bitcast.23), custom_call_target="tpu_custom_call" | custom-call | tf_op jit(solution)/shard_map/pallas_call | solution.py:381
Async XLA Ops:
  2.9 11.2 %copy-start = (f32[2,256,512]{2,1,0:T(8,128)S(1)}, f32[2,256,512]{2,1,0:T(8,128)}, u32[]{:S(2)}) copy-start(f32[2,256,512]{2,1,0:T(8,128)} %states_ref.1) | copy-start | bytes 3145732
  2.9 11.2 %copy-start.3 = (s32[256]{0:T(256)S(1)}, s32[256]{0:T(256)}, u32[]{:S(2)}) copy-start(s32[256]{0:T(256)} %param.9) | copy-start | bytes 3076
  2.9 35.6 %all-to-all-start = ((f32[3072,1,128]{2,1,0:T(1,128)}), f32[3072,1,128]{2,1,0:T(1,128)S(1)}, u32[]{:S(2)}, u32[]{:S(2)}) async-start(f32[3072,1,128]{2,1,0:T(1,128)} %bitcast.28), calls=%async_computation | async-start | bytes 3145728 | tf_op jit(solution)/shard_map/obs_exchange/all_to_all | solution.py:398
  14.2 1.2 %copy-start.1 = (f32[256,1024]{1,0:T(8,128)S(1)}, f32[256,1024]{1,0:T(8,128)}, u32[]{:S(2)}) copy-start(f32[256,1024]{1,0:T(8,128)} %value_ref.1) | copy-start | bytes 3145732
  15.4 1.2 %copy-start.2 = (f32[256,1024]{1,0:T(8,128)S(1)}, f32[256,1024]{1,0:T(8,128)}, u32[]{:S(2)}) copy-start(f32[256,1024]{1,0:T(8,128)} %precision_ref.1) | copy-start | bytes 3145732
  39.8 24.4 %all-to-all-start.1 = ((f32[2176,1,128]{2,1,0:T(1,128)}), f32[2176,1,128]{2,1,0:T(1,128)S(1)}, u32[]{:S(2)}, u32[]{:S(2)}) async-start(f32[2176,1,128]{2,1,0:T(1,128)} %bitcast.30), calls=%async_computation.1 | async-start | bytes 2228224 | tf_op jit(solution)/shard_map/states_exchange/all_to_all | solution.py:398

commit v6 on v5

--- a/solution.py
+++ b/solution.py
@@ -54,14 +54,15 @@
 def owners(counts, half, devices):
     patches = counts.shape[1]
     heavy = (counts > half).astype(F32)
-    before = lax.broadcasted_iota(jnp.int32, (patches, patches), 0) < lax.broadcasted_iota(
-        jnp.int32, (patches, patches), 1
-    )
-    rank = dot(jnp.broadcast_to(heavy, (8, patches)).astype(BF16), before.astype(F32).astype(BF16))[:1]
-    position = lax.broadcasted_iota(jnp.int32, (1, patches), 1).astype(F32)
+    key = counts.astype(F32) * patches + lax.broadcasted_iota(jnp.int32, (1, patches), 1).astype(F32)
+    sign = jnp.where(heavy > 0.0, -1.0, 1.0)
+    order = sign * key
+    column = jnp.broadcast_to(order, (8, patches)).T[:, :1]
+    before = jnp.where((column < order) & ((column < 0.0) == (order < 0.0)), 1.0, 0.0)
+    rank = jnp.sum(before, axis=0, keepdims=True)
     device = lax.broadcasted_iota(jnp.int32, (devices, patches), 0).astype(F32)
     heavies = jnp.where((device == rank) & (heavy > 0.0), 1.0, 0.0)
-    lights = jnp.where((device == position - rank) & (heavy == 0.0), 1.0, 0.0)
+    lights = jnp.where((device == rank) & (heavy == 0.0), 1.0, 0.0)
     return heavies, lights
 
 
@@ -70,8 +71,13 @@
         ref[pl.ds(first + j, x.shape[0], stride=stride), :] = x[:, j * LANES : (j + 1) * LANES]
 
 
-def load_rows(ref, first, rows, blocks):
-    return jnp.concatenate([ref[first + j * rows : first + (j + 1) * rows] for j in range(blocks)], axis=1)
+def tiles_sent(slots):
+    return slots // LANES + slots // LANES // 4
+
+
+def light_position(tile, slots):
+    blocks = slots // LANES
+    return blocks + tile if tile < blocks // 4 else blocks + blocks // 4 - 1 - tile
 
 
 def pick(onehot, x):
@@ -79,12 +85,14 @@
     return dot(jnp.concatenate([chosen] * 3, axis=1), jnp.concatenate(thirds(x), axis=0))
 
 
-def pack_obs_kernel(counts_hbm, obs_hbm, out_hbm, counts_ref, obs_ref, out_ref, table_ref, table, sems, *, slots):
+def pack_obs_kernel(counts_hbm, obs_hbm, out_hbm, flag_ref, counts_ref, obs_ref, out_ref, table_ref, table, sems, *, slots):
     patches = counts_ref.shape[1]
     blocks = slots // LANES
     each = patches * blocks
     local = obs_hbm.shape[0] // each
-    devices, per = out_hbm.shape[:2]
+    sent_tiles = tiles_sent(slots)
+    per = local * sent_tiles
+    devices = out_hbm.shape[0] // per
     count_copy = pltpu.make_async_copy(counts_hbm, counts_ref, sems.at[0])
     count_copy.start()
     copies = []
@@ -97,9 +105,19 @@
     onehots = owners(counts_ref[...], slots // 2, devices)
     position = lax.broadcasted_iota(jnp.int32, (8, patches), 1).astype(F32).astype(BF16)
     index = [dot_nt(position, onehot.astype(BF16)).astype(jnp.int32) for onehot in onehots]
+    lengths = ((counts_ref[...] + (LANES - 1)) >> 7).astype(F32)
+    lengths = jnp.broadcast_to(lengths, (8, patches)).astype(BF16)
+    long, short = (dot_nt(lengths, onehot.astype(BF16)).astype(jnp.int32) for onehot in onehots)
+    excess = jnp.max((long + short).astype(F32), axis=1, keepdims=True) - sent_tiles
+    flag_ref[...] = jnp.broadcast_to(excess, flag_ref.shape)
     start = [(p >> 3) * (8 * blocks) + (p & 7) for p in index]
     row = lax.broadcasted_iota(jnp.int32, (8, devices), 0)
-    table_ref[...] = jnp.where(row == 0, start[0], start[1])
+    entries = jnp.where(row == 0, start[0], start[1])
+    shared = [t for t in range(blocks // 2) if light_position(t, slots) < blocks]
+    for i, t in enumerate(shared):
+        at = light_position(t, slots)
+        entries = jnp.where(row == 2 + i, jnp.where(long > at, start[0] + 8 * at, start[1] + 8 * t), entries)
+    table_ref[...] = entries
     table_copy = pltpu.make_async_copy(table_ref, table, sems.at[0])
     table_copy.start()
     table_copy.wait()
@@ -107,30 +125,42 @@
     for copy in copies:
         copy.wait()
     group = devices // OUT_PIECES
+    own = blocks - len(shared)
+    rest = blocks // 2 - len(shared)
     for g in range(OUT_PIECES):
-
-        @pl.loop(g * group, (g + 1) * group, unroll=32)
-        def _(d):
-            heavy = table[0, d]
-            light = table[1, d]
+        for d in range(g * group, (g + 1) * group):
             for m in range(local):
-                out_ref[d, m * blocks : (m + 1) * blocks, :] = obs_ref[pl.ds(m * each + heavy, blocks, stride=8), :]
-                at = local * blocks + m * blocks // 2
-                out_ref[d, at : at + blocks // 2, :] = obs_ref[pl.ds(m * each + light, blocks // 2, stride=8), :]
-
-        some = pl.ds(g * group, group)
-        sent.append(pltpu.make_async_copy(out_ref.at[some], out_hbm.at[some], sems.at[1 + local * IN_PIECES + g]))
+                first = d * per + m * sent_tiles
+                heavy, light = m * each + table[0, d], m * each + table[1, d]
+                out_ref[first : first + own, :] = obs_ref[pl.ds(heavy, own, stride=8), :]
+                for i, t in enumerate(shared):
+                    at = first + light_position(t, slots)
+                    out_ref[at : at + 1, :] = obs_ref[pl.ds(m * each + table[2 + i, d], 1), :]
+                out_ref[first + blocks : first + blocks + rest, :] = obs_ref[pl.ds(light, rest, stride=8), :]
+        some = pl.ds(g * group * per, group * per)
+        sent.append(
+            pltpu.make_async_copy(out_ref.at[some], out_hbm.at[some], sems.at[1 + local * IN_PIECES + g])
+        )
         sent[-1].start()
     for copy in sent:
         copy.wait()
 
 
-def pack_states_kernel(mine_ref, counts_ref, states_ref, value_ref, precision_ref, out_hbm, rows_ref, out_ref, sem):
+def pack_states_kernel(
+    mine_ref, counts_ref, states_ref, value_ref, precision_ref, obs_hbm, out_hbm, extra_hbm, rows_ref, out_ref, extra_ref, obs_ref, sems
+):
     local, patches, cells = states_ref.shape
     slots = value_ref.shape[1]
     blocks = cells // LANES
     per = 2 * local * blocks + 1
     devices = out_ref.shape[0] // per
+    quarter = slots // 4
+    obs_copies = []
+    for m in range(local):
+        obs_copies.append(
+            pltpu.make_async_copy(obs_hbm.at[m, :, pl.ds(quarter, quarter)], obs_ref.at[m], sems.at[2 + m])
+        )
+        obs_copies[-1].start()
     counts = counts_ref[...]
     heavies, lights = owners(counts, slots // 2, devices)
     both = jnp.concatenate([heavies, lights], axis=0)
@@ -139,8 +169,13 @@
         for k in range(2):
             store_rows(out_ref, (k * local + m) * blocks, per, chosen[k * devices : (k + 1) * devices])
     out_ref[pl.ds(per - 1, devices, stride=per), :] = jnp.zeros((devices, LANES), F32)
-    copy = pltpu.make_async_copy(out_ref, out_hbm, sem)
+    copy = pltpu.make_async_copy(out_ref, out_hbm, sems.at[0])
     copy.start()
+    for m in range(local):
+        obs_copies[m].wait()
+        store_rows(extra_ref, m * quarter // LANES, local * quarter // LANES, pick(lights, obs_ref[m]))
+    extra_copy = pltpu.make_async_copy(extra_ref, extra_hbm, sems.at[1])
+    extra_copy.start()
     here = lax.broadcasted_iota(jnp.int32, (devices, patches), 0) == mine_ref[0]
     own = [jnp.sum(jnp.where(here, onehot, 0.0), axis=0, keepdims=True) for onehot in (heavies, lights)]
     both = jnp.concatenate(own + [jnp.zeros((6, patches), F32)], axis=0)
@@ -152,34 +187,42 @@
         count = jnp.sum(own[k] * counts.astype(F32), axis=1, keepdims=True)
         live = jnp.where(slot < count, 1.0, 0.0)
         rows += [values[k : k + 1], precisions[k : k + 1], live]
-    rows_ref[...] = jnp.concatenate(rows + [jnp.zeros((2, slots), F32)], axis=0)
+    length = jnp.sum(own[0] * counts.astype(F32), axis=1, keepdims=True)
+    rows_ref[...] = jnp.concatenate(rows + [jnp.broadcast_to(length, (2, slots))], axis=0)
     copy.wait()
-
-
-def obs_columns(obs_ref, rows_ref, local):
+    extra_copy.wait()
+
+
+def obs_columns(obs_ref, extra_ref, rows_ref, local):
     slots = rows_ref.shape[1]
-    half = slots // 2
-    per = (slots + half) // LANES * local
+    blocks = slots // LANES
+    per = tiles_sent(slots) * local
     devices = obs_ref.shape[0] // per
+    length = rows_ref[6:7, :LANES]
     for k in range(2):
-        width = slots if k == 0 else half
-        base = 0 if k == 0 else local * (slots // LANES)
-        for c in range(width // LANES):
+        for c in range(blocks if k == 0 else blocks // 2):
             columns = slice(c * LANES, (c + 1) * LANES)
-            parts = [
-                obs_ref[pl.ds(base + m * (width // LANES) + c, devices, stride=per), :] for m in range(local)
-            ]
+            at = c if k == 0 else light_position(c, slots)
+            parts = [obs_ref[pl.ds(m * tiles_sent(slots) + at, devices, stride=per), :] for m in range(local)]
+            if k == 1 and at < blocks:
+                more = [
+                    extra_ref[
+                        pl.ds(m * (blocks // 4) + c - blocks // 4, devices, stride=local * (blocks // 4)), :
+                    ]
+                    for m in range(local)
+                ]
+                parts = [jnp.where(length > at * LANES, x, p) for x, p in zip(more, parts)]
             mean = sum(jnp.sum(p, axis=0, keepdims=True) for p in parts) * (1.0 / (local * devices))
             value, precision, live = (rows_ref[3 * k + i : 3 * k + i + 1, columns] for i in range(3))
             yield k, columns, [p - mean for p in parts], value - mean, precision, live
 
 
-def sums_kernel(obs_ref, rows_ref, states_hbm, out_hbm, row_ref, sem, *, local):
+def sums_kernel(obs_ref, extra_ref, rows_ref, states_hbm, out_hbm, row_ref, sem, *, local):
     devices, per = out_hbm.shape[:2]
     members = local * devices
     misfit = jnp.zeros((1, LANES), F32)
     expected = jnp.zeros((1, LANES), F32)
-    for _, _, parts, innov, precision, live in obs_columns(obs_ref, rows_ref, local):
+    for _, _, parts, innov, precision, live in obs_columns(obs_ref, extra_ref, rows_ref, local):
         spread = sum(jnp.sum(p * p, axis=0, keepdims=True) for p in parts) * (1.0 / (members - 1.0))
         misfit += precision * live * innov * innov
         expected += live * (1.0 + precision * spread)
@@ -195,14 +238,22 @@
     copy.wait()
 
 
+def power_place(powers_ref, more_ref, members, k, i, h):
+    place = (i * 2 + k) * (members // LANES) + h
+    held = powers_ref.shape[0] // members
+    return (powers_ref, place * members) if place < held else (more_ref, (place - held) * members)
+
+
 def gram_kernel(
-    obs_ref, rows_ref, counts_ref, powers_ref, fourth_ref, side_ref, spread_ref, high_ref, low_ref, *, local
+    obs_ref, extra_ref, rows_ref, counts_ref, powers_ref, more_ref, side_ref, spread_hbm, high_ref, low_ref, spread_ref, sem, *, local
 ):
     slots = rows_ref.shape[1]
     members = side_ref.shape[2]
     devices = members // local
     spread_ref[...] = jnp.concatenate(owners(counts_ref[...], slots // 2, devices), axis=0).T.astype(BF16)
-    for k, columns, parts, innov, precision, live in obs_columns(obs_ref, rows_ref, local):
+    copy = pltpu.make_async_copy(spread_ref, spread_hbm, sem)
+    copy.start()
+    for k, columns, parts, innov, precision, live in obs_columns(obs_ref, extra_ref, rows_ref, local):
         scale = jnp.sqrt(precision * live)
         for m in range(local):
             high, low = halves(parts[m] * scale)
@@ -226,21 +277,18 @@
             jnp.sum(jnp.where(diagonal, unit, 0.0), axis=0, keepdims=True), axis=1, keepdims=True
         )
         second = exact_dot(unit, unit)
-        for i, power in enumerate((unit, second, exact_dot(unit, second))):
+        for i, power in enumerate((unit, second, exact_dot(unit, second), exact_dot(second, second))):
             for h in range(members // LANES):
-                first = ((k * 3 + i) * (members // LANES) + h) * members
-                powers_ref[first : first + members] = power[:, h * LANES : (h + 1) * LANES]
-        fourth = exact_dot(second, second)
-        for h in range(members // LANES):
-            first = (k * (members // LANES) + h) * members
-            fourth_ref[first : first + members] = fourth[:, h * LANES : (h + 1) * LANES]
+                ref, first = power_place(powers_ref, more_ref, members, k, i, h)
+                ref[first : first + members] = power[:, h * LANES : (h + 1) * LANES]
         side_ref[k] = jnp.concatenate(
             [forcing, jnp.broadcast_to(size, (8, members)), jnp.broadcast_to(trace, (8, members))], axis=0
         )
+    copy.wait()
 
 
 def update_kernel(
-    states_ref, powers_ref, fourth_ref, side_ref, out_ref, s_ref, z_ref, states_right, center_ref, *, local
+    states_ref, powers_ref, more_ref, side_ref, out_ref, s_ref, z_ref, states_right, center_ref, *, local
 ):
     members = side_ref.shape[2]
     devices = members // local
@@ -294,9 +342,10 @@
         d = (1.5 - 0.5 * s1[0], -0.5 * s1[1], -0.5 * s1[2], -0.5 * s1[3])
         h = -0.5 * b
         z2 = (f * d[0], f * d[1] + h * d[0], f * d[2] + h * d[1], f * d[3] + h * d[2], h * d[3])
-        halfs = members // LANES
-        powers = [load_rows(powers_ref, (k * 3 + i) * halfs * members, members, halfs) for i in range(3)]
-        powers.append(load_rows(fourth_ref, k * halfs * members, members, halfs))
+        powers = []
+        for i in range(4):
+            places = [power_place(powers_ref, more_ref, members, k, i, h) for h in range(members // LANES)]
+            powers.append(jnp.concatenate([ref[first : first + members] for ref, first in places], axis=1))
         put(s_ref, k, plus_diagonal(sum(c * p for c, p in zip(s1[1:], powers)), s1[0]))
         put(z_ref, k, plus_diagonal(sum(c * p for c, p in zip(z2[1:], powers)), z2[0]))
     for k in range(2):
@@ -405,57 +454,71 @@
     members = local * devices
     counts = obs_count.reshape(1, patches)
     mine = lax.axis_index(AXES).astype(jnp.int32).reshape(1)
-    obs_rows = 3 * slots // 2 // LANES * local
+    obs_rows = tiles_sent(slots) * local
+    extra_rows = local * slots // 4 // LANES
     state_rows = 2 * local * cells // LANES
     blocks = slots // LANES
     in_memory = obs_ensemble.reshape(local, patches // 8, 8, blocks, LANES).swapaxes(2, 3).reshape(-1, LANES)
-    (obs_sent,) = call(
+    obs_sent, excess = call(
         functools.partial(pack_obs_kernel, slots=slots),
-        [(devices, obs_rows, LANES)],
+        [(devices * obs_rows, LANES), (8, LANES)],
         (counts, in_memory),
         ins=[HBM, HBM],
-        outs=[HBM],
+        outs=[HBM, WHOLE],
         scratch=[
             pltpu.VMEM((1, patches), jnp.int32),
             pltpu.VMEM(in_memory.shape, F32),
-            pltpu.VMEM((devices, obs_rows, LANES), F32),
+            pltpu.VMEM((devices * obs_rows, LANES), F32),
             pltpu.VMEM((8, devices), jnp.int32),
             pltpu.SMEM((8, devices), jnp.int32),
             pltpu.SemaphoreType.DMA((1 + local * IN_PIECES + OUT_PIECES,)),
         ],
     )
     obs = exchange(obs_sent, "obs_exchange")
-    states_sent, rows = call(
+    states_sent, extra_sent, rows = call(
         pack_states_kernel,
-        [(devices * (state_rows + 1), LANES), (8, slots)],
-        (mine, counts, background, obs_value, obs_precision),
-        ins=[SCALAR] + [WHOLE] * 4,
-        outs=[HBM, WHOLE],
-        scratch=[pltpu.VMEM((devices * (state_rows + 1), LANES), F32), pltpu.SemaphoreType.DMA],
-    )
+        [(devices * (state_rows + 1), LANES), (devices * extra_rows, LANES), (8, slots)],
+        (mine, counts, background, obs_value, obs_precision, obs_ensemble),
+        ins=[SCALAR] + [WHOLE] * 4 + [HBM],
+        outs=[HBM, HBM, WHOLE],
+        scratch=[
+            pltpu.VMEM((devices * (state_rows + 1), LANES), F32),
+            pltpu.VMEM((devices * extra_rows, LANES), F32),
+            pltpu.VMEM((local, patches, slots // 4), F32),
+            pltpu.SemaphoreType.DMA((2 + local,)),
+        ],
+    )
+    obs, extra_sent = lax.optimization_barrier((obs, extra_sent))
+    extra = lax.cond(excess[0, 0] > 0.0, lambda x: exchange(x, "extra_exchange"), jnp.zeros_like, extra_sent)
     states_sent = states_sent.reshape(devices, state_rows + 1, 1, LANES)
     (states_sent,) = call(
         functools.partial(sums_kernel, local=local),
         [states_sent.shape],
-        (obs, rows, states_sent),
-        ins=[WHOLE, WHOLE, HBM],
+        (obs, extra, rows, states_sent),
+        ins=[WHOLE, WHOLE, WHOLE, HBM],
         outs=[HBM],
         scratch=[pltpu.VMEM((devices, 1, LANES), F32), pltpu.SemaphoreType.DMA],
-        aliases={2: 0},
+        aliases={3: 0},
     )
     states = exchange(states_sent, "states_exchange")
-    powers, fourth, side, spread = call(
+    powers, more, side, spread = call(
         functools.partial(gram_kernel, local=local),
-        [obs.shape, (2 * members * members // LANES, LANES), (2, 24, members), (patches, members)],
-        (obs, rows, counts),
+        [obs.shape, (8 * members * members // LANES - obs.shape[0], LANES), (2, 24, members), (patches, members)],
+        (obs, extra, rows, counts),
+        outs=[WHOLE, WHOLE, WHOLE, HBM],
         types=[F32, F32, F32, BF16],
-        scratch=[pltpu.VMEM((2, members + 16, slots), BF16)] * 2,
+        scratch=[
+            pltpu.VMEM((2, members + 16, slots), BF16),
+            pltpu.VMEM((2, members + 16, slots), BF16),
+            pltpu.VMEM((patches, members), BF16),
+            pltpu.SemaphoreType.DMA,
+        ],
         aliases={0: 0},
     )
     (update,) = call(
         functools.partial(update_kernel, local=local),
         [(devices * state_rows, LANES)],
-        (states, powers, fourth, side),
+        (states, powers, more, side),
         scratch=[
             pltpu.VMEM((2, 2, members, members), BF16),
             pltpu.VMEM((2, 2, members, members), BF16),

time: 95.5 us -> 93.3 us (0.977)
  waiting for transfers between devices: 35.7 us -> 31.2 us
  Pallas kernels: 17.7 us -> 19.8 us
    all_to_all x2, waiting for transfers between devices: 35.7 us -> 31.2 us  [exchange(): lax.all_to_all(rows, AXES, split_axis=0, concat_axis=0, tiled=True)]
    pallas_call x6, Pallas kernels: 17.7 us -> 19.8 us  [call(): pl.pallas_call(kernel, out_shape=[pltpu.HBM(shape, kind) if s is HBM else...]
    unnamed x8 -> x12, local copies, waits for them, and re-layouts: 2.46 us -> 1.25 us
  transfers between devices with their start and end apart: 2 -> 2, of which waited for: 2 -> 2; matrix products, arithmetic and copies ran while one was open for 0% -> 1% of each run, Pallas kernels for 6% -> 8%
where the time goes in v6:
time: 93.3 us; the launch traced here: 92.9 us
  waiting for transfers between devices  31.2 us (33%)
  blocking collectives  23.1 us (25%)
  Pallas kernels  19.8 us (21%)
  starting transfers between devices  16 us (17%)
  local copies, waits for them, and re-layouts  1.78 us (2%)
  between operations  0.97 us (1%)
    all_to_all x2, waiting for transfers between devices, exchange(): lax.all_to_all(rows, AXES, split_axis=0, concat_axis=0, tiled=True)  31.2 us
    all_to_all x1, blocking collectives, exchange(): lax.all_to_all(rows, AXES, split_axis=0, concat_axis=0, tiled=True)  23.1 us
    pallas_call x6, Pallas kernels, call(): pl.pallas_call(kernel, out_shape=[pltpu.HBM(shape, kind) if s is HBM else...  19.8 us
    all_to_all x2, starting transfers between devices, exchange(): lax.all_to_all(rows, AXES, split_axis=0, concat_axis=0, tiled=True)  16 us
  transfers between devices with their start and end apart: 2, of which 2 were waited for; matrix products, arithmetic and copies ran while one was open for 1% of the time, Pallas kernels for 8%

profile of v6, /device:TPU:0, one launch (start us, length us, event | category | flops | bytes accessed | tf_op | source)
XLA Modules:
  0.0 92.9 jit_solution(12909405190582037008)
XLA Ops:
  0.0 3.2 %shard_map.55 = (f32[2560,128]{1,0:T(8,128)}, f32[8,128]{1,0:T(8,128)S(1)}) custom-call(s32[1,256]{1,0:T(1,128)} %bitcast.28, f32[4096,128]{1,0:T(8,128)} %bitcast.31), custom_call_target="tpu_custom_call" | custom-call | tf_op jit(solution)/shard_map/pallas_call | solution.py:430
  3.3 0.0 copy-start
  3.3 0.0 copy-start.1
  3.3 0.0 copy-start.4
  3.3 11.2 %all-to-all-start.1 = ((f32[2560,1,128]{2,1,0:T(1,128)}), f32[2560,1,128]{2,1,0:T(1,128)S(1)}, u32[]{:S(2)}, u32[]{:S(2)}) async-start(f32[2560,1,128]{2,1,0:T(1,128)} %bitcast.35), calls=%async_computation.1 | async-start | bytes 2621440 | tf_op jit(solution)/shard_map/obs_exchange/all_to_all | solution.py:447
  14.5 0.5 slice.3
  15.7 0.0 copy-done
  15.7 0.0 copy-done.1
  15.7 0.0 copy-done.4
  15.7 0.0 copy-start.2
  15.7 1.2 %copy-done.2 = f32[256,1024]{1,0:T(8,128)S(1)} copy-done((f32[256,1024]{1,0:T(8,128)S(1)}, f32[256,1024]{1,0:T(8,128)}, u32[]{:S(2)}) %copy-start.2) | copy-done | bytes 1048600
  16.9 2.3 %shard_map.56 = (f32[2176,128]{1,0:T(8,128)}, f32[512,128]{1,0:T(8,128)}, f32[8,1024]{1,0:T(8,128)S(1)}) custom-call(s32[1]{0:T(128)} %bitcast.9.mine_ref, s32[1,256]{1,0:T(1,128)S(1)} %bitcast.29, f32[2,256,512]{2,1,0:T(8,128)S(1)} %copy-done, f32[256,1024]{1,0:T(8,128)S(1)} %copy-done.1, f32[256,1024]{1,0:T(8,128)S(1)} %copy-done.2, f32[2,256,1024]{2,1,0:T(8,128)} %obs_hbm.1), custom_call_target="tpu_custom_call" | custom-call | tf_op jit(solution)/shard_map/pallas_call | solution.py:430
  19.2 17.0 %all-to-all-done.1 = f32[2560,1,128]{2,1,0:T(1,128)S(1)} async-done(((f32[2560,1,128]{2,1,0:T(1,128)}), f32[2560,1,128]{2,1,0:T(1,128)S(1)}, u32[]{:S(2)}, u32[]{:S(2)}) %all-to-all-start.1) | async-done | bytes 1310752 | tf_op jit(solution)/shard_map/obs_exchange/all_to_all | solution.py:447
  36.3 0.0 copy-start.5
  36.3 1.1 %shard_map.58 = f32[128,17,1,128]{3,2,1,0:T(1,128)} custom-call(f32[2560,128]{1,0:T(8,128)S(1)} %bitcast.23, f32[512,128]{1,0:T(8,128)S(1)} %get-tuple-element.31.extra_ref, f32[8,1024]{1,0:T(8,128)S(1)} %get-tuple-element.25.rows_ref, f32[128,17,1,128]{3,2,1,0:T(1,128)} %bitcast.32), custom_call_target="tpu_custom_call", output_to_operand_aliasing={{}: (3, {})} | custom-call | tf_op jit(solution)/shard_map/pallas_call | solution.py:430
  37.4 0.0 copy-done.5
  37.4 4.8 %all-to-all-start.2 = ((f32[2176,1,128]{2,1,0:T(1,128)}), f32[2176,1,128]{2,1,0:T(1,128)S(1)}, u32[]{:S(2)}, u32[]{:S(2)}) async-start(f32[2176,1,128]{2,1,0:T(1,128)} %bitcast.33), calls=%async_computation.2 | async-start | bytes 2228224 | tf_op jit(solution)/shard_map/states_exchange/all_to_all | solution.py:447
  42.2 5.3 %shard_map.57 = (f32[2560,128]{1,0:T(8,128)S(1)}, f32[1536,128]{1,0:T(8,128)S(1)}, f32[2,24,256]{2,1,0:T(8,128)S(1)}, bf16[256,256]{1,0:T(8,128)(2,1)}) custom-call(f32[2560,128]{1,0:T(8,128)S(1)} %bitcast.24, f32[512,128]{1,0:T(8,128)} %copy-done.5, f32[8,1024]{1,0:T(8,128)S(1)} %get-tuple-element.25.rows_ref, ...), custom_call_target="tpu_custom_call", output_to_operand_aliasing={{0}: (0, {})} | custom-call | tf_op jit(solution)/shard_map/pallas_call | solution.py:430
  47.6 14.2 %all-to-all-done.2 = f32[2176,1,128]{2,1,0:T(1,128)S(1)} async-done(((f32[2176,1,128]{2,1,0:T(1,128)}), f32[2176,1,128]{2,1,0:T(1,128)S(1)}, u32[]{:S(2)}, u32[]{:S(2)}) %all-to-all-start.2) | async-done | bytes 1114144 | tf_op jit(solution)/shard_map/states_exchange/all_to_all | solution.py:447
  61.7 6.3 %shard_map.59 = f32[2048,128]{1,0:T(8,128)S(1)} custom-call(f32[2176,128]{1,0:T(8,128)S(1)} %bitcast.25, f32[2560,128]{1,0:T(8,128)S(1)} %get-tuple-element.28.powers_ref, f32[1536,128]{1,0:T(8,128)S(1)} %get-tuple-element.29.more_ref, f32[2,24,256]{2,1,0:T(8,128)S(1)} %get-tuple-element.30.side_ref), custom_call_target="tpu_custom_call" | custom-call | tf_op jit(solution)/shard_map/pallas_call | solution.py:430
  68.1 0.0 copy-start.3
  68.1 23.1 %all_to_all.20 = f32[2048,1,128]{2,1,0:T(1,128)S(1)} all-to-all(f32[2048,1,128]{2,1,0:T(1,128)S(1)} %bitcast.27), channel_id=1, replica_groups=mesh['grp'=8,'mem'=16] {'grp','mem'}, dimensions={0} | all-to-all | bytes 2097152 | tf_op jit(solution)/shard_map/return_exchange/all_to_all | solution.py:447
  91.2 0.0 copy-done.3
  91.2 1.5 %shard_map.60 = f32[2,256,512]{2,1,0:T(8,128)} custom-call(bf16[256,256]{1,0:T(8,128)(2,1)S(1)} %copy-done.3, f32[2048,128]{1,0:T(8,128)S(1)} %bitcast.26), custom_call_target="tpu_custom_call" | custom-call | tf_op jit(solution)/shard_map/pallas_call | solution.py:430
  (2 shorter events, 0.0 us)
Async XLA Ops:
  3.3 12.4 %copy-start = (f32[2,256,512]{2,1,0:T(8,128)S(1)}, f32[2,256,512]{2,1,0:T(8,128)}, u32[]{:S(2)}) copy-start(f32[2,256,512]{2,1,0:T(8,128)} %states_ref.1) | copy-start | bytes 3145732
  3.3 12.4 %copy-start.1 = (f32[256,1024]{1,0:T(8,128)S(1)}, f32[256,1024]{1,0:T(8,128)}, u32[]{:S(2)}) copy-start(f32[256,1024]{1,0:T(8,128)} %value_ref.1) | copy-start | bytes 3145732
  3.3 12.4 %copy-start.4 = (s32[256]{0:T(256)S(1)}, s32[256]{0:T(256)}, u32[]{:S(2)}) copy-start(s32[256]{0:T(256)} %param.11) | copy-start | bytes 3076
  3.3 32.9 %all-to-all-start.1 = ((f32[2560,1,128]{2,1,0:T(1,128)}), f32[2560,1,128]{2,1,0:T(1,128)S(1)}, u32[]{:S(2)}, u32[]{:S(2)}) async-start(f32[2560,1,128]{2,1,0:T(1,128)} %bitcast.35), calls=%async_computation.1 | async-start | bytes 2621440 | tf_op jit(solution)/shard_map/obs_exchange/all_to_all | solution.py:447
  15.7 1.2 %copy-start.2 = (f32[256,1024]{1,0:T(8,128)S(1)}, f32[256,1024]{1,0:T(8,128)}, u32[]{:S(2)}) copy-start(f32[256,1024]{1,0:T(8,128)} %precision_ref.1) | copy-start | bytes 3145732
  36.3 1.1 %copy-start.5 = (f32[512,128]{1,0:T(8,128)}, f32[512,128]{1,0:T(8,128)S(1)}, u32[]{:S(2)}) copy-start(f32[512,128]{1,0:T(8,128)S(1)} %get-tuple-element.31.extra_ref) | copy-start | bytes 786436
  37.4 24.4 %all-to-all-start.2 = ((f32[2176,1,128]{2,1,0:T(1,128)}), f32[2176,1,128]{2,1,0:T(1,128)S(1)}, u32[]{:S(2)}, u32[]{:S(2)}) async-start(f32[2176,1,128]{2,1,0:T(1,128)} %bitcast.33), calls=%async_computation.2 | async-start | bytes 2228224 | tf_op jit(solution)/shard_map/states_exchange/all_to_all | solution.py:447
  68.1 23.2 %copy-start.3 = (bf16[256,256]{1,0:T(8,128)(2,1)S(1)}, bf16[256,256]{1,0:T(8,128)(2,1)}, u32[]{:S(2)}) copy-start(bf16[256,256]{1,0:T(8,128)(2,1)} %get-tuple-element.26.spread_ref) | copy-start | bytes 393220

commit v7 on v6

--- a/solution.py
+++ b/solution.py
@@ -14,7 +14,7 @@
 BF16 = jnp.bfloat16
 VMEM_LIMIT = 12 << 20
 IN_PIECES = 2
-OUT_PIECES = 4
+OUT_PIECES = 8
 
 
 def dot(a, b):
@@ -85,7 +85,7 @@
     return dot(jnp.concatenate([chosen] * 3, axis=1), jnp.concatenate(thirds(x), axis=0))
 
 
-def pack_obs_kernel(counts_hbm, obs_hbm, out_hbm, flag_ref, counts_ref, obs_ref, out_ref, table_ref, table, sems, *, slots):
+def pack_obs_kernel(counts_hbm, obs_hbm, out_hbm, flag_ref, counts_ref, obs_ref, out_ref, sems, *, slots):
     patches = counts_ref.shape[1]
     blocks = slots // LANES
     each = patches * blocks
@@ -103,24 +103,21 @@
         copies[-1].start()
     count_copy.wait()
     onehots = owners(counts_ref[...], slots // 2, devices)
-    position = lax.broadcasted_iota(jnp.int32, (8, patches), 1).astype(F32).astype(BF16)
-    index = [dot_nt(position, onehot.astype(BF16)).astype(jnp.int32) for onehot in onehots]
     lengths = ((counts_ref[...] + (LANES - 1)) >> 7).astype(F32)
-    lengths = jnp.broadcast_to(lengths, (8, patches)).astype(BF16)
-    long, short = (dot_nt(lengths, onehot.astype(BF16)).astype(jnp.int32) for onehot in onehots)
+    position = lax.broadcasted_iota(jnp.int32, (8, patches), 1).astype(F32)
+    first_row = lax.broadcasted_iota(jnp.int32, (8, patches), 0) == 0
+    facts = dot_nt(
+        jnp.where(first_row, position, lengths).astype(BF16), jnp.concatenate(onehots, axis=0).astype(BF16)
+    ).astype(jnp.int32)
+    index = [facts[:1, :devices], facts[:1, devices:]]
+    long, short = facts[1:2, :devices], facts[1:2, devices:]
     excess = jnp.max((long + short).astype(F32), axis=1, keepdims=True) - sent_tiles
     flag_ref[...] = jnp.broadcast_to(excess, flag_ref.shape)
     start = [(p >> 3) * (8 * blocks) + (p & 7) for p in index]
-    row = lax.broadcasted_iota(jnp.int32, (8, devices), 0)
-    entries = jnp.where(row == 0, start[0], start[1])
     shared = [t for t in range(blocks // 2) if light_position(t, slots) < blocks]
+    packed = start[0] + (start[1] << 12)
     for i, t in enumerate(shared):
-        at = light_position(t, slots)
-        entries = jnp.where(row == 2 + i, jnp.where(long > at, start[0] + 8 * at, start[1] + 8 * t), entries)
-    table_ref[...] = entries
-    table_copy = pltpu.make_async_copy(table_ref, table, sems.at[0])
-    table_copy.start()
-    table_copy.wait()
+        packed += jnp.where(long > light_position(t, slots), 1 << (24 + i), 0)
     sent = []
     for copy in copies:
         copy.wait()
@@ -129,13 +126,23 @@
     rest = blocks // 2 - len(shared)
     for g in range(OUT_PIECES):
         for d in range(g * group, (g + 1) * group):
+            entry = packed[0, d]
+            heavy_start, light_start = entry & 4095, (entry >> 12) & 4095
+            middle = [
+                jnp.where(
+                    (entry >> (24 + i)) & 1 == 1,
+                    heavy_start + 8 * light_position(t, slots),
+                    light_start + 8 * t,
+                )
+                for i, t in enumerate(shared)
+            ]
             for m in range(local):
                 first = d * per + m * sent_tiles
-                heavy, light = m * each + table[0, d], m * each + table[1, d]
+                heavy, light = m * each + heavy_start, m * each + light_start
                 out_ref[first : first + own, :] = obs_ref[pl.ds(heavy, own, stride=8), :]
                 for i, t in enumerate(shared):
                     at = first + light_position(t, slots)
-                    out_ref[at : at + 1, :] = obs_ref[pl.ds(m * each + table[2 + i, d], 1), :]
+                    out_ref[at : at + 1, :] = obs_ref[pl.ds(m * each + middle[i], 1), :]
                 out_ref[first + blocks : first + blocks + rest, :] = obs_ref[pl.ds(light, rest, stride=8), :]
         some = pl.ds(g * group * per, group * per)
         sent.append(
@@ -469,8 +476,6 @@
             pltpu.VMEM((1, patches), jnp.int32),
             pltpu.VMEM(in_memory.shape, F32),
             pltpu.VMEM((devices * obs_rows, LANES), F32),
-            pltpu.VMEM((8, devices), jnp.int32),
-            pltpu.SMEM((8, devices), jnp.int32),
             pltpu.SemaphoreType.DMA((1 + local * IN_PIECES + OUT_PIECES,)),
         ],
     )

time: 93.3 us -> 93.2 us (level)
  no operation moved by 1% of the time
where the time goes in v7:
time: 93.2 us; the launch traced here: 92.9 us
  waiting for transfers between devices  31.2 us (33%)
  blocking collectives  23.1 us (25%)
  Pallas kernels  19.8 us (21%)
  starting transfers between devices  16 us (17%)
  local copies, waits for them, and re-layouts  1.78 us (2%)
  between operations  0.97 us (1%)
    all_to_all x2, waiting for transfers between devices, exchange(): lax.all_to_all(rows, AXES, split_axis=0, concat_axis=0, tiled=True)  31.2 us
    all_to_all x1, blocking collectives, exchange(): lax.all_to_all(rows, AXES, split_axis=0, concat_axis=0, tiled=True)  23.1 us
    pallas_call x6, Pallas kernels, call(): pl.pallas_call(kernel, out_shape=[pltpu.HBM(shape, kind) if s is HBM else...  19.8 us
    all_to_all x2, starting transfers between devices, exchange(): lax.all_to_all(rows, AXES, split_axis=0, concat_axis=0, tiled=True)  16 us
  transfers between devices with their start and end apart: 2, of which 2 were waited for; matrix products, arithmetic and copies ran while one was open for 1% of the time, Pallas kernels for 8%

profile of v7, /device:TPU:0, one launch (start us, length us, event | category | flops | bytes accessed | tf_op | source)
XLA Modules:
  0.0 92.9 jit_solution(14135939042674869600)
XLA Ops:
  0.0 3.2 %shard_map.55 = (f32[2560,128]{1,0:T(8,128)}, f32[8,128]{1,0:T(8,128)S(1)}) custom-call(s32[1,256]{1,0:T(1,128)} %bitcast.28, f32[4096,128]{1,0:T(8,128)} %bitcast.31), custom_call_target="tpu_custom_call" | custom-call | tf_op jit(solution)/shard_map/pallas_call | solution.py:437
  3.2 0.0 copy-start
  3.2 0.0 copy-start.1
  3.2 0.0 copy-start.4
  3.3 11.2 %all-to-all-start.1 = ((f32[2560,1,128]{2,1,0:T(1,128)}), f32[2560,1,128]{2,1,0:T(1,128)S(1)}, u32[]{:S(2)}, u32[]{:S(2)}) async-start(f32[2560,1,128]{2,1,0:T(1,128)} %bitcast.35), calls=%async_computation.1 | async-start | bytes 2621440 | tf_op jit(solution)/shard_map/obs_exchange/all_to_all | solution.py:454
  14.4 0.5 slice.3
  15.6 0.0 copy-done
  15.6 0.0 copy-done.1
  15.6 0.0 copy-done.4
  15.6 0.0 copy-start.2
  15.7 1.2 %copy-done.2 = f32[256,1024]{1,0:T(8,128)S(1)} copy-done((f32[256,1024]{1,0:T(8,128)S(1)}, f32[256,1024]{1,0:T(8,128)}, u32[]{:S(2)}) %copy-start.2) | copy-done | bytes 1048600
  16.9 2.3 %shard_map.56 = (f32[2176,128]{1,0:T(8,128)}, f32[512,128]{1,0:T(8,128)}, f32[8,1024]{1,0:T(8,128)S(1)}) custom-call(s32[1]{0:T(128)} %bitcast.9.mine_ref, s32[1,256]{1,0:T(1,128)S(1)} %bitcast.29, f32[2,256,512]{2,1,0:T(8,128)S(1)} %copy-done, f32[256,1024]{1,0:T(8,128)S(1)} %copy-done.1, f32[256,1024]{1,0:T(8,128)S(1)} %copy-done.2, f32[2,256,1024]{2,1,0:T(8,128)} %obs_hbm.1), custom_call_target="tpu_custom_call" | custom-call | tf_op jit(solution)/shard_map/pallas_call | solution.py:437
  19.2 17.0 %all-to-all-done.1 = f32[2560,1,128]{2,1,0:T(1,128)S(1)} async-done(((f32[2560,1,128]{2,1,0:T(1,128)}), f32[2560,1,128]{2,1,0:T(1,128)S(1)}, u32[]{:S(2)}, u32[]{:S(2)}) %all-to-all-start.1) | async-done | bytes 1310752 | tf_op jit(solution)/shard_map/obs_exchange/all_to_all | solution.py:454
  36.2 0.0 copy-start.5
  36.2 1.1 %shard_map.58 = f32[128,17,1,128]{3,2,1,0:T(1,128)} custom-call(f32[2560,128]{1,0:T(8,128)S(1)} %bitcast.23, f32[512,128]{1,0:T(8,128)S(1)} %get-tuple-element.31.extra_ref, f32[8,1024]{1,0:T(8,128)S(1)} %get-tuple-element.25.rows_ref, f32[128,17,1,128]{3,2,1,0:T(1,128)} %bitcast.32), custom_call_target="tpu_custom_call", output_to_operand_aliasing={{}: (3, {})} | custom-call | tf_op jit(solution)/shard_map/pallas_call | solution.py:437
  37.3 0.0 copy-done.5
  37.3 4.8 %all-to-all-start.2 = ((f32[2176,1,128]{2,1,0:T(1,128)}), f32[2176,1,128]{2,1,0:T(1,128)S(1)}, u32[]{:S(2)}, u32[]{:S(2)}) async-start(f32[2176,1,128]{2,1,0:T(1,128)} %bitcast.33), calls=%async_computation.2 | async-start | bytes 2228224 | tf_op jit(solution)/shard_map/states_exchange/all_to_all | solution.py:454
  42.2 5.3 %shard_map.57 = (f32[2560,128]{1,0:T(8,128)S(1)}, f32[1536,128]{1,0:T(8,128)S(1)}, f32[2,24,256]{2,1,0:T(8,128)S(1)}, bf16[256,256]{1,0:T(8,128)(2,1)}) custom-call(f32[2560,128]{1,0:T(8,128)S(1)} %bitcast.24, f32[512,128]{1,0:T(8,128)} %copy-done.5, f32[8,1024]{1,0:T(8,128)S(1)} %get-tuple-element.25.rows_ref, ...), custom_call_target="tpu_custom_call", output_to_operand_aliasing={{0}: (0, {})} | custom-call | tf_op jit(solution)/shard_map/pallas_call | solution.py:437
  47.5 14.2 %all-to-all-done.2 = f32[2176,1,128]{2,1,0:T(1,128)S(1)} async-done(((f32[2176,1,128]{2,1,0:T(1,128)}), f32[2176,1,128]{2,1,0:T(1,128)S(1)}, u32[]{:S(2)}, u32[]{:S(2)}) %all-to-all-start.2) | async-done | bytes 1114144 | tf_op jit(solution)/shard_map/states_exchange/all_to_all | solution.py:454
  61.7 6.3 %shard_map.59 = f32[2048,128]{1,0:T(8,128)S(1)} custom-call(f32[2176,128]{1,0:T(8,128)S(1)} %bitcast.25, f32[2560,128]{1,0:T(8,128)S(1)} %get-tuple-element.28.powers_ref, f32[1536,128]{1,0:T(8,128)S(1)} %get-tuple-element.29.more_ref, f32[2,24,256]{2,1,0:T(8,128)S(1)} %get-tuple-element.30.side_ref), custom_call_target="tpu_custom_call" | custom-call | tf_op jit(solution)/shard_map/pallas_call | solution.py:437
  68.0 0.0 copy-start.3
  68.1 23.1 %all_to_all.20 = f32[2048,1,128]{2,1,0:T(1,128)S(1)} all-to-all(f32[2048,1,128]{2,1,0:T(1,128)S(1)} %bitcast.27), channel_id=1, replica_groups=mesh['grp'=8,'mem'=16] {'grp','mem'}, dimensions={0} | all-to-all | bytes 2097152 | tf_op jit(solution)/shard_map/return_exchange/all_to_all | solution.py:454
  91.2 0.0 copy-done.3
  91.2 1.5 %shard_map.60 = f32[2,256,512]{2,1,0:T(8,128)} custom-call(bf16[256,256]{1,0:T(8,128)(2,1)S(1)} %copy-done.3, f32[2048,128]{1,0:T(8,128)S(1)} %bitcast.26), custom_call_target="tpu_custom_call" | custom-call | tf_op jit(solution)/shard_map/pallas_call | solution.py:437
  (2 shorter events, 0.0 us)
Async XLA Ops:
  3.2 12.4 %copy-start = (f32[2,256,512]{2,1,0:T(8,128)S(1)}, f32[2,256,512]{2,1,0:T(8,128)}, u32[]{:S(2)}) copy-start(f32[2,256,512]{2,1,0:T(8,128)} %states_ref.1) | copy-start | bytes 3145732
  3.2 12.4 %copy-start.1 = (f32[256,1024]{1,0:T(8,128)S(1)}, f32[256,1024]{1,0:T(8,128)}, u32[]{:S(2)}) copy-start(f32[256,1024]{1,0:T(8,128)} %value_ref.1) | copy-start | bytes 3145732
  3.2 12.4 %copy-start.4 = (s32[256]{0:T(256)S(1)}, s32[256]{0:T(256)}, u32[]{:S(2)}) copy-start(s32[256]{0:T(256)} %param.11) | copy-start | bytes 3076
  3.3 32.9 %all-to-all-start.1 = ((f32[2560,1,128]{2,1,0:T(1,128)}), f32[2560,1,128]{2,1,0:T(1,128)S(1)}, u32[]{:S(2)}, u32[]{:S(2)}) async-start(f32[2560,1,128]{2,1,0:T(1,128)} %bitcast.35), calls=%async_computation.1 | async-start | bytes 2621440 | tf_op jit(solution)/shard_map/obs_exchange/all_to_all | solution.py:454
  15.6 1.2 %copy-start.2 = (f32[256,1024]{1,0:T(8,128)S(1)}, f32[256,1024]{1,0:T(8,128)}, u32[]{:S(2)}) copy-start(f32[256,1024]{1,0:T(8,128)} %precision_ref.1) | copy-start | bytes 3145732
  36.2 1.1 %copy-start.5 = (f32[512,128]{1,0:T(8,128)}, f32[512,128]{1,0:T(8,128)S(1)}, u32[]{:S(2)}) copy-start(f32[512,128]{1,0:T(8,128)S(1)} %get-tuple-element.31.extra_ref) | copy-start | bytes 786436
  37.3 24.4 %all-to-all-start.2 = ((f32[2176,1,128]{2,1,0:T(1,128)}), f32[2176,1,128]{2,1,0:T(1,128)S(1)}, u32[]{:S(2)}, u32[]{:S(2)}) async-start(f32[2176,1,128]{2,1,0:T(1,128)} %bitcast.33), calls=%async_computation.2 | async-start | bytes 2228224 | tf_op jit(solution)/shard_map/states_exchange/all_to_all | solution.py:454
  68.0 23.2 %copy-start.3 = (bf16[256,256]{1,0:T(8,128)(2,1)S(1)}, bf16[256,256]{1,0:T(8,128)(2,1)}, u32[]{:S(2)}) copy-start(bf16[256,256]{1,0:T(8,128)(2,1)} %get-tuple-element.26.spread_ref) | copy-start | bytes 393220

commit v8 on v6

--- a/solution.py
+++ b/solution.py
@@ -358,7 +358,7 @@
             center_ref[k, :, columns] = jnp.broadcast_to(center, (8, LANES))
             for m in range(local):
                 high, low = halves(parts[m] - center)
-                for i, piece in enumerate((high, low, high)):
+                for i, piece in enumerate((high, low)):
                     first = i * members + m * devices
                     states_right[k, first : first + devices, columns] = piece
 
@@ -370,13 +370,17 @@
             put(s_ref, k, s)
             put(z_ref, k, roots[k])
 
-    for k in range(2):
-        root = advance(k)
+    roots = [advance(k) for k in range(2)]
+    transforms = []
+    for k in range(2):
+        root = roots[k]
         forcing = squared / scalers[k] * side_ref[k, :1]
         half_way = jnp.sum(root * forcing, axis=1, keepdims=True)
         shifts = jnp.sum(root * half_way, axis=0, keepdims=True)
-        transform = (inflation * free**0.5 / jnp.sqrt(scalers[k])) * root + shifts
-        update = dot(left_form(transform), states_right[k]) + center_ref[k, :1]
+        transforms.append((inflation * free**0.5 / jnp.sqrt(scalers[k])) * root + shifts)
+    for k in range(2):
+        high, low = states_right[k, :members], states_right[k, members:]
+        update = dot(left_form(transforms[k]), jnp.concatenate([high, low, high], axis=0)) + center_ref[k, :1]
         for c in range(blocks):
             for m in range(local):
                 piece = update[m * devices : (m + 1) * devices, c * LANES : (c + 1) * LANES]
@@ -522,7 +526,7 @@
         scratch=[
             pltpu.VMEM((2, 2, members, members), BF16),
             pltpu.VMEM((2, 2, members, members), BF16),
-            pltpu.VMEM((2, 3 * members, cells), BF16),
+            pltpu.VMEM((2, 2 * members, cells), BF16),
             pltpu.VMEM((2, 8, cells), F32),
         ],
     )

time: 93.3 us -> 93 us (level)
  no operation moved by 1% of the time
where the time goes in v8:
time: 93 us; the launch traced here: 92.7 us
  waiting for transfers between devices  31.2 us (34%)
  blocking collectives  23.1 us (25%)
  Pallas kernels  19.6 us (21%)
  starting transfers between devices  16 us (17%)
  local copies, waits for them, and re-layouts  1.78 us (2%)
  between operations  0.97 us (1%)
    all_to_all x2, waiting for transfers between devices, exchange(): lax.all_to_all(rows, AXES, split_axis=0, concat_axis=0, tiled=True)  31.2 us
    all_to_all x1, blocking collectives, exchange(): lax.all_to_all(rows, AXES, split_axis=0, concat_axis=0, tiled=True)  23.1 us
    pallas_call x6, Pallas kernels, call(): pl.pallas_call(kernel, out_shape=[pltpu.HBM(shape, kind) if s is HBM else...  19.6 us
    all_to_all x2, starting transfers between devices, exchange(): lax.all_to_all(rows, AXES, split_axis=0, concat_axis=0, tiled=True)  16 us
  transfers between devices with their start and end apart: 2, of which 2 were waited for; matrix products, arithmetic and copies ran while one was open for 1% of the time, Pallas kernels for 8%

profile of v8, /device:TPU:0, one launch (start us, length us, event | category | flops | bytes accessed | tf_op | source)
XLA Modules:
  0.0 92.7 jit_solution(2742417998573008399)
XLA Ops:
  0.0 3.2 %shard_map.55 = (f32[2560,128]{1,0:T(8,128)}, f32[8,128]{1,0:T(8,128)S(1)}) custom-call(s32[1,256]{1,0:T(1,128)} %bitcast.28, f32[4096,128]{1,0:T(8,128)} %bitcast.31), custom_call_target="tpu_custom_call" | custom-call | tf_op jit(solution)/shard_map/pallas_call | solution.py:434
  3.3 0.0 copy-start
  3.3 0.0 copy-start.1
  3.3 0.0 copy-start.4
  3.3 11.2 %all-to-all-start.1 = ((f32[2560,1,128]{2,1,0:T(1,128)}), f32[2560,1,128]{2,1,0:T(1,128)S(1)}, u32[]{:S(2)}, u32[]{:S(2)}) async-start(f32[2560,1,128]{2,1,0:T(1,128)} %bitcast.35), calls=%async_computation.1 | async-start | bytes 2621440 | tf_op jit(solution)/shard_map/obs_exchange/all_to_all | solution.py:451
  14.5 0.5 slice.3
  15.7 0.0 copy-done
  15.7 0.0 copy-done.1
  15.7 0.0 copy-done.4
  15.7 0.0 copy-start.2
  15.7 1.2 %copy-done.2 = f32[256,1024]{1,0:T(8,128)S(1)} copy-done((f32[256,1024]{1,0:T(8,128)S(1)}, f32[256,1024]{1,0:T(8,128)}, u32[]{:S(2)}) %copy-start.2) | copy-done | bytes 1048600
  16.9 2.3 %shard_map.56 = (f32[2176,128]{1,0:T(8,128)}, f32[512,128]{1,0:T(8,128)}, f32[8,1024]{1,0:T(8,128)S(1)}) custom-call(s32[1]{0:T(128)} %bitcast.9.mine_ref, s32[1,256]{1,0:T(1,128)S(1)} %bitcast.29, f32[2,256,512]{2,1,0:T(8,128)S(1)} %copy-done, f32[256,1024]{1,0:T(8,128)S(1)} %copy-done.1, f32[256,1024]{1,0:T(8,128)S(1)} %copy-done.2, f32[2,256,1024]{2,1,0:T(8,128)} %obs_hbm.1), custom_call_target="tpu_custom_call" | custom-call | tf_op jit(solution)/shard_map/pallas_call | solution.py:434
  19.2 17.0 %all-to-all-done.1 = f32[2560,1,128]{2,1,0:T(1,128)S(1)} async-done(((f32[2560,1,128]{2,1,0:T(1,128)}), f32[2560,1,128]{2,1,0:T(1,128)S(1)}, u32[]{:S(2)}, u32[]{:S(2)}) %all-to-all-start.1) | async-done | bytes 1310752 | tf_op jit(solution)/shard_map/obs_exchange/all_to_all | solution.py:451
  36.3 0.0 copy-start.5
  36.3 1.1 %shard_map.58 = f32[128,17,1,128]{3,2,1,0:T(1,128)} custom-call(f32[2560,128]{1,0:T(8,128)S(1)} %bitcast.23, f32[512,128]{1,0:T(8,128)S(1)} %get-tuple-element.31.extra_ref, f32[8,1024]{1,0:T(8,128)S(1)} %get-tuple-element.25.rows_ref, f32[128,17,1,128]{3,2,1,0:T(1,128)} %bitcast.32), custom_call_target="tpu_custom_call", output_to_operand_aliasing={{}: (3, {})} | custom-call | tf_op jit(solution)/shard_map/pallas_call | solution.py:434
  37.4 0.0 copy-done.5
  37.4 4.8 %all-to-all-start.2 = ((f32[2176,1,128]{2,1,0:T(1,128)}), f32[2176,1,128]{2,1,0:T(1,128)S(1)}, u32[]{:S(2)}, u32[]{:S(2)}) async-start(f32[2176,1,128]{2,1,0:T(1,128)} %bitcast.33), calls=%async_computation.2 | async-start | bytes 2228224 | tf_op jit(solution)/shard_map/states_exchange/all_to_all | solution.py:451
  42.2 5.3 %shard_map.57 = (f32[2560,128]{1,0:T(8,128)S(1)}, f32[1536,128]{1,0:T(8,128)S(1)}, f32[2,24,256]{2,1,0:T(8,128)S(1)}, bf16[256,256]{1,0:T(8,128)(2,1)}) custom-call(f32[2560,128]{1,0:T(8,128)S(1)} %bitcast.24, f32[512,128]{1,0:T(8,128)} %copy-done.5, f32[8,1024]{1,0:T(8,128)S(1)} %get-tuple-element.25.rows_ref, ...), custom_call_target="tpu_custom_call", output_to_operand_aliasing={{0}: (0, {})} | custom-call | tf_op jit(solution)/shard_map/pallas_call | solution.py:434
  47.6 14.2 %all-to-all-done.2 = f32[2176,1,128]{2,1,0:T(1,128)S(1)} async-done(((f32[2176,1,128]{2,1,0:T(1,128)}), f32[2176,1,128]{2,1,0:T(1,128)S(1)}, u32[]{:S(2)}, u32[]{:S(2)}) %all-to-all-start.2) | async-done | bytes 1114144 | tf_op jit(solution)/shard_map/states_exchange/all_to_all | solution.py:451
  61.7 6.1 %shard_map.59 = f32[2048,128]{1,0:T(8,128)S(1)} custom-call(f32[2176,128]{1,0:T(8,128)S(1)} %bitcast.25, f32[2560,128]{1,0:T(8,128)S(1)} %get-tuple-element.28.powers_ref, f32[1536,128]{1,0:T(8,128)S(1)} %get-tuple-element.29.more_ref, f32[2,24,256]{2,1,0:T(8,128)S(1)} %get-tuple-element.30.side_ref), custom_call_target="tpu_custom_call" | custom-call | tf_op jit(solution)/shard_map/pallas_call | solution.py:434
  67.8 0.0 copy-start.3
  67.8 23.1 %all_to_all.20 = f32[2048,1,128]{2,1,0:T(1,128)S(1)} all-to-all(f32[2048,1,128]{2,1,0:T(1,128)S(1)} %bitcast.27), channel_id=1, replica_groups=mesh['grp'=8,'mem'=16] {'grp','mem'}, dimensions={0} | all-to-all | bytes 2097152 | tf_op jit(solution)/shard_map/return_exchange/all_to_all | solution.py:451
  91.0 0.0 copy-done.3
  91.0 1.5 %shard_map.60 = f32[2,256,512]{2,1,0:T(8,128)} custom-call(bf16[256,256]{1,0:T(8,128)(2,1)S(1)} %copy-done.3, f32[2048,128]{1,0:T(8,128)S(1)} %bitcast.26), custom_call_target="tpu_custom_call" | custom-call | tf_op jit(solution)/shard_map/pallas_call | solution.py:434
  (2 shorter events, 0.0 us)
Async XLA Ops:
  3.3 12.4 %copy-start = (f32[2,256,512]{2,1,0:T(8,128)S(1)}, f32[2,256,512]{2,1,0:T(8,128)}, u32[]{:S(2)}) copy-start(f32[2,256,512]{2,1,0:T(8,128)} %states_ref.1) | copy-start | bytes 3145732
  3.3 12.4 %copy-start.1 = (f32[256,1024]{1,0:T(8,128)S(1)}, f32[256,1024]{1,0:T(8,128)}, u32[]{:S(2)}) copy-start(f32[256,1024]{1,0:T(8,128)} %value_ref.1) | copy-start | bytes 3145732
  3.3 12.4 %copy-start.4 = (s32[256]{0:T(256)S(1)}, s32[256]{0:T(256)}, u32[]{:S(2)}) copy-start(s32[256]{0:T(256)} %param.11) | copy-start | bytes 3076
  3.3 32.9 %all-to-all-start.1 = ((f32[2560,1,128]{2,1,0:T(1,128)}), f32[2560,1,128]{2,1,0:T(1,128)S(1)}, u32[]{:S(2)}, u32[]{:S(2)}) async-start(f32[2560,1,128]{2,1,0:T(1,128)} %bitcast.35), calls=%async_computation.1 | async-start | bytes 2621440 | tf_op jit(solution)/shard_map/obs_exchange/all_to_all | solution.py:451
  15.7 1.2 %copy-start.2 = (f32[256,1024]{1,0:T(8,128)S(1)}, f32[256,1024]{1,0:T(8,128)}, u32[]{:S(2)}) copy-start(f32[256,1024]{1,0:T(8,128)} %precision_ref.1) | copy-start | bytes 3145732
  36.3 1.1 %copy-start.5 = (f32[512,128]{1,0:T(8,128)}, f32[512,128]{1,0:T(8,128)S(1)}, u32[]{:S(2)}) copy-start(f32[512,128]{1,0:T(8,128)S(1)} %get-tuple-element.31.extra_ref) | copy-start | bytes 786436
  37.4 24.4 %all-to-all-start.2 = ((f32[2176,1,128]{2,1,0:T(1,128)}), f32[2176,1,128]{2,1,0:T(1,128)S(1)}, u32[]{:S(2)}, u32[]{:S(2)}) async-start(f32[2176,1,128]{2,1,0:T(1,128)} %bitcast.33), calls=%async_computation.2 | async-start | bytes 2228224 | tf_op jit(solution)/shard_map/states_exchange/all_to_all | solution.py:451
  67.8 23.2 %copy-start.3 = (bf16[256,256]{1,0:T(8,128)(2,1)S(1)}, bf16[256,256]{1,0:T(8,128)(2,1)}, u32[]{:S(2)}) copy-start(bf16[256,256]{1,0:T(8,128)(2,1)} %get-tuple-element.26.spread_ref) | copy-start | bytes 393220

commit v9 on v7

--- a/solution.py
+++ b/solution.py
@@ -365,7 +365,7 @@
             center_ref[k, :, columns] = jnp.broadcast_to(center, (8, LANES))
             for m in range(local):
                 high, low = halves(parts[m] - center)
-                for i, piece in enumerate((high, low, high)):
+                for i, piece in enumerate((high, low)):
                     first = i * members + m * devices
                     states_right[k, first : first + devices, columns] = piece
 
@@ -377,13 +377,17 @@
             put(s_ref, k, s)
             put(z_ref, k, roots[k])
 
-    for k in range(2):
-        root = advance(k)
+    roots = [advance(k) for k in range(2)]
+    transforms = []
+    for k in range(2):
+        root = roots[k]
         forcing = squared / scalers[k] * side_ref[k, :1]
         half_way = jnp.sum(root * forcing, axis=1, keepdims=True)
         shifts = jnp.sum(root * half_way, axis=0, keepdims=True)
-        transform = (inflation * free**0.5 / jnp.sqrt(scalers[k])) * root + shifts
-        update = dot(left_form(transform), states_right[k]) + center_ref[k, :1]
+        transforms.append((inflation * free**0.5 / jnp.sqrt(scalers[k])) * root + shifts)
+    for k in range(2):
+        high, low = states_right[k, :members], states_right[k, members:]
+        update = dot(left_form(transforms[k]), jnp.concatenate([high, low, high], axis=0)) + center_ref[k, :1]
         for c in range(blocks):
             for m in range(local):
                 piece = update[m * devices : (m + 1) * devices, c * LANES : (c + 1) * LANES]
@@ -527,7 +531,7 @@
         scratch=[
             pltpu.VMEM((2, 2, members, members), BF16),
             pltpu.VMEM((2, 2, members, members), BF16),
-            pltpu.VMEM((2, 3 * members, cells), BF16),
+            pltpu.VMEM((2, 2 * members, cells), BF16),
             pltpu.VMEM((2, 8, cells), F32),
         ],
     )

time: 93.2 us -> 93 us (level)
  no operation moved by 1% of the time
where the time goes in v9:
time: 93 us; the launch traced here: 92.6 us
  waiting for transfers between devices  31.2 us (34%)
  blocking collectives  23.1 us (25%)
  Pallas kernels  19.5 us (21%)
  starting transfers between devices  16 us (17%)
  local copies, waits for them, and re-layouts  1.78 us (2%)
  between operations  0.97 us (1%)
    all_to_all x2, waiting for transfers between devices, exchange(): lax.all_to_all(rows, AXES, split_axis=0, concat_axis=0, tiled=True)  31.2 us
    all_to_all x1, blocking collectives, exchange(): lax.all_to_all(rows, AXES, split_axis=0, concat_axis=0, tiled=True)  23.1 us
    pallas_call x6, Pallas kernels, call(): pl.pallas_call(kernel, out_shape=[pltpu.HBM(shape, kind) if s is HBM else...  19.5 us
    all_to_all x2, starting transfers between devices, exchange(): lax.all_to_all(rows, AXES, split_axis=0, concat_axis=0, tiled=True)  16 us
  transfers between devices with their start and end apart: 2, of which 2 were waited for; matrix products, arithmetic and copies ran while one was open for 1% of the time, Pallas kernels for 8%

profile of v9, /device:TPU:0, one launch (start us, length us, event | category | flops | bytes accessed | tf_op | source)
XLA Modules:
  0.0 92.6 jit_solution(13215944906186346561)
XLA Ops:
  0.0 3.2 %shard_map.55 = (f32[2560,128]{1,0:T(8,128)}, f32[8,128]{1,0:T(8,128)S(1)}) custom-call(s32[1,256]{1,0:T(1,128)} %bitcast.28, f32[4096,128]{1,0:T(8,128)} %bitcast.31), custom_call_target="tpu_custom_call" | custom-call | tf_op jit(solution)/shard_map/pallas_call | solution.py:441
  3.2 0.0 copy-start
  3.2 0.0 copy-start.1
  3.2 0.0 copy-start.4
  3.3 11.2 %all-to-all-start.1 = ((f32[2560,1,128]{2,1,0:T(1,128)}), f32[2560,1,128]{2,1,0:T(1,128)S(1)}, u32[]{:S(2)}, u32[]{:S(2)}) async-start(f32[2560,1,128]{2,1,0:T(1,128)} %bitcast.35), calls=%async_computation.1 | async-start | bytes 2621440 | tf_op jit(solution)/shard_map/obs_exchange/all_to_all | solution.py:458
  14.4 0.5 slice.3
  15.6 0.0 copy-done
  15.6 0.0 copy-done.1
  15.6 0.0 copy-done.4
  15.6 0.0 copy-start.2
  15.7 1.2 %copy-done.2 = f32[256,1024]{1,0:T(8,128)S(1)} copy-done((f32[256,1024]{1,0:T(8,128)S(1)}, f32[256,1024]{1,0:T(8,128)}, u32[]{:S(2)}) %copy-start.2) | copy-done | bytes 1048600
  16.9 2.3 %shard_map.56 = (f32[2176,128]{1,0:T(8,128)}, f32[512,128]{1,0:T(8,128)}, f32[8,1024]{1,0:T(8,128)S(1)}) custom-call(s32[1]{0:T(128)} %bitcast.9.mine_ref, s32[1,256]{1,0:T(1,128)S(1)} %bitcast.29, f32[2,256,512]{2,1,0:T(8,128)S(1)} %copy-done, f32[256,1024]{1,0:T(8,128)S(1)} %copy-done.1, f32[256,1024]{1,0:T(8,128)S(1)} %copy-done.2, f32[2,256,1024]{2,1,0:T(8,128)} %obs_hbm.1), custom_call_target="tpu_custom_call" | custom-call | tf_op jit(solution)/shard_map/pallas_call | solution.py:441
  19.2 17.0 %all-to-all-done.1 = f32[2560,1,128]{2,1,0:T(1,128)S(1)} async-done(((f32[2560,1,128]{2,1,0:T(1,128)}), f32[2560,1,128]{2,1,0:T(1,128)S(1)}, u32[]{:S(2)}, u32[]{:S(2)}) %all-to-all-start.1) | async-done | bytes 1310752 | tf_op jit(solution)/shard_map/obs_exchange/all_to_all | solution.py:458
  36.2 0.0 copy-start.5
  36.2 1.1 %shard_map.58 = f32[128,17,1,128]{3,2,1,0:T(1,128)} custom-call(f32[2560,128]{1,0:T(8,128)S(1)} %bitcast.23, f32[512,128]{1,0:T(8,128)S(1)} %get-tuple-element.31.extra_ref, f32[8,1024]{1,0:T(8,128)S(1)} %get-tuple-element.25.rows_ref, f32[128,17,1,128]{3,2,1,0:T(1,128)} %bitcast.32), custom_call_target="tpu_custom_call", output_to_operand_aliasing={{}: (3, {})} | custom-call | tf_op jit(solution)/shard_map/pallas_call | solution.py:441
  37.3 0.0 copy-done.5
  37.3 4.8 %all-to-all-start.2 = ((f32[2176,1,128]{2,1,0:T(1,128)}), f32[2176,1,128]{2,1,0:T(1,128)S(1)}, u32[]{:S(2)}, u32[]{:S(2)}) async-start(f32[2176,1,128]{2,1,0:T(1,128)} %bitcast.33), calls=%async_computation.2 | async-start | bytes 2228224 | tf_op jit(solution)/shard_map/states_exchange/all_to_all | solution.py:458
  42.2 5.3 %shard_map.57 = (f32[2560,128]{1,0:T(8,128)S(1)}, f32[1536,128]{1,0:T(8,128)S(1)}, f32[2,24,256]{2,1,0:T(8,128)S(1)}, bf16[256,256]{1,0:T(8,128)(2,1)}) custom-call(f32[2560,128]{1,0:T(8,128)S(1)} %bitcast.24, f32[512,128]{1,0:T(8,128)} %copy-done.5, f32[8,1024]{1,0:T(8,128)S(1)} %get-tuple-element.25.rows_ref, ...), custom_call_target="tpu_custom_call", output_to_operand_aliasing={{0}: (0, {})} | custom-call | tf_op jit(solution)/shard_map/pallas_call | solution.py:441
  47.5 14.2 %all-to-all-done.2 = f32[2176,1,128]{2,1,0:T(1,128)S(1)} async-done(((f32[2176,1,128]{2,1,0:T(1,128)}), f32[2176,1,128]{2,1,0:T(1,128)S(1)}, u32[]{:S(2)}, u32[]{:S(2)}) %all-to-all-start.2) | async-done | bytes 1114144 | tf_op jit(solution)/shard_map/states_exchange/all_to_all | solution.py:458
  61.7 6.1 %shard_map.59 = f32[2048,128]{1,0:T(8,128)S(1)} custom-call(f32[2176,128]{1,0:T(8,128)S(1)} %bitcast.25, f32[2560,128]{1,0:T(8,128)S(1)} %get-tuple-element.28.powers_ref, f32[1536,128]{1,0:T(8,128)S(1)} %get-tuple-element.29.more_ref, f32[2,24,256]{2,1,0:T(8,128)S(1)} %get-tuple-element.30.side_ref), custom_call_target="tpu_custom_call" | custom-call | tf_op jit(solution)/shard_map/pallas_call | solution.py:441
  67.8 0.0 copy-start.3
  67.8 23.1 %all_to_all.20 = f32[2048,1,128]{2,1,0:T(1,128)S(1)} all-to-all(f32[2048,1,128]{2,1,0:T(1,128)S(1)} %bitcast.27), channel_id=1, replica_groups=mesh['grp'=8,'mem'=16] {'grp','mem'}, dimensions={0} | all-to-all | bytes 2097152 | tf_op jit(solution)/shard_map/return_exchange/all_to_all | solution.py:458
  90.9 0.0 copy-done.3
  90.9 1.5 %shard_map.60 = f32[2,256,512]{2,1,0:T(8,128)} custom-call(bf16[256,256]{1,0:T(8,128)(2,1)S(1)} %copy-done.3, f32[2048,128]{1,0:T(8,128)S(1)} %bitcast.26), custom_call_target="tpu_custom_call" | custom-call | tf_op jit(solution)/shard_map/pallas_call | solution.py:441
  (2 shorter events, 0.0 us)
Async XLA Ops:
  3.2 12.4 %copy-start = (f32[2,256,512]{2,1,0:T(8,128)S(1)}, f32[2,256,512]{2,1,0:T(8,128)}, u32[]{:S(2)}) copy-start(f32[2,256,512]{2,1,0:T(8,128)} %states_ref.1) | copy-start | bytes 3145732
  3.2 12.4 %copy-start.1 = (f32[256,1024]{1,0:T(8,128)S(1)}, f32[256,1024]{1,0:T(8,128)}, u32[]{:S(2)}) copy-start(f32[256,1024]{1,0:T(8,128)} %value_ref.1) | copy-start | bytes 3145732
  3.2 12.4 %copy-start.4 = (s32[256]{0:T(256)S(1)}, s32[256]{0:T(256)}, u32[]{:S(2)}) copy-start(s32[256]{0:T(256)} %param.11) | copy-start | bytes 3076
  3.3 32.9 %all-to-all-start.1 = ((f32[2560,1,128]{2,1,0:T(1,128)}), f32[2560,1,128]{2,1,0:T(1,128)S(1)}, u32[]{:S(2)}, u32[]{:S(2)}) async-start(f32[2560,1,128]{2,1,0:T(1,128)} %bitcast.35), calls=%async_computation.1 | async-start | bytes 2621440 | tf_op jit(solution)/shard_map/obs_exchange/all_to_all | solution.py:458
  15.6 1.2 %copy-start.2 = (f32[256,1024]{1,0:T(8,128)S(1)}, f32[256,1024]{1,0:T(8,128)}, u32[]{:S(2)}) copy-start(f32[256,1024]{1,0:T(8,128)} %precision_ref.1) | copy-start | bytes 3145732
  36.2 1.1 %copy-start.5 = (f32[512,128]{1,0:T(8,128)}, f32[512,128]{1,0:T(8,128)S(1)}, u32[]{:S(2)}) copy-start(f32[512,128]{1,0:T(8,128)S(1)} %get-tuple-element.31.extra_ref) | copy-start | bytes 786436
  37.3 24.4 %all-to-all-start.2 = ((f32[2176,1,128]{2,1,0:T(1,128)}), f32[2176,1,128]{2,1,0:T(1,128)S(1)}, u32[]{:S(2)}, u32[]{:S(2)}) async-start(f32[2176,1,128]{2,1,0:T(1,128)} %bitcast.33), calls=%async_computation.2 | async-start | bytes 2228224 | tf_op jit(solution)/shard_map/states_exchange/all_to_all | solution.py:458
  67.8 23.2 %copy-start.3 = (bf16[256,256]{1,0:T(8,128)(2,1)S(1)}, bf16[256,256]{1,0:T(8,128)(2,1)}, u32[]{:S(2)}) copy-start(bf16[256,256]{1,0:T(8,128)(2,1)} %get-tuple-element.26.spread_ref) | copy-start | bytes 393220
